TPU v7x, 128 devices: a whole 4x4x4 slice. The times are simulated.
128 devices in a mesh: ctx: 64 (over z, x_hi, y, core), head: 2 (over x_lo).
Axes of the slice: x: 4 (x_hi: 2, x_lo: 2; x = x_hi * 2 + x_lo), y: 4, z: 4, core: 2. Of those that a mesh axis runs over, the one named last changes fastest.
Arguments:
- queries: bfloat16 [64, 1024, 2048], P('ctx', None, 'head'), may hold values from -8 to 8
- keys: bfloat16 [64, 1024, 2048], P('ctx', None, 'head'), may hold values from -8 to 8
- values: bfloat16 [64, 1024, 2048], P('ctx', None, 'head'), may hold values from -24 to 24
- w_out: bfloat16 [2048, 4096], P('head'), may hold values from -0.125 to 0.125
Outputs:
- mixed: bfloat16 [64, 1024, 4096], P('ctx', 'head')
All inputs are finite; a program needn't handle non-finite values.
Results may differ from a plain program's by a relative error of at most 0.013.
Values may be sent and summed in bfloat16 or wider, within the bound.
No kernel may reach another device: no remote copies, remote signals or barrier semaphores. Data moves between devices by JAX's collectives and lax.ppermute only.
A program may use at most 128 MiB of HBM per device.

v0:
```python
import jax
import jax.numpy as jnp
from jax import lax
from jax.sharding import PartitionSpec as P

HD = 128
GROUP = 4


masked_score = -1e30


def in_blocks(x, dim, devices):
    before, after = (x.shape[:dim], x.shape[dim + 1 :])
    return jnp.moveaxis(x.reshape(*before, devices, -1, *after), dim, 0)


def summed_on_arrival(x, axis, dim):
    devices = lax.axis_size(axis)
    parts = lax.all_to_all(in_blocks(x, dim, devices), axis, 0, 0, tiled=True)
    return jnp.sum(parts.astype(jnp.float32), axis=0)


def split_kinds(tensor, parity):
    groups = tensor.shape[2] // (2 * GROUP * HD)
    shaped = tensor.reshape((tensor.shape[0], tensor.shape[1], groups, 2, GROUP, HD))
    return shaped[:, :, :, parity].reshape((tensor.shape[0], tensor.shape[1], groups * GROUP, HD))


def normalized(scores):
    top = jnp.max(scores, axis=-1, keepdims=True)
    expo = jnp.exp(scores - top)
    total = jnp.sum(expo, axis=-1, keepdims=True)
    return (expo / total).astype(jnp.bfloat16)


def row_attention(queries, keys, values):
    scale = jnp.float32(1.0 / HD**0.5)
    length = queries.shape[1]
    causal = lax.broadcasted_iota(jnp.int32, (length, length), 1) <= lax.broadcasted_iota(
        jnp.int32, (length, length), 0
    )

    def one_row(triple):
        query_row, key_row, value_row = triple
        scores = (
            jnp.einsum("qhd,khd->hqk", query_row, key_row, preferred_element_type=jnp.float32)
            * scale
        )
        scores = jnp.where(causal, scores, masked_score)
        weights = normalized(scores)
        return jnp.einsum(
            "hqk,khd->qhd", weights, value_row, preferred_element_type=jnp.float32
        ).astype(jnp.bfloat16)

    return lax.map(one_row, (queries, keys, values))


def column_attention(triple):
    queries, keys, values = triple
    scale = jnp.float32(1.0 / HD**0.5)
    height = queries.shape[0]
    causal = lax.broadcasted_iota(jnp.int32, (height, height), 1) <= lax.broadcasted_iota(
        jnp.int32, (height, height), 0
    )
    scores = (
        jnp.einsum("rchd,schd->chrs", queries, keys, preferred_element_type=jnp.float32) * scale
    )
    scores = jnp.where(causal, scores, masked_score)
    weights = normalized(scores)
    attended = jnp.einsum(
        "chrs,schd->rchd", weights, values, preferred_element_type=jnp.float32
    ).astype(jnp.bfloat16)
    return lax.all_to_all(attended, "ctx", split_axis=0, concat_axis=1, tiled=True)


def on_device(queries, keys, values, w_out):
    rows_dev, stride, local_feat = queries.shape
    model_width = w_out.shape[1]
    groups = local_feat // (2 * GROUP * HD)
    row_out = row_attention(split_kinds(queries, 0), split_kinds(keys, 0), split_kinds(values, 0))
    col_triple = (split_kinds(queries, 1), split_kinds(keys, 1), split_kinds(values, 1))
    col_out = column_attention(
        (
            lax.all_to_all(col_triple[0], "ctx", split_axis=1, concat_axis=0, tiled=True),
            lax.all_to_all(col_triple[1], "ctx", split_axis=1, concat_axis=0, tiled=True),
            lax.all_to_all(col_triple[2], "ctx", split_axis=1, concat_axis=0, tiled=True),
        )
    )
    joined = jnp.stack(
        [
            row_out.reshape((rows_dev, stride, groups, GROUP, HD)),
            col_out.reshape((rows_dev, stride, groups, GROUP, HD)),
        ],
        axis=3,
    ).reshape((rows_dev * stride, local_feat))
    partial_value = jnp.dot(joined, w_out, preferred_element_type=jnp.float32)
    partial_value = partial_value.reshape((rows_dev, stride, model_width))
    return summed_on_arrival(partial_value.astype(jnp.bfloat16), "head", 1).astype(jnp.bfloat16)


def solution(mesh):
    return jax.shard_map(
        on_device,
        mesh=mesh,
        in_specs=(
            P("ctx", None, "head"),
            P("ctx", None, "head"),
            P("ctx", None, "head"),
            P("head", None),
        ),
        out_specs=P("ctx", "head", None),
        check_vma=False,
    )
```

profile of v0, /device:TPU:1, one launch (start us, length us, event | category | flops | bytes accessed | tf_op | source)
XLA Modules:
  0.0 234.4 jit_solution(8424355942385947717)
XLA Ops:
  0.0 2.9 %copy.40 = bf16[1,1024,1024]{1,2,0:T(8,128)(2,1)S(1)} copy(bf16[1,1024,1024]{2,1,0:T(8,128)(2,1)} %param.5) | data formatting | bytes 4194304 | tf_op args[1]
  2.9 0.0 copy-start
  2.9 0.1 slice_bitcast_fusion.1
  3.0 1.7 copy.46
  4.7 0.0 copy-done
  4.7 12.7 %all-to-all-start.1 = ((bf16[1,1024,4,128]{3,2,0,1:T(4,128)(2,1)}), bf16[1,1024,4,128]{3,2,0,1:T(4,128)(2,1)}, u32[]{:S(2)}, u32[]{:S(2)}) async-start(bf16[1,1024,4,128]{3,2,0,1:T(4,128)(2,1)} %copy.46), calls=%async_computation.1 | async-start | bytes 2097152 | tf_op jit(solution)/shard_map/all_to_all | solution.py:86
  17.3 2.9 %copy.38 = bf16[1,1024,1024]{1,2,0:T(8,128)(2,1)S(1)} copy(bf16[1,1024,1024]{2,1,0:T(8,128)(2,1)} %param.4) | data formatting | bytes 4194304 | tf_op args[0]
  20.2 0.0 copy-start.1
  20.2 0.1 slice_bitcast_fusion.2
  20.3 1.6 copy.44
  21.9 0.0 copy-done.1
  21.9 14.8 %all-to-all-done.1 = bf16[1,1024,4,128]{3,2,0,1:T(4,128)(2,1)} async-done(((bf16[1,1024,4,128]{3,2,0,1:T(4,128)(2,1)}), bf16[1,1024,4,128]{3,2,0,1:T(4,128)(2,1)}, u32[]{:S(2)}, u32[]{:S(2)}) %all-to-all-start.1) | async-done | bytes 1048608 | tf_op jit(solution)/shard_map/all_to_all | solution.py:86
  36.7 5.2 %all-to-all-start = ((bf16[1,1024,4,128]{3,2,0,1:T(4,128)(2,1)}), bf16[1,1024,4,128]{3,2,0,1:T(4,128)(2,1)}, u32[]{:S(2)}, u32[]{:S(2)}) async-start(bf16[1,1024,4,128]{3,2,0,1:T(4,128)(2,1)} %copy.44), calls=%async_computation | async-start | bytes 2097152 | tf_op jit(solution)/shard_map/all_to_all | solution.py:85
  41.9 2.9 %copy.42 = bf16[1,1024,1024]{1,2,0:T(8,128)(2,1)S(1)} copy(bf16[1,1024,1024]{2,1,0:T(8,128)(2,1)} %param.6) | data formatting | bytes 4194304 | tf_op args[2]
  44.7 0.1 slice_bitcast_fusion
  44.8 1.5 copy.50
  46.3 1.3 iota_compare_fusion
  47.6 13.7 %all-to-all-done = bf16[1,1024,4,128]{3,2,0,1:T(4,128)(2,1)} async-done(((bf16[1,1024,4,128]{3,2,0,1:T(4,128)(2,1)}), bf16[1,1024,4,128]{3,2,0,1:T(4,128)(2,1)}, u32[]{:S(2)}, u32[]{:S(2)}) %all-to-all-start) | async-done | bytes 1048608 | tf_op jit(solution)/shard_map/all_to_all | solution.py:85
  61.4 4.7 %all-to-all-start.2 = ((bf16[1,1024,4,128]{3,2,0,1:T(4,128)(2,1)}), bf16[1,1024,4,128]{3,2,0,1:T(4,128)(2,1)S(1)}, u32[]{:S(2)}, u32[]{:S(2)}) async-start(bf16[1,1024,4,128]{3,2,0,1:T(4,128)(2,1)} %copy.50), calls=%async_computation.2 | async-start | bytes 2097152 | tf_op jit(solution)/shard_map/all_to_all | solution.py:87
  66.0 11.7 %fusion.43 = (f32[4,1024]{1,0:T(4,128)S(1)}, f32[4,1024,1024]{1,2,0:T(8,128)}) fusion(pred[1024,1024]{0,1:T(8,128)(4,1)} %iota_compare_fusion, bf16[1,1024,1,2,4,128]{1,5,4,3,2,0:T(8,128)(2,1)} %bitcast.59, bf16[1,1024,1,2,4,128]{1,5,4,3,2,0:T(8,128)(2,1)} %bitcast.57), kind=kOutput, calls=%fused_computation.43 | convolution fusion | flops 1090520064 | bytes 19939328 | tf_op jit(solution)/shard_map/while/body/eval_jaxpr/sub | solution.py:32
  77.8 4.8 %fusion.38 = (f32[16,4,64]{2,1,0:T(4,128)S(1)}, f32[16,4,64,64]{2,3,1,0:T(8,128)}) fusion(pred[64,64]{0,1:T(8,128)(4,1)S(1)} %iota_compare_fusion.1, bf16[64,16,4,128]{3,2,1,0:T(4,128)(2,1)} %bitcast.11, bf16[64,16,4,128]{3,2,1,0:T(4,128)(2,1)} %bitcast.9), kind=kOutput, calls=%fused_computation.42 | convolution fusion | flops 68157504 | bytes 3166208 | tf_op jit(solution)/shard_map/sub | solution.py:32
  82.6 2.9 %all-to-all-done.2 = bf16[1,1024,4,128]{3,2,0,1:T(4,128)(2,1)S(1)} async-done(((bf16[1,1024,4,128]{3,2,0,1:T(4,128)(2,1)}), bf16[1,1024,4,128]{3,2,0,1:T(4,128)(2,1)S(1)}, u32[]{:S(2)}, u32[]{:S(2)}) %all-to-all-start.2) | async-done | bytes 1048608 | tf_op jit(solution)/shard_map/all_to_all | solution.py:87
  85.5 2.9 %fusion.11 = bf16[64,16,4,128]{3,0,2,1:T(8,128)(2,1)S(1)} fusion(f32[16,4,64,64]{2,3,1,0:T(8,128)} %get-tuple-element.16, bf16[64,16,4,128]{3,2,1,0:T(4,128)(2,1)S(1)} %bitcast.62, f32[16,4,64]{2,1,0:T(4,128)S(1)} %get-tuple-element.15), kind=kOutput, calls=%fused_computation.20 | convolution fusion | flops 68157440 | bytes 3162112 | tf_op jit(solution)/shard_map/chrs,schd->rchd/dot_general | solution.py:71
  88.4 1.8 copy.54
  90.2 7.4 %all-to-all-start.3 = ((bf16[64,16,4,128]{3,2,1,0:T(4,128)(2,1)}), bf16[64,16,4,128]{3,2,1,0:T(4,128)(2,1)S(1)}, u32[]{:S(2)}, u32[]{:S(2)}) async-start(bf16[64,16,4,128]{3,2,1,0:T(4,128)(2,1)} %copy.54), calls=%async_computation.3 | async-start | bytes 2097152 | tf_op jit(solution)/shard_map/all_to_all | solution.py:74
  97.6 8.1 %fusion.12 = bf16[1,1024,1,1,4,128]{1,5,4,3,2,0:T(8,128)(2,1)} fusion(f32[4,1024,1024]{1,2,0:T(8,128)} %get-tuple-element.24, f32[4,1024]{1,0:T(4,128)S(1)} %get-tuple-element.17, bf16[1,1024,1,2,4,128]{1,5,4,3,2,0:T(8,128)(2,1)S(1)} %bitcast.55), kind=kOutput, calls=%fused_computation.21 | convolution fusion | flops 1082654720 | bytes 18890752 | tf_op jit(solution)/shard_map/while/body/eval_jaxpr/hqk,khd->qhd/dot_general | solution.py:52
  105.7 0.0 copy-start.2
  105.7 11.4 %all-to-all-done.3 = bf16[64,16,4,128]{3,2,1,0:T(4,128)(2,1)S(1)} async-done(((bf16[64,16,4,128]{3,2,1,0:T(4,128)(2,1)}), bf16[64,16,4,128]{3,2,1,0:T(4,128)(2,1)S(1)}, u32[]{:S(2)}, u32[]{:S(2)}) %all-to-all-start.3) | async-done | bytes 1048608 | tf_op jit(solution)/shard_map/all_to_all | solution.py:74
  117.1 0.7 copy.56
  117.7 0.0 copy-done.2
  117.7 0.2 pad_maximum_fusion
  117.9 11.4 %convolution_convert_fusion = bf16[1024,4096]{1,0:T(8,128)(2,1)S(1)} fusion(bf16[1024,1024]{0,1:T(8,128)(2,1)S(1)} %bitcast.61, bf16[1024,4096]{1,0:T(8,128)(2,1)} %param.7), kind=kOutput, calls=%fused_computation.10 | convolution fusion | flops 8594128896 | bytes 18874368 | tf_op jit(solution)/shard_map/dot_general | solution.py:97
  129.3 96.4 %all_to_all.50 = bf16[2,1,512,4096]{3,2,1,0:T(8,128)(2,1)} all-to-all(bf16[2,1,512,4096]{3,2,1,0:T(8,128)(2,1)S(1)} %bitcast.53), channel_id=1, replica_groups=mesh['ctx'=64,'head'=2] {'head'}, dimensions={0} | all-to-all | bytes 16777216 | tf_op jit(solution)/shard_map/all_to_all | solution.py:20
  225.7 8.6 %reduce_sum.35 = bf16[512,4096]{1,0:T(8,128)(2,1)} reduce(bf16[2,1,512,4096]{3,2,1,0:T(8,128)(2,1)} %all_to_all.50, bf16[]{:T(256)} %constant.29.clone.1), dimensions={0,1}, to_apply=%region_4.5 | reduce | flops 2097152 | bytes 12582914 | tf_op jit(solution)/shard_map/reduce_sum | solution.py:21
  (1 shorter events, 0.0 us)
Async XLA Ops:
  2.9 1.8 copy-start
  4.7 32.0 %all-to-all-start.1 = ((bf16[1,1024,4,128]{3,2,0,1:T(4,128)(2,1)}), bf16[1,1024,4,128]{3,2,0,1:T(4,128)(2,1)}, u32[]{:S(2)}, u32[]{:S(2)}) async-start(bf16[1,1024,4,128]{3,2,0,1:T(4,128)(2,1)} %copy.46), calls=%async_computation.1 | async-start | bytes 2097152 | tf_op jit(solution)/shard_map/all_to_all | solution.py:86
  20.2 1.7 copy-start.1
  36.7 24.7 %all-to-all-start = ((bf16[1,1024,4,128]{3,2,0,1:T(4,128)(2,1)}), bf16[1,1024,4,128]{3,2,0,1:T(4,128)(2,1)}, u32[]{:S(2)}, u32[]{:S(2)}) async-start(bf16[1,1024,4,128]{3,2,0,1:T(4,128)(2,1)} %copy.44), calls=%async_computation | async-start | bytes 2097152 | tf_op jit(solution)/shard_map/all_to_all | solution.py:85
  61.4 24.1 %all-to-all-start.2 = ((bf16[1,1024,4,128]{3,2,0,1:T(4,128)(2,1)}), bf16[1,1024,4,128]{3,2,0,1:T(4,128)(2,1)S(1)}, u32[]{:S(2)}, u32[]{:S(2)}) async-start(bf16[1,1024,4,128]{3,2,0,1:T(4,128)(2,1)} %copy.50), calls=%async_computation.2 | async-start | bytes 2097152 | tf_op jit(solution)/shard_map/all_to_all | solution.py:87
  90.2 26.9 %all-to-all-start.3 = ((bf16[64,16,4,128]{3,2,1,0:T(4,128)(2,1)}), bf16[64,16,4,128]{3,2,1,0:T(4,128)(2,1)S(1)}, u32[]{:S(2)}, u32[]{:S(2)}) async-start(bf16[64,16,4,128]{3,2,1,0:T(4,128)(2,1)} %copy.54), calls=%async_computation.3 | async-start | bytes 2097152 | tf_op jit(solution)/shard_map/all_to_all | solution.py:74
  105.7 12.1 %copy-start.2 = (bf16[1,1024,1,1,4,128]{1,5,4,3,2,0:T(8,128)(2,1)S(1)}, bf16[1,1024,1,1,4,128]{1,5,4,3,2,0:T(8,128)(2,1)}, u32[]{:S(2)}) copy-start(bf16[1,1024,1,1,4,128]{1,5,4,3,2,0:T(8,128)(2,1)} %fusion.12) | copy-start | bytes 3145732
where the time goes:
time: 235 us; the launch traced here: 234 us
  blocking collectives  96.4 us (41%)
  waiting for transfers between devices  42.8 us (18%)
  matrix products  38.9 us (17%)
  starting transfers between devices  30 us (13%)
  local copies, waits for them, and re-layouts  16 us (7%)
  other arithmetic  10.2 us (4%)
    all_to_all x1, blocking collectives, summed_on_arrival(): parts = lax.all_to_all(in_blocks(x, dim, devices), axis, 0, 0, tiled=True)  96.4 us
    sub x2, matrix products, normalized(): expo = jnp.exp(scores - top)  16.5 us
    all_to_all x1, waiting for transfers between devices, on_device(): lax.all_to_all(col_triple[1], 'ctx', split_axis=1, concat_axis=0, tiled=T...  14.8 us
    all_to_all x1, waiting for transfers between devices, on_device(): lax.all_to_all(col_triple[0], 'ctx', split_axis=1, concat_axis=0, tiled=T...  13.7 us
    all_to_all x1, starting transfers between devices, on_device(): lax.all_to_all(col_triple[1], 'ctx', split_axis=1, concat_axis=0, tiled=T...  12.7 us
    dot_general x1, matrix products, on_device(): partial_value = jnp.dot(joined, w_out, preferred_element_type=jnp.float32)  11.4 us
    all_to_all x1, waiting for transfers between devices, column_attention(): lax.all_to_all(attended, 'ctx', split_axis=0, concat_axis=1, tiled=True)  11.4 us
    reduce_sum x1, other arithmetic, summed_on_arrival(): return jnp.sum(parts.astype(jnp.float32), axis=0)  8.63 us
  transfers between devices with their start and end apart: 4, of which 4 were waited for; matrix products, arithmetic and copies ran while one was open for 15% of the time, Pallas kernels for 0%

commit v1 on v0

v1 whole, which is shorter than its diff:
```python
import functools
import itertools
import math

import jax
import jax.numpy as jnp
from jax import lax
from jax.experimental import pallas as pl
from jax.experimental.pallas import tpu as pltpu
from jax.sharding import PartitionSpec as P

HD = 128
GROUP = 4
LOCAL = GROUP * HD
LENGTH = 1024
ROWS = 64
HALF = LENGTH // 2
WIDTH = 4096
BLOCK = 256
SCALE = math.log2(math.e) / math.sqrt(HD)
MASKED = -1e30
VMEM = 60 << 20

GATHER_GROUPS = [
    [z * 16 + x_hi * 8 + rest for z, rest in itertools.product(range(4), range(8))]
    for x_hi in range(2)
]
GATHER_SIZE = 32


def softmax_rows(scores):
    top = jnp.max(scores, axis=-1, keepdims=True)
    expo = jnp.exp2((scores - top) * SCALE)
    total = jnp.sum(expo, axis=-1, keepdims=True)
    return expo.astype(jnp.bfloat16), total


def dot_nt(a, b):
    return lax.dot_general(a, b, (((1,), (1,)), ((), ())), preferred_element_type=jnp.float32)


def dot_nn(a, b):
    return jnp.dot(a, b, preferred_element_type=jnp.float32)


def row_kernel(q_ref, k_ref, v_ref, own_ref, other_ref):
    me = lax.axis_index("head")
    lower = lax.broadcasted_iota(jnp.int32, (BLOCK, BLOCK), 1) <= lax.broadcasted_iota(
        jnp.int32, (BLOCK, BLOCK), 0
    )
    per_half = HALF // BLOCK
    for i in range(LENGTH // BLOCK):
        q = q_ref[0, i * BLOCK : (i + 1) * BLOCK, :]
        end = (i + 1) * BLOCK
        diag = jnp.where(lower, dot_nt(q, k_ref[0, i * BLOCK : end, :]), MASKED)
        if i:
            scores = jnp.concatenate([dot_nt(q, k_ref[0, : i * BLOCK, :]), diag], axis=1)
        else:
            scores = diag
        probs, total = softmax_rows(scores)
        out = (dot_nn(probs, v_ref[0, :end, :]) / total).astype(jnp.bfloat16)
        at = pl.ds((i % per_half) * BLOCK, BLOCK)

        @pl.when(me == i // per_half)
        def _():
            own_ref[at, :] = out

        @pl.when(me != i // per_half)
        def _():
            other_ref[at, :] = out


def row_attention(queries, keys, values):
    spec = pl.BlockSpec((1, LENGTH, HD), lambda h: (0, 0, h))
    out_spec = pl.BlockSpec((HALF, HD), lambda h: (0, h))
    shape = jax.ShapeDtypeStruct((HALF, LOCAL), jnp.bfloat16)
    return pl.pallas_call(
        row_kernel,
        grid=(GROUP,),
        in_specs=[spec] * 3,
        out_specs=[out_spec] * 2,
        out_shape=[shape, shape],
        compiler_params=pltpu.CompilerParams(vmem_limit_bytes=VMEM),
        cost_estimate=pl.CostEstimate(
            flops=4 * GROUP * LENGTH * LENGTH * HD,
            transcendentals=GROUP * LENGTH * LENGTH,
            bytes_accessed=4 * 2 * LENGTH * LOCAL,
        ),
        name="row_attention",
    )(queries, keys, values)


COLS = 16
SUB = 16
TOKENS = SUB * COLS


def column_kernel(x_ref, o_ref):
    to = lax.broadcasted_iota(jnp.int32, (TOKENS, TOKENS), 0)
    of = lax.broadcasted_iota(jnp.int32, (TOKENS, TOKENS), 1)
    swap = ((to % SUB) * COLS + to // SUB == of).astype(jnp.bfloat16)
    back = ((to % COLS) * SUB + to // COLS == of).astype(jnp.bfloat16)
    blocks = ROWS // SUB
    regrouped = []
    for b in range(blocks):
        x = x_ref[b * SUB : (b + 1) * SUB]
        parts = [x[:, t * COLS : (t + 1) * COLS, :].reshape(TOKENS, HD) for t in range(3)]
        regrouped.append(dot_nn(swap, jnp.concatenate(parts, axis=1)).astype(jnp.bfloat16))
    span = TOKENS // blocks
    row_of = (to // span) * SUB + to % SUB
    row_at = (of // span) * SUB + of % SUB
    allowed = ((to // SUB) % (span // SUB) == (of // SUB) % (span // SUB)) & (row_at <= row_of)
    outs = []
    for g in range(TOKENS // span):
        mine = jnp.concatenate([y[g * span : (g + 1) * span] for y in regrouped], axis=0)
        q, k, v = (mine[:, t * HD : (t + 1) * HD] for t in range(3))
        probs, total = softmax_rows(jnp.where(allowed, dot_nt(q, k), MASKED))
        outs.append((dot_nn(probs, v) / total).astype(jnp.bfloat16))
    for b in range(blocks):
        y = jnp.concatenate([o[b * span : (b + 1) * span] for o in outs], axis=0)
        z = dot_nn(back, y).astype(jnp.bfloat16)
        o_ref[b * SUB : (b + 1) * SUB] = z.reshape(SUB, COLS, HD)


def column_attention(x):
    return pl.pallas_call(
        column_kernel,
        grid=(GROUP,),
        in_specs=[pl.BlockSpec((ROWS, 3 * COLS, HD), lambda h: (0, 0, h))],
        out_specs=pl.BlockSpec((ROWS, COLS, HD), lambda h: (0, 0, h)),
        out_shape=jax.ShapeDtypeStruct((ROWS, COLS, LOCAL), jnp.bfloat16),
        compiler_params=pltpu.CompilerParams(vmem_limit_bytes=VMEM),
        cost_estimate=pl.CostEstimate(
            flops=4 * GROUP * ROWS * COLS * TOKENS * HD,
            transcendentals=GROUP * ROWS * COLS * TOKENS,
            bytes_accessed=4 * 2 * ROWS * COLS * LOCAL,
        ),
        name="column_attention",
    )(x)


TILE = 512


def row_project_kernel(a_ref, b_ref, w_ref, u_ref, o_ref):
    o_ref[...] = dot_nn(a_ref[...], w_ref[...]) + dot_nn(b_ref[...], u_ref[...])


def row_project(own, other, w_own, w_other):
    whole = pl.BlockSpec((HALF, LOCAL), lambda n: (0, 0))
    w_spec = pl.BlockSpec((LOCAL, TILE), lambda n: (0, n))
    return pl.pallas_call(
        row_project_kernel,
        grid=(WIDTH // TILE,),
        in_specs=[whole, whole, w_spec, w_spec],
        out_specs=pl.BlockSpec((HALF, TILE), lambda n: (0, n)),
        out_shape=jax.ShapeDtypeStruct((HALF, WIDTH), jnp.float32),
        compiler_params=pltpu.CompilerParams(vmem_limit_bytes=VMEM),
        cost_estimate=pl.CostEstimate(
            flops=4 * HALF * LOCAL * WIDTH, transcendentals=0, bytes_accessed=16 << 20
        ),
        name="row_project",
    )(own, other, w_own, w_other)


def column_project_kernel(acc_ref, a_ref, w_ref, u_ref, o_ref):
    me = lax.axis_index("head")
    own = a_ref[:, me].reshape(HALF, LOCAL)
    other = a_ref[:, 1 - me].reshape(HALF, LOCAL)
    total = acc_ref[...] + dot_nn(own, w_ref[...]) + dot_nn(other, u_ref[...])
    o_ref[0] = total.astype(jnp.bfloat16)


def column_project(acc, attended, w_own, w_other):
    w_spec = pl.BlockSpec((LOCAL, TILE), lambda n: (1, n))
    return pl.pallas_call(
        column_project_kernel,
        grid=(WIDTH // TILE,),
        in_specs=[
            pl.BlockSpec((HALF, TILE), lambda n: (0, n)),
            pl.BlockSpec((ROWS, 2, 8, LOCAL), lambda n: (0, 0, 0, 0)),
            w_spec,
            w_spec,
        ],
        out_specs=pl.BlockSpec((1, HALF, TILE), lambda n: (0, 0, n)),
        out_shape=jax.ShapeDtypeStruct((1, HALF, WIDTH), jnp.bfloat16),
        compiler_params=pltpu.CompilerParams(vmem_limit_bytes=VMEM),
        cost_estimate=pl.CostEstimate(
            flops=4 * HALF * LOCAL * WIDTH, transcendentals=0, bytes_accessed=20 << 20
        ),
        name="column_project",
    )(acc, attended, w_own, w_other)


SWAP = [(0, 1), (1, 0)]


def other_weights(w_out):
    ctx = lax.axis_index("ctx")
    place = (ctx // 16) * 8 + ctx % 8
    rows = w_out.shape[0] // GATHER_SIZE
    piece = lax.dynamic_slice_in_dim(w_out, place * rows, rows, 0)
    piece = lax.ppermute(piece, "head", SWAP)
    return lax.all_gather(piece, "ctx", axis=0, tiled=True, axis_index_groups=GATHER_GROUPS)


def packed(tensor):
    x = tensor[0, :, LOCAL:].reshape(2, ROWS, 8, LOCAL)
    return jnp.swapaxes(x, 0, 1).reshape(ROWS, COLS, LOCAL)


def on_device(queries, keys, values, w_out):
    sent = jnp.concatenate([packed(queries), packed(keys), packed(values)], axis=1)
    arrived = lax.all_to_all(sent, "ctx", split_axis=0, concat_axis=0, tiled=True)
    w_other = other_weights(w_out)
    row_own, row_away = row_attention(queries, keys, values)
    arrived, row_own, row_away = lax.optimization_barrier((arrived, row_own, row_away))
    row_other = lax.ppermute(row_away, "head", SWAP)
    acc = row_project(row_own, row_other, w_out, w_other)
    col = column_attention(arrived).reshape(2 * ROWS, 8, LOCAL)
    col = lax.all_to_all(col, ("ctx", "head"), split_axis=0, concat_axis=0, tiled=True)
    return column_project(acc, col.reshape(ROWS, 2, 8, LOCAL), w_out, w_other)


def solution(mesh):
    return jax.shard_map(
        on_device,
        mesh=mesh,
        in_specs=(
            P("ctx", None, "head"),
            P("ctx", None, "head"),
            P("ctx", None, "head"),
            P("head", None),
        ),
        out_specs=P("ctx", "head", None),
        check_vma=False,
    )
```

time: 235 us -> 146 us (0.62)
  blocking collectives: 96.4 us -> 0 us
  Pallas kernels: 0 us -> 40.8 us
  matrix products: 38.9 us -> 0 us
  waiting for transfers between devices: 42.8 us -> 59.5 us
  between operations: 0.14 us -> 13.5 us
  local copies, waits for them, and re-layouts: 16 us -> 7.26 us
  other arithmetic: 10.2 us -> 1.79 us
  starting transfers between devices: 30 us -> 22.1 us
    all_to_all x1 -> x0, blocking collectives: 96.4 us -> none  [summed_on_arrival(): parts = lax.all_to_all(in_blocks(x, dim, devices), axis, 0, 0, tiled=True)]
    pallas_call x0 -> x4, Pallas kernels: none -> 40.8 us  [the longest x1 12.1 us: column_project(): pl.pallas_call(column_project_kernel, grid=(WIDTH // TILE,), in_specs=[pl...]
    ppermute x0 -> x2, waiting for transfers between devices: none -> 28 us  [the longest x1 22.5 us: on_device(): row_other = lax.ppermute(row_away, 'head', SWAP)]
    dot_general x3 -> x0, matrix products: 22.3 us -> none  [the longest x1 11.4 us: on_device(): partial_value = jnp.dot(joined, w_out, preferred_element_type=jnp.float32)]
    sub x2 -> x0, matrix products: 16.5 us -> none  [normalized(): expo = jnp.exp(scores - top)]
    all_to_all x4 -> x2, starting transfers between devices: 30 us -> 18.5 us  [the longest x1 12.9 us: on_device(): lax.all_to_all(sent, 'ctx', split_axis=0, concat_axis=0, tiled=True)]
    all_to_all x4 -> x2, waiting for transfers between devices: 42.8 us -> 31.5 us  [the longest x1 31.5 us: on_device(): lax.all_to_all(sent, 'ctx', split_axis=0, concat_axis=0, tiled=True)]
    reduce_sum x1 -> x0, other arithmetic: 8.63 us -> none  [summed_on_arrival(): return jnp.sum(parts.astype(jnp.float32), axis=0)]
  transfers between devices with their start and end apart: 4 -> 5, of which waited for: 4 -> 3; matrix products, arithmetic and copies ran while one was open for 15% -> 3% of each run, Pallas kernels for 0% -> 20%
where the time goes in v1:
time: 146 us; the launch traced here: 145 us
  waiting for transfers between devices  59.5 us (41%)
  Pallas kernels  40.8 us (28%)
  starting transfers between devices  22.1 us (15%)
  between operations  13.5 us (9%)
  local copies, waits for them, and re-layouts  7.26 us (5%)
  other arithmetic  1.79 us (1%)
    all_to_all x1, waiting for transfers between devices, on_device(): lax.all_to_all(sent, 'ctx', split_axis=0, concat_axis=0, tiled=True)  31.5 us
    ppermute x1, waiting for transfers between devices, on_device(): row_other = lax.ppermute(row_away, 'head', SWAP)  22.5 us
    all_to_all x1, starting transfers between devices, on_device(): lax.all_to_all(sent, 'ctx', split_axis=0, concat_axis=0, tiled=True)  12.9 us
    pallas_call x1, Pallas kernels, column_project(): pl.pallas_call(column_project_kernel, grid=(WIDTH // TILE,), in_specs=[pl...  12.1 us
    pallas_call x1, Pallas kernels, row_project(): pl.pallas_call(row_project_kernel, grid=(WIDTH // TILE,), in_specs=[whole...  11.1 us
    pallas_call x1, Pallas kernels, row_attention(): pl.pallas_call(row_kernel, grid=(GROUP,), in_specs=[spec] * 3, out_specs=...  10.7 us
    pallas_call x1, Pallas kernels, column_attention(): pl.pallas_call(column_kernel, grid=(GROUP,), in_specs=[pl.BlockSpec((ROWS...  6.91 us
    all_to_all x1, starting transfers between devices, on_device(): lax.all_to_all(col, ('ctx', 'head'), split_axis=0, concat_axis=0, tiled=T...  5.58 us
  transfers between devices with their start and end apart: 5, of which 3 were waited for; matrix products, arithmetic and copies ran while one was open for 3% of the time, Pallas kernels for 20%

profile of v1, /device:TPU:1, one launch (start us, length us, event | category | flops | bytes accessed | tf_op | source)
XLA Modules:
  0.0 145.0 jit_solution(13644201117952234944)
XLA Ops:
  6.5 0.0 all-gather.2.cloned.1.call-start
  6.5 1.0 constant_dynamic-slice_fusion
  7.5 2.1 %collective-permute-start.1 = (bf16[32,4096]{1,0:T(8,128)(2,1)S(1)}, bf16[32,4096]{1,0:T(8,128)(2,1)S(1)}, u32[]{:S(2)}, u32[]{:S(2)}) collective-permute-start(bf16[32,4096]{1,0:T(8,128)(2,1)S(1)} %constant_dynamic-slice_fusion), channel_id=1, source_target_pairs={{0,1},{1,0},{2,3},{3,2},{4,5},{5,4},{6,7},{7,6},{8,9},{9,8},{10,11... | collective-permute-start | bytes 786440 | tf_op jit(solution)/shard_map/ppermute | solution.py:203
  9.6 5.5 %collective-permute-done.1 = bf16[32,4096]{1,0:T(8,128)(2,1)S(1)} collective-permute-done((bf16[32,4096]{1,0:T(8,128)(2,1)S(1)}, bf16[32,4096]{1,0:T(8,128)(2,1)S(1)}, u32[]{:S(2)}, u32[]{:S(2)}) %collective-permute-start.1) | collective-permute-done | bytes 262176 | tf_op jit(solution)/shard_map/ppermute | solution.py:203
  15.2 0.0 copy-start.3
  15.2 0.7 copy-done.3
  15.9 0.0 all-gather.2.cloned.1.call-update
  15.9 0.0 slice-start
  15.9 0.0 slice-start.1
  15.9 1.4 slice.9
  17.4 0.1 copy.11
  17.5 0.0 slice-done
  17.5 0.2 slice-done.1
  17.8 0.3 copy_bitcast_fusion
  18.1 1.8 %pad_maximum_fusion = bf16[64,48,512]{2,1,0:T(8,128)(2,1)} fusion(bf16[64,16,512]{2,1,0:T(8,128)(2,1)S(1)} %get-tuple-element.15, bf16[64,16,512]{2,1,0:T(8,128)(2,1)S(1)} %get-tuple-element.16, bf16[64,16,512]{2,1,0:T(8,128)(2,1)S(1)} %bitcast.20), kind=kLoop, calls=%fused_computation | loop fusion | flops 9437184 | bytes 6291456 | tf_op jit(solution)/shard_map/concatenate | solution.py:213
  19.9 12.9 %all-to-all-start = ((bf16[64,48,512]{2,1,0:T(8,128)(2,1)}), bf16[64,48,512]{2,1,0:T(8,128)(2,1)S(1)}, u32[]{:S(2)}, u32[]{:S(2)}) async-start(bf16[64,48,512]{2,1,0:T(8,128)(2,1)} %pad_maximum_fusion), calls=%async_computation | async-start | bytes 6291456 | tf_op jit(solution)/shard_map/all_to_all | solution.py:214
  32.8 10.7 %row_attention.1 = (bf16[512,512]{1,0:T(8,128)(2,1)}, bf16[512,512]{1,0:T(8,128)(2,1)}) custom-call(bf16[1,1024,1024]{2,1,0:T(8,128)(2,1)} %q_ref.1, bf16[1,1024,1024]{2,1,0:T(8,128)(2,1)} %k_ref.1, bf16[1,1024,1024]{2,1,0:T(8,128)(2,1)} %v_ref.1), custom_call_target="tpu_custom_call" | custom-call | flops 2147483648 | bytes 4194304 | tf_op jit(solution)/shard_map/row_attention/pallas_call | solution.py:77
  43.5 31.5 %all-to-all-done.x_ref = bf16[64,48,512]{2,1,0:T(8,128)(2,1)S(1)} async-done(((bf16[64,48,512]{2,1,0:T(8,128)(2,1)}), bf16[64,48,512]{2,1,0:T(8,128)(2,1)S(1)}, u32[]{:S(2)}, u32[]{:S(2)}) %all-to-all-start) | async-done | bytes 3145760 | tf_op jit(solution)/shard_map/all_to_all | solution.py:214
  75.0 0.0 copy-start
  75.0 1.7 %copy-done = bf16[64,48,512]{2,1,0:T(8,128)(2,1)} copy-done((bf16[64,48,512]{2,1,0:T(8,128)(2,1)}, bf16[64,48,512]{2,1,0:T(8,128)(2,1)S(1)}, u32[]{:S(2)}) %copy-start) | copy-done | bytes 3145752
  76.6 6.9 %column_attention.1 = bf16[64,16,512]{2,1,0:T(8,128)(2,1)} custom-call(bf16[64,48,512]{2,1,0:T(8,128)(2,1)} %copy-done), custom_call_target="tpu_custom_call" | custom-call | flops 536870912 | bytes 4194304 | tf_op jit(solution)/shard_map/column_attention/pallas_call | solution.py:126
  83.6 5.6 %all-to-all-start.1 = ((bf16[128,8,512]{2,1,0:T(8,128)(2,1)}), bf16[128,8,512]{2,1,0:T(8,128)(2,1)S(1)}, u32[]{:S(2)}, u32[]{:S(2)}) async-start(bf16[128,8,512]{2,1,0:T(8,128)(2,1)} %bitcast.19), calls=%async_computation.1 | async-start | bytes 2097152 | tf_op jit(solution)/shard_map/all_to_all | solution.py:221
  89.1 1.5 %collective-permute-start = (bf16[512,512]{1,0:T(8,128)(2,1)}, bf16[512,512]{1,0:T(8,128)(2,1)S(1)}, u32[]{:S(2)}, u32[]{:S(2)}) collective-permute-start(bf16[512,512]{1,0:T(8,128)(2,1)} %get-tuple-element.13), channel_id=1, source_target_pairs={{0,1},{1,0},{2,3},{3,2},{4,5},{5,4},{6,7},{7,6},{8,9},{9,8},{10,11... | collective-permute-start | bytes 1572872 | tf_op jit(solution)/shard_map/ppermute | solution.py:218
  90.6 22.5 %collective-permute-done.b_ref = bf16[512,512]{1,0:T(8,128)(2,1)S(1)} collective-permute-done((bf16[512,512]{1,0:T(8,128)(2,1)}, bf16[512,512]{1,0:T(8,128)(2,1)S(1)}, u32[]{:S(2)}, u32[]{:S(2)}) %collective-permute-start) | collective-permute-done | bytes 524320 | tf_op jit(solution)/shard_map/ppermute | solution.py:218
  113.1 0.0 copy-start.2
  113.1 0.0 all-gather.2.cloned.1.call-done.u_ref
  113.1 0.8 copy-done.2
  113.9 11.1 %row_project.1.acc_ref = f32[512,4096]{1,0:T(8,128)} custom-call(bf16[512,512]{1,0:T(8,128)(2,1)} %get-tuple-element.12.a_ref, bf16[512,512]{1,0:T(8,128)(2,1)} %copy-done.2, bf16[1024,4096]{1,0:T(8,128)(2,1)} %w_ref.3, bf16[1024,4096]{1,0:T(8,128)(2,1)} %all-gather.2.cloned.1.call-done.u_ref), custom_call_target="tpu_custom_call" | custom-call | flops 4294967296 | bytes 16777216 | tf_op jit(solution)/shard_map/row_project/pallas_call | solution.py:152
  125.0 0.0 all-to-all-done.1
  125.0 0.0 copy-start.1
  125.0 1.0 copy-done.1
  126.0 12.1 %column_project.1 = bf16[1,512,4096]{2,1,0:T(8,128)(2,1)} custom-call(f32[512,4096]{1,0:T(8,128)} %row_project.1.acc_ref, bf16[64,2,8,512]{3,2,1,0:T(8,128)(2,1)} %bitcast.23, bf16[1024,4096]{1,0:T(8,128)(2,1)} %w_ref.3, bf16[1024,4096]{1,0:T(8,128)(2,1)} %all-gather.2.cloned.1.call-done.u_ref), custom_call_target="tpu_custom_call" | custom-call | flops 4294967296 | bytes 20971520 | tf_op jit(solution)/shard_map/column_project/pallas_call | solution.py:176
Async XLA Ops:
  6.5 106.6 %all-gather.2.cloned.1.call-start = ((), (), s32[]{:S(2)}) async-start(), calls=%async_computation.2 | async-start | bytes 8650752 | tf_op jit(solution)/shard_map/all_gather | solution.py:204
  7.5 7.6 %collective-permute-start.1 = (bf16[32,4096]{1,0:T(8,128)(2,1)S(1)}, bf16[32,4096]{1,0:T(8,128)(2,1)S(1)}, u32[]{:S(2)}, u32[]{:S(2)}) collective-permute-start(bf16[32,4096]{1,0:T(8,128)(2,1)S(1)} %constant_dynamic-slice_fusion), channel_id=1, source_target_pairs={{0,1},{1,0},{2,3},{3,2},{4,5},{5,4},{6,7},{7,6},{8,9},{9,8},{10,11... | collective-permute-start | bytes 786440 | tf_op jit(solution)/shard_map/ppermute | solution.py:203
  15.2 0.7 copy-start.3
  15.9 1.6 %slice-start = ((bf16[1,1024,1024]{2,1,0:T(8,128)(2,1)}), bf16[1,1024,512]{2,1,0:T(8,128)(2,1)S(1)}, s32[]{:S(2)}) async-start(bf16[1,1024,1024]{2,1,0:T(8,128)(2,1)} %k_ref.1), calls=%async_computation.3 | async-start | bytes 2097152 | tf_op jit(solution)/shard_map/slice | solution.py:208
  15.9 1.8 %slice-start.1 = ((bf16[1,1024,1024]{2,1,0:T(8,128)(2,1)}), bf16[1,1024,512]{2,1,0:T(8,128)(2,1)S(1)}, s32[]{:S(2)}) async-start(bf16[1,1024,1024]{2,1,0:T(8,128)(2,1)} %v_ref.1), calls=%async_computation.4 | async-start | bytes 2097152 | tf_op jit(solution)/shard_map/slice | solution.py:208
  19.9 55.1 %all-to-all-start = ((bf16[64,48,512]{2,1,0:T(8,128)(2,1)}), bf16[64,48,512]{2,1,0:T(8,128)(2,1)S(1)}, u32[]{:S(2)}, u32[]{:S(2)}) async-start(bf16[64,48,512]{2,1,0:T(8,128)(2,1)} %pad_maximum_fusion), calls=%async_computation | async-start | bytes 6291456 | tf_op jit(solution)/shard_map/all_to_all | solution.py:214
  75.0 1.7 %copy-start = (bf16[64,48,512]{2,1,0:T(8,128)(2,1)}, bf16[64,48,512]{2,1,0:T(8,128)(2,1)S(1)}, u32[]{:S(2)}) copy-start(bf16[64,48,512]{2,1,0:T(8,128)(2,1)S(1)} %all-to-all-done.x_ref) | copy-start | bytes 9437188
  83.6 41.4 %all-to-all-start.1 = ((bf16[128,8,512]{2,1,0:T(8,128)(2,1)}), bf16[128,8,512]{2,1,0:T(8,128)(2,1)S(1)}, u32[]{:S(2)}, u32[]{:S(2)}) async-start(bf16[128,8,512]{2,1,0:T(8,128)(2,1)} %bitcast.19), calls=%async_computation.1 | async-start | bytes 2097152 | tf_op jit(solution)/shard_map/all_to_all | solution.py:221
  89.1 24.0 %collective-permute-start = (bf16[512,512]{1,0:T(8,128)(2,1)}, bf16[512,512]{1,0:T(8,128)(2,1)S(1)}, u32[]{:S(2)}, u32[]{:S(2)}) collective-permute-start(bf16[512,512]{1,0:T(8,128)(2,1)} %get-tuple-element.13), channel_id=1, source_target_pairs={{0,1},{1,0},{2,3},{3,2},{4,5},{5,4},{6,7},{7,6},{8,9},{9,8},{10,11... | collective-permute-start | bytes 1572872 | tf_op jit(solution)/shard_map/ppermute | solution.py:218
  113.1 0.8 copy-start.2
  125.0 1.0 copy-start.1
Sparse Core Ops, SparseCore 0:
  16.0 97.0 all-gather.1

commit v2 on v1

v2 whole, which is shorter than its diff:
```python
import itertools
import math

import jax
import jax.numpy as jnp
from jax import lax
from jax.experimental import pallas as pl
from jax.experimental.pallas import tpu as pltpu
from jax.sharding import PartitionSpec as P

HD = 128
GROUP = 4
LOCAL = GROUP * HD
LENGTH = 1024
ROWS = 64
HALF = LENGTH // 2
WIDTH = 4096
BLOCK = 256
SCALE = math.log2(math.e) / math.sqrt(HD)
MASKED = -1e30
SMALL_VMEM = 16 << 20
COST = pl.CostEstimate(flops=1 << 20, transcendentals=0, bytes_accessed=1 << 10)
LONG = pl.CostEstimate(flops=1 << 38, transcendentals=0, bytes_accessed=1 << 20)

PLACES = list(itertools.product(range(4), range(4), range(4), range(2)))
HALF_WIDTH = WIDTH // 2
PIECE = LENGTH // 4


def index_of(x, y, z, core):
    return (((z % 4) * 2 + (x % 4) // 2) * 4 + y % 4) * 4 + core * 2 + x % 2


def pair(at, core):
    return at + 1 if at % 2 == core else at - 1


def moves(step):
    return [(index_of(*place), index_of(*step(*place))) for place in PLACES]


ALONG_X = moves(lambda x, y, z, core: (x + 1 - 2 * core, y, z, core))
ALONG_Y = moves(lambda x, y, z, core: (x, pair(y, core), z, core))
ALONG_Z = moves(lambda x, y, z, core: (x, y, pair(z, core), core))
ALONG_N = moves(lambda x, y, z, core: (x - 1 + 2 * (x % 2), y, z, core))
TO_CORE = moves(lambda x, y, z, core: (x, y, z, 1 - core))
TO_HEAD = moves(lambda x, y, z, core: (x + 1 - 2 * (x % 2), y, z, core))


def position():
    ctx = lax.axis_index("ctx")
    return ctx & 1, (ctx >> 1) & 1, (ctx >> 4) & 1


def permute(x, pairs):
    return lax.ppermute(x, ("ctx", "head"), pairs)


def in_hbm(x):
    return pltpu.with_memory_space_constraint(x, pltpu.HBM)


def softmax_rows(scores):
    top = jnp.max(scores, axis=-1, keepdims=True)
    expo = jnp.exp2((scores - top) * SCALE)
    total = jnp.sum(expo, axis=-1, keepdims=True)
    return expo.astype(jnp.bfloat16), total


def dot_nt(a, b):
    return lax.dot_general(a, b, (((1,), (1,)), ((), ())), preferred_element_type=jnp.float32)


def dot_nn(a, b):
    return jnp.dot(a, b, preferred_element_type=jnp.float32)


def row_kernel(q_ref, k_ref, v_ref, own_ref, other_ref):
    me = lax.axis_index("head")
    lower = lax.broadcasted_iota(jnp.int32, (BLOCK, BLOCK), 1) <= lax.broadcasted_iota(
        jnp.int32, (BLOCK, BLOCK), 0
    )
    per_half = HALF // BLOCK
    other_ref[HALF:] = jnp.zeros((HALF, HD), jnp.bfloat16)
    for i in range(LENGTH // BLOCK):
        q = q_ref[0, i * BLOCK : (i + 1) * BLOCK, :]
        end = (i + 1) * BLOCK
        diag = jnp.where(lower, dot_nt(q, k_ref[0, i * BLOCK : end, :]), MASKED)
        if i:
            scores = jnp.concatenate([dot_nt(q, k_ref[0, : i * BLOCK, :]), diag], axis=1)
        else:
            scores = diag
        probs, total = softmax_rows(scores)
        out = (dot_nn(probs, v_ref[0, :end, :]) / total).astype(jnp.bfloat16)
        at = pl.ds((i % per_half) * BLOCK, BLOCK)

        @pl.when(me == i // per_half)
        def _():
            own_ref[at, :] = out

        @pl.when(me != i // per_half)
        def _():
            other_ref[at, :] = out


def row_attention(queries, keys, values):
    spec = pl.BlockSpec((1, LENGTH, HD), lambda h: (0, 0, h))
    return pl.pallas_call(
        row_kernel,
        grid=(GROUP,),
        in_specs=[spec] * 3,
        out_specs=[
            pl.BlockSpec((HALF, HD), lambda h: (0, h)),
            pl.BlockSpec((2 * HALF, HD), lambda h: (0, h)),
        ],
        out_shape=[
            pltpu.HBM((HALF, LOCAL), jnp.bfloat16),
            pltpu.HBM((2 * HALF, LOCAL), jnp.bfloat16),
        ],
        compiler_params=pltpu.CompilerParams(vmem_limit_bytes=SMALL_VMEM),
        cost_estimate=LONG,
        name="row_attention",
    )(in_hbm(queries), in_hbm(keys), in_hbm(values))


COLS = 16
SUB = 16
TOKENS = SUB * COLS


def column_kernel(x_ref, o_ref):
    to = lax.broadcasted_iota(jnp.int32, (TOKENS, TOKENS), 0)
    of = lax.broadcasted_iota(jnp.int32, (TOKENS, TOKENS), 1)
    swap = ((to % SUB) * COLS + to // SUB == of).astype(jnp.bfloat16)
    back = ((to % COLS) * SUB + to // COLS == of).astype(jnp.bfloat16)
    blocks = ROWS // SUB
    regrouped = []
    for b in range(blocks):
        x = x_ref[b * SUB : (b + 1) * SUB]
        parts = [x[:, t * COLS : (t + 1) * COLS, :].reshape(TOKENS, HD) for t in range(3)]
        regrouped.append(dot_nn(swap, jnp.concatenate(parts, axis=1)).astype(jnp.bfloat16))
    span = TOKENS // blocks
    row_of = (to // span) * SUB + to % SUB
    row_at = (of // span) * SUB + of % SUB
    allowed = ((to // SUB) % (span // SUB) == (of // SUB) % (span // SUB)) & (row_at <= row_of)
    outs = []
    for g in range(TOKENS // span):
        mine = jnp.concatenate([y[g * span : (g + 1) * span] for y in regrouped], axis=0)
        q, k, v = (mine[:, t * HD : (t + 1) * HD] for t in range(3))
        probs, total = softmax_rows(jnp.where(allowed, dot_nt(q, k), MASKED))
        outs.append((dot_nn(probs, v) / total).astype(jnp.bfloat16))
    for b in range(blocks):
        y = jnp.concatenate([o[b * span : (b + 1) * span] for o in outs], axis=0)
        z = dot_nn(back, y).astype(jnp.bfloat16)
        o_ref[b * SUB : (b + 1) * SUB] = z.reshape(SUB, COLS, HD)


def column_attention(x):
    return pl.pallas_call(
        column_kernel,
        grid=(GROUP,),
        in_specs=[pl.BlockSpec((ROWS, 3 * COLS, HD), lambda h: (0, 0, h))],
        out_specs=pl.BlockSpec((ROWS, COLS, HD), lambda h: (0, 0, h)),
        out_shape=pltpu.HBM((ROWS, COLS, LOCAL), jnp.bfloat16),
        compiler_params=pltpu.CompilerParams(vmem_limit_bytes=SMALL_VMEM),
        cost_estimate=COST,
        name="column_attention",
    )(x)


TILE = 512
TILES = WIDTH // TILE


def tile_of(n, core):
    return lax.rem(n + core * (TILES // 2), TILES)


def join_kernel(s_ref, row_own, row_other, x_ref, a_ref):
    mine, me = 2 * s_ref[1] + s_ref[2], s_ref[3]
    a_ref[:, :LOCAL] = row_own[...]
    a_ref[:, LOCAL : 2 * LOCAL] = x_ref[:, me].reshape(HALF, LOCAL)
    other = x_ref[:, 1 - me].reshape(HALF, LOCAL)
    quarters = [row_other[:, :PIECE], row_other[:, PIECE:], other[:, :PIECE], other[:, PIECE:]]
    for i in range(4):
        picked = quarters[0]
        for q in range(1, 4):
            picked = jnp.where(lax.bitwise_xor(mine, i) == q, quarters[q], picked)
        a_ref[:, 2 * LOCAL + i * PIECE : 2 * LOCAL + (i + 1) * PIECE] = picked


def join(place, row_own, row_other, attended):
    return pl.pallas_call(
        join_kernel,
        grid=(1,),
        in_specs=[
            pl.BlockSpec(memory_space=pltpu.SMEM),
            pl.BlockSpec((HALF, LOCAL), lambda n: (0, 0)),
            pl.BlockSpec((HALF, LOCAL), lambda n: (0, 0)),
            pl.BlockSpec((ROWS, 2, 8, LOCAL), lambda n: (0, 0, 0, 0)),
        ],
        out_shape=jax.ShapeDtypeStruct((HALF, 4 * LOCAL), jnp.bfloat16),
        compiler_params=pltpu.CompilerParams(vmem_limit_bytes=SMALL_VMEM),
        cost_estimate=LONG,
        name="join",
    )(place, in_hbm(row_own), row_other, attended)


def project_kernel(s_ref, a_ref, w_ref, *refs):
    near, far, o_ref = refs[:4], refs[4:8], refs[8]
    n = pl.program_id(0)

    def product(pieces):
        weights = jnp.concatenate([w_ref[...], *[p[...] for p in pieces]], axis=0)
        o_ref[0] = dot_nn(a_ref[...], weights).astype(jnp.bfloat16)

    @pl.when(n < TILES // 2)
    def _():
        product(near)

    @pl.when(n >= TILES // 2)
    def _():
        product(far)


def project(place, joined, w_own, pieces):
    half = TILES // 2
    near = pl.BlockSpec((PIECE, TILE), lambda n, s: (0, jnp.minimum(n, half - 1)))
    far = pl.BlockSpec((PIECE, TILE), lambda n, s: (0, jnp.maximum(n - half, 0)))
    return pl.pallas_call(
        project_kernel,
        grid_spec=pltpu.PrefetchScalarGridSpec(
            num_scalar_prefetch=1,
            grid=(TILES,),
            in_specs=[
                pl.BlockSpec((HALF, 4 * LOCAL), lambda n, s: (0, 0)),
                pl.BlockSpec((2 * LOCAL, TILE), lambda n, s: (0, tile_of(n, s[0]))),
                *[near] * 4,
                *[far] * 4,
            ],
            out_specs=pl.BlockSpec((1, HALF, TILE), lambda n, s: (0, 0, tile_of(n, s[0]))),
        ),
        out_shape=jax.ShapeDtypeStruct((1, HALF, WIDTH), jnp.bfloat16),
        compiler_params=pltpu.CompilerParams(vmem_limit_bytes=24 << 20),
        cost_estimate=COST,
        name="project",
    )(place, joined, in_hbm(w_own), *map(in_hbm, pieces))


def slice_kernel(s_ref, w_ref, x_ref, y_ref, buf, in_sems, out_sems):
    columns = pl.ds(pl.multiple_of(s_ref[0] * HALF_WIDTH, HALF_WIDTH), HALF_WIDTH)
    outs = (x_ref, y_ref)
    mine = 2 * s_ref[1] + s_ref[2]
    loads, stores = [], []
    for i, quarter in enumerate((mine, 3 - mine)):
        start = pl.multiple_of(quarter * PIECE, PIECE)
        loads.append(
            pltpu.make_async_copy(w_ref.at[pl.ds(start, PIECE), columns], buf.at[i], in_sems.at[i])
        )
        stores.append(pltpu.make_async_copy(buf.at[i], outs[i], out_sems.at[i]))
    for load in loads:
        load.start()
    for load, store in zip(loads, stores):
        load.wait()
        store.start()
    for store in stores:
        store.wait()


def slices(place, w_out):
    shape = pltpu.HBM((PIECE, HALF_WIDTH), jnp.bfloat16)
    return pl.pallas_call(
        slice_kernel,
        in_specs=[pl.BlockSpec(memory_space=pltpu.SMEM), pl.BlockSpec(memory_space=pl.ANY)],
        out_specs=[pl.BlockSpec(memory_space=pl.ANY)] * 2,
        out_shape=[shape, shape],
        scratch_shapes=[
            pltpu.VMEM((2, PIECE, HALF_WIDTH), jnp.bfloat16),
            pltpu.SemaphoreType.DMA((2,)),
            pltpu.SemaphoreType.DMA((2,)),
        ],
        compiler_params=pltpu.CompilerParams(vmem_limit_bytes=SMALL_VMEM),
        cost_estimate=COST,
        name="slices",
    )(place, in_hbm(w_out))


PACK_STEPS = 4


def pack_kernel(q_ref, k_ref, v_ref, o_ref, buf, in_sems, out_sems):
    step = ROWS // PACK_STEPS
    loads, stores = [], []
    for n in range(PACK_STEPS):
        at = pl.ds(n * step, step)
        loads.append(
            [
                pltpu.make_async_copy(
                    ref.at[0, half, at, :, pl.ds(LOCAL, LOCAL)],
                    buf.at[at, 2 * t + half],
                    in_sems.at[n, 2 * t + half],
                )
                for t, ref in enumerate((q_ref, k_ref, v_ref))
                for half in range(2)
            ]
        )
        stores.append(pltpu.make_async_copy(buf.at[at], o_ref.at[at], out_sems.at[n]))
    for group in loads:
        for load in group:
            load.start()
    for group, store in zip(loads, stores):
        for load in group:
            load.wait()
        store.start()
    for store in stores:
        store.wait()


def packed(*tensors):
    return pl.pallas_call(
        pack_kernel,
        in_specs=[pl.BlockSpec(memory_space=pl.ANY)] * 3,
        out_specs=pl.BlockSpec(memory_space=pl.ANY),
        out_shape=pltpu.HBM((ROWS, 6, 8, LOCAL), jnp.bfloat16),
        scratch_shapes=[
            pltpu.VMEM((ROWS, 6, 8, LOCAL), jnp.bfloat16),
            pltpu.SemaphoreType.DMA((PACK_STEPS, 6)),
            pltpu.SemaphoreType.DMA((PACK_STEPS,)),
        ],
        compiler_params=pltpu.CompilerParams(vmem_limit_bytes=SMALL_VMEM),
        cost_estimate=COST,
        name="pack",
    )(*[in_hbm(t.reshape(1, 2, ROWS, 8, 2 * LOCAL)) for t in tensors]).reshape(ROWS, 3 * COLS, LOCAL)


def on_device(queries, keys, values, w_out):
    place = jnp.stack([*position(), lax.axis_index("head")])
    pieces, *col_qkv = lax.optimization_barrier((slices(place, w_out), queries, keys, values))
    mine = permute(pieces[0], ALONG_X)
    sent = packed(*col_qkv)
    arrived = lax.all_to_all(sent, "ctx", split_axis=0, concat_axis=0, tiled=True)
    mine, away, *row_qkv = lax.optimization_barrier((mine, pieces[1], queries, keys, values))
    row_own, row_away = row_attention(*row_qkv)
    mine, away, row_own, row_away = lax.optimization_barrier((mine, away, row_own, row_away))
    quarters = [mine, permute(mine, ALONG_Z), permute(mine, ALONG_Y), permute(away, ALONG_N)]
    row_other = permute(row_away, TO_HEAD)
    col = column_attention(arrived)
    *quarters, row_other, _ = lax.optimization_barrier((*quarters, row_other, col))
    quarters += [permute(quarter, TO_CORE) for quarter in quarters]
    col = col.reshape(2 * ROWS, 8, LOCAL)
    col = lax.all_to_all(col, ("ctx", "head"), split_axis=0, concat_axis=0, tiled=True)
    joined = join(place, row_own, row_other, col.reshape(ROWS, 2, 8, LOCAL))
    return project(place, joined, w_out, quarters)


def solution(mesh):
    return jax.shard_map(
        on_device,
        mesh=mesh,
        in_specs=(
            P("ctx", None, "head"),
            P("ctx", None, "head"),
            P("ctx", None, "head"),
            P("head", None),
        ),
        out_specs=P("ctx", "head", None),
        check_vma=False,
    )
```

time: 146 us -> 113 us (0.77)
  waiting for transfers between devices: 59.5 us -> 42.6 us
  between operations: 13.5 us -> 0.11 us
  starting transfers between devices: 22.1 us -> 29.7 us
  local copies, waits for them, and re-layouts: 7.26 us -> 0.01 us
  other arithmetic: 1.79 us -> 0.08 us
    ppermute x2 -> x9, waiting for transfers between devices: 28 us -> 5.82 us  [permute(): return lax.ppermute(x, ('ctx', 'head'), pairs)]
    all_to_all x1, waiting for transfers between devices: 0.01 us -> 14.5 us  [on_device(): lax.all_to_all(col, ('ctx', 'head'), split_axis=0, concat_axis=0, tiled=T...]
    ppermute x2 -> x9, starting transfers between devices: 3.58 us -> 13.2 us  [permute(): return lax.ppermute(x, ('ctx', 'head'), pairs)]
    all_to_all x1, waiting for transfers between devices: 31.5 us -> 22.3 us  [on_device(): lax.all_to_all(sent, 'ctx', split_axis=0, concat_axis=0, tiled=True)]
    unnamed x8 -> x6, local copies, waits for them, and re-layouts: 4.16 us -> 0.01 us
    all_to_all x1, starting transfers between devices: 12.9 us -> 10.5 us  [on_device(): lax.all_to_all(sent, 'ctx', split_axis=0, concat_axis=0, tiled=True)]
    concatenate x1 -> x0, other arithmetic: 1.79 us -> none  [on_device(): jnp.concatenate([packed(queries), packed(keys), packed(values)], axis=1)]
    slice x5 -> x0, local copies, waits for them, and re-layouts: 1.69 us -> none  [packed(): x = tensor[0, :, LOCAL:].reshape(2, ROWS, 8, LOCAL)]
  transfers between devices with their start and end apart: 5 -> 11, of which waited for: 3 -> 3; matrix products, arithmetic and copies ran while one was open for 3% -> 0% of each run, Pallas kernels for 20% -> 19%
where the time goes in v2:
time: 113 us; the launch traced here: 112 us
  waiting for transfers between devices  42.6 us (38%)
  Pallas kernels  39.9 us (35%)
  starting transfers between devices  29.7 us (26%)
    all_to_all x1, waiting for transfers between devices, on_device(): lax.all_to_all(sent, 'ctx', split_axis=0, concat_axis=0, tiled=True)  22.3 us
    pallas_call x1, Pallas kernels, project(): pl.pallas_call(project_kernel, grid_spec=pltpu.PrefetchScalarGridSpec(num...  14.9 us
    all_to_all x1, waiting for transfers between devices, on_device(): lax.all_to_all(col, ('ctx', 'head'), split_axis=0, concat_axis=0, tiled=T...  14.5 us
    ppermute x9, starting transfers between devices, permute(): return lax.ppermute(x, ('ctx', 'head'), pairs)  13.2 us
    pallas_call x1, Pallas kernels, row_attention(): pl.pallas_call(row_kernel, grid=(GROUP,), in_specs=[spec] * 3, out_specs=...  10.8 us
    all_to_all x1, starting transfers between devices, on_device(): lax.all_to_all(sent, 'ctx', split_axis=0, concat_axis=0, tiled=True)  10.5 us
    pallas_call x1, Pallas kernels, column_attention(): pl.pallas_call(column_kernel, grid=(GROUP,), in_specs=[pl.BlockSpec((ROWS...  6.67 us
    all_to_all x1, starting transfers between devices, on_device(): lax.all_to_all(col, ('ctx', 'head'), split_axis=0, concat_axis=0, tiled=T...  5.96 us
  transfers between devices with their start and end apart: 11, of which 3 were waited for; matrix products, arithmetic and copies ran while one was open for 0% of the time, Pallas kernels for 19%

profile of v2, /device:TPU:1, one launch (start us, length us, event | category | flops | bytes accessed | tf_op | source)
XLA Modules:
  0.0 112.5 jit_solution(11252085105045103473)
XLA Ops:
  0.0 0.1 pad_add_fusion.s_ref
  0.1 0.0 copy-start
  0.1 3.1 %slices.1 = (bf16[256,2048]{1,0:T(8,128)(2,1)}, bf16[256,2048]{1,0:T(8,128)(2,1)}) custom-call(s32[4]{0:T(128)S(1)} %pad_add_fusion.s_ref, bf16[1024,4096]{1,0:T(8,128)(2,1)} %w_ref.3), custom_call_target="tpu_custom_call" | custom-call | flops 1048576 | bytes 1024 | tf_op jit(solution)/shard_map/slices/pallas_call | solution.py:272
  3.2 0.0 copy-done
  3.2 3.4 %collective-permute-start = (bf16[256,2048]{1,0:T(8,128)(2,1)}, bf16[256,2048]{1,0:T(8,128)(2,1)}, u32[]{:S(2)}, u32[]{:S(2)}) collective-permute-start(bf16[256,2048]{1,0:T(8,128)(2,1)} %get-tuple-element.30), channel_id=1, source_target_pairs={{0,1},{2,19},{32,33},{34,51},{64,65},{66,83},{96,97},{98,115},{4,5... | collective-permute-start | bytes 3145736 | tf_op jit(solution)/shard_map/ppermute | solution.py:56
  6.6 3.1 %pack.1 = bf16[64,6,8,512]{3,2,1,0:T(8,128)(2,1)} custom-call(bf16[1,2,64,8,1024]{4,3,2,1,0:T(8,128)(2,1)} %bitcast.13, bf16[1,2,64,8,1024]{4,3,2,1,0:T(8,128)(2,1)} %bitcast.14, bf16[1,2,64,8,1024]{4,3,2,1,0:T(8,128)(2,1)} %bitcast.15), custom_call_target="tpu_custom_call" | custom-call | flops 1048576 | bytes 1024 | tf_op jit(solution)/shard_map/pack/pallas_call | solution.py:320
  9.7 10.5 %all-to-all-start = ((bf16[64,48,512]{2,1,0:T(8,128)(2,1)}), bf16[64,48,512]{2,1,0:T(8,128)(2,1)}, u32[]{:S(2)}, u32[]{:S(2)}) async-start(bf16[64,48,512]{2,1,0:T(8,128)(2,1)} %bitcast.11), calls=%async_computation | async-start | bytes 6291456 | tf_op jit(solution)/shard_map/all_to_all | solution.py:341
  20.2 0.0 collective-permute-done.refs_0_
  20.2 0.0 copy-start.2
  20.2 10.8 %row_attention.1 = (bf16[512,512]{1,0:T(8,128)(2,1)}, bf16[1024,512]{1,0:T(8,128)(2,1)}) custom-call(bf16[1,1024,1024]{2,1,0:T(8,128)(2,1)} %q_ref, bf16[1,1024,1024]{2,1,0:T(8,128)(2,1)} %k_ref, bf16[1,1024,1024]{2,1,0:T(8,128)(2,1)} %v_ref), custom_call_target="tpu_custom_call" | custom-call | flops 274877906944 | bytes 1048576 | tf_op jit(solution)/shard_map/row_attention/pallas_call | solution.py:108
  31.1 0.0 copy-done.2
  31.1 0.0 copy-start.1
  31.1 2.0 %collective-permute-start.3 = (bf16[256,2048]{1,0:T(8,128)(2,1)S(1)}, bf16[256,2048]{1,0:T(8,128)(2,1)}, u32[]{:S(2)}, u32[]{:S(2)}) collective-permute-start(bf16[256,2048]{1,0:T(8,128)(2,1)S(1)} %copy-done.2), channel_id=1, source_target_pairs={{0,17},{2,19},{32,49},{34,51},{64,81},{66,83},{96,113},{98,115},{4... | collective-permute-start | bytes 3145736 | tf_op jit(solution)/shard_map/ppermute | solution.py:56
  33.1 0.6 collective-permute-start.4
  33.7 2.4 %collective-permute-start.2 = (bf16[256,2048]{1,0:T(8,128)(2,1)}, bf16[256,2048]{1,0:T(8,128)(2,1)}, u32[]{:S(2)}, u32[]{:S(2)}) collective-permute-start(bf16[256,2048]{1,0:T(8,128)(2,1)} %collective-permute-done.refs_0_), channel_id=1, source_target_pairs={{0,4},{2,14},{32,36},{34,46},{64,68},{66,78},{96,100},{98,110},{4,... | collective-permute-start | bytes 3145736 | tf_op jit(solution)/shard_map/ppermute | solution.py:56
  36.1 3.4 %collective-permute-start.1 = (bf16[256,2048]{1,0:T(8,128)(2,1)}, bf16[256,2048]{1,0:T(8,128)(2,1)}, u32[]{:S(2)}, u32[]{:S(2)}) collective-permute-start(bf16[256,2048]{1,0:T(8,128)(2,1)} %collective-permute-done.refs_0_), channel_id=1, source_target_pairs={{0,32},{2,98},{32,0},{34,66},{64,96},{66,34},{96,64},{98,2},{4,36}... | collective-permute-start | bytes 3145736 | tf_op jit(solution)/shard_map/ppermute | solution.py:56
  39.5 22.3 %all-to-all-done.x_ref = bf16[64,48,512]{2,1,0:T(8,128)(2,1)} async-done(((bf16[64,48,512]{2,1,0:T(8,128)(2,1)}), bf16[64,48,512]{2,1,0:T(8,128)(2,1)}, u32[]{:S(2)}, u32[]{:S(2)}) %all-to-all-start) | async-done | bytes 3145760 | tf_op jit(solution)/shard_map/all_to_all | solution.py:341
  61.8 6.7 %column_attention.1 = bf16[64,16,512]{2,1,0:T(8,128)(2,1)} custom-call(bf16[64,48,512]{2,1,0:T(8,128)(2,1)} %all-to-all-done.x_ref), custom_call_target="tpu_custom_call" | custom-call | flops 1048576 | bytes 1024 | tf_op jit(solution)/shard_map/column_attention/pallas_call | solution.py:159
  68.5 6.0 %all-to-all-start.1 = ((bf16[128,8,512]{2,1,0:T(8,128)(2,1)}), bf16[128,8,512]{2,1,0:T(8,128)(2,1)S(1)}, u32[]{:S(2)}, u32[]{:S(2)}) async-start(bf16[128,8,512]{2,1,0:T(8,128)(2,1)} %bitcast.12), calls=%async_computation.1 | async-start | bytes 2097152 | tf_op jit(solution)/shard_map/all_to_all | solution.py:351
  74.4 5.8 %collective-permute-done.3.refs_3_ = bf16[256,2048]{1,0:T(8,128)(2,1)} collective-permute-done((bf16[256,2048]{1,0:T(8,128)(2,1)S(1)}, bf16[256,2048]{1,0:T(8,128)(2,1)}, u32[]{:S(2)}, u32[]{:S(2)}) %collective-permute-start.3) | collective-permute-done | bytes 1048608 | tf_op jit(solution)/shard_map/ppermute | solution.py:56
  80.2 0.0 collective-permute-done.4.row_other
  80.2 0.0 collective-permute-done.2.refs_2_
  80.2 0.0 collective-permute-done.1.refs_1_
  80.2 0.8 collective-permute-start.5
  81.1 0.1 collective-permute-start.6
  81.2 0.4 collective-permute-start.7
  81.6 0.1 collective-permute-start.8
  81.7 14.5 %all-to-all-done.1 = bf16[128,8,512]{2,1,0:T(8,128)(2,1)S(1)} async-done(((bf16[128,8,512]{2,1,0:T(8,128)(2,1)}), bf16[128,8,512]{2,1,0:T(8,128)(2,1)S(1)}, u32[]{:S(2)}, u32[]{:S(2)}) %all-to-all-start.1) | async-done | bytes 1048608 | tf_op jit(solution)/shard_map/all_to_all | solution.py:351
  96.2 0.0 copy-done.1
  96.2 1.3 %join.1.a_ref = bf16[512,2048]{1,0:T(8,128)(2,1)S(1)} custom-call(s32[4]{0:T(128)S(1)} %copy-done.1, bf16[512,512]{1,0:T(8,128)(2,1)} %get-tuple-element.39.row_own, bf16[1024,512]{1,0:T(8,128)(2,1)S(1)} %collective-permute-done.4.row_other, bf16[64,2,8,512]{3,2,1,0:T(8,128)(2,1)S(1)} %bitcast.10), custom_call_target="tpu_custom_call" | custom-call | flops 274877906944 | bytes 1048576 | tf_op jit(solution)/shard_map/join/pallas_call | solution.py:193
  97.5 0.0 collective-permute-done.5.refs_4_
  97.6 0.0 collective-permute-done.6.refs_5_
  97.6 0.0 collective-permute-done.7.refs_6_
  97.6 0.0 collective-permute-done.8.refs_7_
  97.6 14.9 %project.1 = bf16[1,512,4096]{2,1,0:T(8,128)(2,1)} custom-call(s32[4]{0:T(128)S(1)} %copy-done.1, bf16[512,2048]{1,0:T(8,128)(2,1)S(1)} %join.1.a_ref, bf16[1024,4096]{1,0:T(8,128)(2,1)} %w_ref.3, bf16[256,2048]{1,0:T(8,128)(2,1)} %collective-permute-done.refs_0_, bf16[256,2048]{1,0:T(8,128)(2,1)} %collective-permute-done.1.refs_1_, ...), custom_call_target="tpu_custom_call" | custom-call | flops 1048576 | bytes 1024 | tf_op jit(solution)/shard_map/project/pallas_call | solution.py:230
Async XLA Ops:
  0.1 3.1 %copy-start = (s32[4]{0:T(128)}, s32[4]{0:T(128)S(1)}, u32[]{:S(2)}) copy-start(s32[4]{0:T(128)S(1)} %pad_add_fusion.s_ref) | copy-start | bytes 52
  3.2 17.0 %collective-permute-start = (bf16[256,2048]{1,0:T(8,128)(2,1)}, bf16[256,2048]{1,0:T(8,128)(2,1)}, u32[]{:S(2)}, u32[]{:S(2)}) collective-permute-start(bf16[256,2048]{1,0:T(8,128)(2,1)} %get-tuple-element.30), channel_id=1, source_target_pairs={{0,1},{2,19},{32,33},{34,51},{64,65},{66,83},{96,97},{98,115},{4,5... | collective-permute-start | bytes 3145736 | tf_op jit(solution)/shard_map/ppermute | solution.py:56
  9.7 52.1 %all-to-all-start = ((bf16[64,48,512]{2,1,0:T(8,128)(2,1)}), bf16[64,48,512]{2,1,0:T(8,128)(2,1)}, u32[]{:S(2)}, u32[]{:S(2)}) async-start(bf16[64,48,512]{2,1,0:T(8,128)(2,1)} %bitcast.11), calls=%async_computation | async-start | bytes 6291456 | tf_op jit(solution)/shard_map/all_to_all | solution.py:341
  20.2 10.8 %copy-start.2 = (bf16[256,2048]{1,0:T(8,128)(2,1)S(1)}, bf16[256,2048]{1,0:T(8,128)(2,1)}, u32[]{:S(2)}) copy-start(bf16[256,2048]{1,0:T(8,128)(2,1)} %get-tuple-element.41) | copy-start | bytes 3145732
  31.1 65.1 %copy-start.1 = (s32[4]{0:T(128)S(1)}, s32[4]{0:T(128)}, u32[]{:S(2)}) copy-start(s32[4]{0:T(128)} %copy-done) | copy-start | bytes 52
  31.1 49.1 %collective-permute-start.3 = (bf16[256,2048]{1,0:T(8,128)(2,1)S(1)}, bf16[256,2048]{1,0:T(8,128)(2,1)}, u32[]{:S(2)}, u32[]{:S(2)}) collective-permute-start(bf16[256,2048]{1,0:T(8,128)(2,1)S(1)} %copy-done.2), channel_id=1, source_target_pairs={{0,17},{2,19},{32,49},{34,51},{64,81},{66,83},{96,113},{98,115},{4... | collective-permute-start | bytes 3145736 | tf_op jit(solution)/shard_map/ppermute | solution.py:56
  33.1 47.1 %collective-permute-start.4 = (bf16[1024,512]{1,0:T(8,128)(2,1)}, bf16[1024,512]{1,0:T(8,128)(2,1)S(1)}, u32[]{:S(2)}, u32[]{:S(2)}) collective-permute-start(bf16[1024,512]{1,0:T(8,128)(2,1)} %get-tuple-element.42), channel_id=1, source_target_pairs={{0,1},{2,3},{32,33},{34,35},{64,65},{66,67},{96,97},{98,99},{4,5},... | collective-permute-start | bytes 3145736 | tf_op jit(solution)/shard_map/ppermute | solution.py:56
  33.7 46.5 %collective-permute-start.2 = (bf16[256,2048]{1,0:T(8,128)(2,1)}, bf16[256,2048]{1,0:T(8,128)(2,1)}, u32[]{:S(2)}, u32[]{:S(2)}) collective-permute-start(bf16[256,2048]{1,0:T(8,128)(2,1)} %collective-permute-done.refs_0_), channel_id=1, source_target_pairs={{0,4},{2,14},{32,36},{34,46},{64,68},{66,78},{96,100},{98,110},{4,... | collective-permute-start | bytes 3145736 | tf_op jit(solution)/shard_map/ppermute | solution.py:56
  36.1 44.1 %collective-permute-start.1 = (bf16[256,2048]{1,0:T(8,128)(2,1)}, bf16[256,2048]{1,0:T(8,128)(2,1)}, u32[]{:S(2)}, u32[]{:S(2)}) collective-permute-start(bf16[256,2048]{1,0:T(8,128)(2,1)} %collective-permute-done.refs_0_), channel_id=1, source_target_pairs={{0,32},{2,98},{32,0},{34,66},{64,96},{66,34},{96,64},{98,2},{4,36}... | collective-permute-start | bytes 3145736 | tf_op jit(solution)/shard_map/ppermute | solution.py:56
  68.5 27.7 %all-to-all-start.1 = ((bf16[128,8,512]{2,1,0:T(8,128)(2,1)}), bf16[128,8,512]{2,1,0:T(8,128)(2,1)S(1)}, u32[]{:S(2)}, u32[]{:S(2)}) async-start(bf16[128,8,512]{2,1,0:T(8,128)(2,1)} %bitcast.12), calls=%async_computation.1 | async-start | bytes 2097152 | tf_op jit(solution)/shard_map/all_to_all | solution.py:351
  80.2 17.3 %collective-permute-start.5 = (bf16[256,2048]{1,0:T(8,128)(2,1)}, bf16[256,2048]{1,0:T(8,128)(2,1)}, u32[]{:S(2)}, u32[]{:S(2)}) collective-permute-start(bf16[256,2048]{1,0:T(8,128)(2,1)} %collective-permute-done.refs_0_), channel_id=1, source_target_pairs={{0,2},{2,0},{32,34},{34,32},{64,66},{66,64},{96,98},{98,96},{4,6},... | collective-permute-start | bytes 3145736 | tf_op jit(solution)/shard_map/ppermute | solution.py:56
  81.1 16.5 %collective-permute-start.6 = (bf16[256,2048]{1,0:T(8,128)(2,1)}, bf16[256,2048]{1,0:T(8,128)(2,1)}, u32[]{:S(2)}, u32[]{:S(2)}) collective-permute-start(bf16[256,2048]{1,0:T(8,128)(2,1)} %collective-permute-done.1.refs_1_), channel_id=1, source_target_pairs={{0,2},{2,0},{32,34},{34,32},{64,66},{66,64},{96,98},{98,96},{4,6},... | collective-permute-start | bytes 3145736 | tf_op jit(solution)/shard_map/ppermute | solution.py:56
  81.2 16.4 %collective-permute-start.7 = (bf16[256,2048]{1,0:T(8,128)(2,1)}, bf16[256,2048]{1,0:T(8,128)(2,1)}, u32[]{:S(2)}, u32[]{:S(2)}) collective-permute-start(bf16[256,2048]{1,0:T(8,128)(2,1)} %collective-permute-done.2.refs_2_), channel_id=1, source_target_pairs={{0,2},{2,0},{32,34},{34,32},{64,66},{66,64},{96,98},{98,96},{4,6},... | collective-permute-start | bytes 3145736 | tf_op jit(solution)/shard_map/ppermute | solution.py:56
  81.6 16.0 %collective-permute-start.8 = (bf16[256,2048]{1,0:T(8,128)(2,1)}, bf16[256,2048]{1,0:T(8,128)(2,1)}, u32[]{:S(2)}, u32[]{:S(2)}) collective-permute-start(bf16[256,2048]{1,0:T(8,128)(2,1)} %collective-permute-done.3.refs_3_), channel_id=1, source_target_pairs={{0,2},{2,0},{32,34},{34,32},{64,66},{66,64},{96,98},{98,96},{4,6},... | collective-permute-start | bytes 3145736 | tf_op jit(solution)/shard_map/ppermute | solution.py:56

commit v3 on v2

--- a/solution.py
+++ b/solution.py
@@ -1,3 +1,4 @@
+import functools
 import itertools
 import math
 
@@ -126,6 +127,7 @@
 COLS = 16
 SUB = 16
 TOKENS = SUB * COLS
+AT_ONCE = 2
 
 
 def column_kernel(x_ref, o_ref):
@@ -134,10 +136,12 @@
     swap = ((to % SUB) * COLS + to // SUB == of).astype(jnp.bfloat16)
     back = ((to % COLS) * SUB + to // COLS == of).astype(jnp.bfloat16)
     blocks = ROWS // SUB
+    heads = o_ref.shape[2] // HD
+    width = heads * HD
     regrouped = []
     for b in range(blocks):
         x = x_ref[b * SUB : (b + 1) * SUB]
-        parts = [x[:, t * COLS : (t + 1) * COLS, :].reshape(TOKENS, HD) for t in range(3)]
+        parts = [x[:, t * COLS : (t + 1) * COLS, :].reshape(TOKENS, width) for t in range(3)]
         regrouped.append(dot_nn(swap, jnp.concatenate(parts, axis=1)).astype(jnp.bfloat16))
     span = TOKENS // blocks
     row_of = (to // span) * SUB + to % SUB
@@ -146,21 +150,24 @@
     outs = []
     for g in range(TOKENS // span):
         mine = jnp.concatenate([y[g * span : (g + 1) * span] for y in regrouped], axis=0)
-        q, k, v = (mine[:, t * HD : (t + 1) * HD] for t in range(3))
-        probs, total = softmax_rows(jnp.where(allowed, dot_nt(q, k), MASKED))
-        outs.append((dot_nn(probs, v) / total).astype(jnp.bfloat16))
+        across = []
+        for h in range(heads):
+            q, k, v = (mine[:, t * width + h * HD : t * width + (h + 1) * HD] for t in range(3))
+            probs, total = softmax_rows(jnp.where(allowed, dot_nt(q, k), MASKED))
+            across.append((dot_nn(probs, v) / total).astype(jnp.bfloat16))
+        outs.append(jnp.concatenate(across, axis=1))
     for b in range(blocks):
         y = jnp.concatenate([o[b * span : (b + 1) * span] for o in outs], axis=0)
         z = dot_nn(back, y).astype(jnp.bfloat16)
-        o_ref[b * SUB : (b + 1) * SUB] = z.reshape(SUB, COLS, HD)
+        o_ref[b * SUB : (b + 1) * SUB] = z.reshape(SUB, COLS, width)
 
 
 def column_attention(x):
     return pl.pallas_call(
         column_kernel,
-        grid=(GROUP,),
-        in_specs=[pl.BlockSpec((ROWS, 3 * COLS, HD), lambda h: (0, 0, h))],
-        out_specs=pl.BlockSpec((ROWS, COLS, HD), lambda h: (0, 0, h)),
+        grid=(GROUP // AT_ONCE,),
+        in_specs=[pl.BlockSpec((ROWS, 3 * COLS, AT_ONCE * HD), lambda h: (0, 0, h))],
+        out_specs=pl.BlockSpec((ROWS, COLS, AT_ONCE * HD), lambda h: (0, 0, h)),
         out_shape=pltpu.HBM((ROWS, COLS, LOCAL), jnp.bfloat16),
         compiler_params=pltpu.CompilerParams(vmem_limit_bytes=SMALL_VMEM),
         cost_estimate=COST,
@@ -168,96 +175,146 @@
     )(x)
 
 
-TILE = 512
+TILE = 1024
 TILES = WIDTH // TILE
-
-
-def tile_of(n, core):
-    return lax.rem(n + core * (TILES // 2), TILES)
-
-
-def join_kernel(s_ref, row_own, row_other, x_ref, a_ref):
-    mine, me = 2 * s_ref[1] + s_ref[2], s_ref[3]
-    a_ref[:, :LOCAL] = row_own[...]
-    a_ref[:, LOCAL : 2 * LOCAL] = x_ref[:, me].reshape(HALF, LOCAL)
-    other = x_ref[:, 1 - me].reshape(HALF, LOCAL)
-    quarters = [row_other[:, :PIECE], row_other[:, PIECE:], other[:, :PIECE], other[:, PIECE:]]
+CHUNK = 512
+CHUNKS = WIDTH // CHUNK
+WHOLE = pl.BlockSpec(memory_space=pltpu.VMEM)
+ANYWHERE = pl.BlockSpec(memory_space=pl.ANY)
+
+
+def own_rows_kernel(a_ref, w_ref, o_ref):
+    o_ref[...] = dot_nn(a_ref[...], w_ref[...]).astype(jnp.bfloat16)
+
+
+def project_own_rows(own, w_own):
+    return pl.pallas_call(
+        own_rows_kernel,
+        grid=(TILES,),
+        in_specs=[
+            pl.BlockSpec((HALF, LOCAL), lambda n: (0, 0)),
+            pl.BlockSpec((LOCAL, TILE), lambda n: (0, n)),
+        ],
+        out_specs=pl.BlockSpec((HALF, TILE), lambda n: (0, n)),
+        out_shape=pltpu.HBM((HALF, WIDTH), jnp.bfloat16),
+        compiler_params=pltpu.CompilerParams(vmem_limit_bytes=SMALL_VMEM),
+        cost_estimate=COST,
+        name="own_rows",
+    )(in_hbm(own), in_hbm(w_own))
+
+
+def join_kernel(s_ref, x_ref, a_ref):
+    me = s_ref[3]
+    a_ref[:, :LOCAL] = x_ref[:, me].reshape(HALF, LOCAL)
+    a_ref[:, LOCAL:] = x_ref[:, 1 - me].reshape(HALF, LOCAL)
+
+
+def join(place, attended):
+    return pl.pallas_call(
+        join_kernel,
+        in_specs=[pl.BlockSpec(memory_space=pltpu.SMEM), WHOLE],
+        out_specs=WHOLE,
+        out_shape=jax.ShapeDtypeStruct((HALF, 2 * LOCAL), jnp.bfloat16),
+        compiler_params=pltpu.CompilerParams(vmem_limit_bytes=SMALL_VMEM),
+        cost_estimate=LONG,
+        name="join",
+    )(place, attended)
+
+
+def project_kernel(s_ref, x_ref, y_ref, acc_ref, w_ref, *refs):
+    pieces, o_ref = refs[:8], refs[8]
+    a_buf, w_buf, acc_buf, o_buf, load_sems, store_sems = refs[9:]
+    core, mine = s_ref[0], 2 * s_ref[1] + s_ref[2]
+    half = CHUNKS // 2
+
+    def columns_of(n):
+        at = lax.rem(n + core * half, CHUNKS)
+        return pl.ds(pl.multiple_of(at * CHUNK, CHUNK), CHUNK)
+
+    def loads_of(n):
+        columns = columns_of(n)
+        there = pl.ds(n % half * CHUNK, CHUNK)
+        rows = pl.ds(LOCAL, LOCAL)
+        loads = [
+            pltpu.make_async_copy(acc_ref.at[:, columns], acc_buf.at[n], load_sems.at[n, 0]),
+            pltpu.make_async_copy(
+                w_ref.at[rows, columns], w_buf.at[n, pl.ds(0, LOCAL)], load_sems.at[n, 1]
+            ),
+        ]
+        for i, piece in enumerate(pieces[:4] if n < half else pieces[4:]):
+            to = w_buf.at[n, pl.ds(LOCAL + i * PIECE, PIECE)]
+            loads.append(pltpu.make_async_copy(piece.at[:, there], to, load_sems.at[n, 2 + i]))
+        return loads
+
+    def store_of(n):
+        return pltpu.make_async_copy(o_buf.at[n], o_ref.at[0, :, columns_of(n)], store_sems.at[n])
+
+    for n in range(CHUNKS):
+        for load in loads_of(n):
+            load.start()
+    a_buf[:, :LOCAL] = y_ref[:, :LOCAL]
     for i in range(4):
-        picked = quarters[0]
-        for q in range(1, 4):
-            picked = jnp.where(lax.bitwise_xor(mine, i) == q, quarters[q], picked)
-        a_ref[:, 2 * LOCAL + i * PIECE : 2 * LOCAL + (i + 1) * PIECE] = picked
-
-
-def join(place, row_own, row_other, attended):
-    return pl.pallas_call(
-        join_kernel,
-        grid=(1,),
+        quarter = lax.bitwise_xor(mine, i)
+        to = slice(LOCAL + i * PIECE, LOCAL + (i + 1) * PIECE)
+
+        @pl.when(quarter < 2)
+        def _():
+            a_buf[:, to] = x_ref[:HALF, pl.ds(pl.multiple_of(quarter * PIECE, PIECE), PIECE)]
+
+        @pl.when(quarter >= 2)
+        def _():
+            a_buf[:, to] = y_ref[:, pl.ds(pl.multiple_of(quarter * PIECE, PIECE), PIECE)]
+
+    for n in range(CHUNKS):
+        for load in loads_of(n):
+            load.wait()
+        total = acc_buf[n].astype(jnp.float32) + dot_nn(a_buf[...], w_buf[n])
+        o_buf[n] = total.astype(jnp.bfloat16)
+        store_of(n).start()
+    for n in range(CHUNKS):
+        store_of(n).wait()
+
+
+def project(place, row_other, joined, acc, w_own, pieces):
+    depth = LOCAL + 4 * PIECE
+    return pl.pallas_call(
+        project_kernel,
         in_specs=[
             pl.BlockSpec(memory_space=pltpu.SMEM),
-            pl.BlockSpec((HALF, LOCAL), lambda n: (0, 0)),
-            pl.BlockSpec((HALF, LOCAL), lambda n: (0, 0)),
-            pl.BlockSpec((ROWS, 2, 8, LOCAL), lambda n: (0, 0, 0, 0)),
-        ],
-        out_shape=jax.ShapeDtypeStruct((HALF, 4 * LOCAL), jnp.bfloat16),
-        compiler_params=pltpu.CompilerParams(vmem_limit_bytes=SMALL_VMEM),
-        cost_estimate=LONG,
-        name="join",
-    )(place, in_hbm(row_own), row_other, attended)
-
-
-def project_kernel(s_ref, a_ref, w_ref, *refs):
-    near, far, o_ref = refs[:4], refs[4:8], refs[8]
-    n = pl.program_id(0)
-
-    def product(pieces):
-        weights = jnp.concatenate([w_ref[...], *[p[...] for p in pieces]], axis=0)
-        o_ref[0] = dot_nn(a_ref[...], weights).astype(jnp.bfloat16)
-
-    @pl.when(n < TILES // 2)
-    def _():
-        product(near)
-
-    @pl.when(n >= TILES // 2)
-    def _():
-        product(far)
-
-
-def project(place, joined, w_own, pieces):
-    half = TILES // 2
-    near = pl.BlockSpec((PIECE, TILE), lambda n, s: (0, jnp.minimum(n, half - 1)))
-    far = pl.BlockSpec((PIECE, TILE), lambda n, s: (0, jnp.maximum(n - half, 0)))
-    return pl.pallas_call(
-        project_kernel,
-        grid_spec=pltpu.PrefetchScalarGridSpec(
-            num_scalar_prefetch=1,
-            grid=(TILES,),
-            in_specs=[
-                pl.BlockSpec((HALF, 4 * LOCAL), lambda n, s: (0, 0)),
-                pl.BlockSpec((2 * LOCAL, TILE), lambda n, s: (0, tile_of(n, s[0]))),
-                *[near] * 4,
-                *[far] * 4,
-            ],
-            out_specs=pl.BlockSpec((1, HALF, TILE), lambda n, s: (0, 0, tile_of(n, s[0]))),
-        ),
-        out_shape=jax.ShapeDtypeStruct((1, HALF, WIDTH), jnp.bfloat16),
-        compiler_params=pltpu.CompilerParams(vmem_limit_bytes=24 << 20),
+            WHOLE,
+            WHOLE,
+            *[ANYWHERE] * 10,
+        ],
+        out_specs=ANYWHERE,
+        out_shape=pltpu.HBM((1, HALF, WIDTH), jnp.bfloat16),
+        scratch_shapes=[
+            pltpu.VMEM((HALF, depth), jnp.bfloat16),
+            pltpu.VMEM((CHUNKS, depth, CHUNK), jnp.bfloat16),
+            pltpu.VMEM((CHUNKS, HALF, CHUNK), jnp.bfloat16),
+            pltpu.VMEM((CHUNKS, HALF, CHUNK), jnp.bfloat16),
+            pltpu.SemaphoreType.DMA((CHUNKS, 6)),
+            pltpu.SemaphoreType.DMA((CHUNKS,)),
+        ],
+        compiler_params=pltpu.CompilerParams(vmem_limit_bytes=40 << 20),
         cost_estimate=COST,
         name="project",
-    )(place, joined, in_hbm(w_own), *map(in_hbm, pieces))
-
-
-def slice_kernel(s_ref, w_ref, x_ref, y_ref, buf, in_sems, out_sems):
+    )(place, row_other, joined, in_hbm(acc), in_hbm(w_own), *map(in_hbm, pieces))
+
+
+def slice_kernel(opposite, s_ref, w_ref, x_ref, buf, in_sems, out_sems):
     columns = pl.ds(pl.multiple_of(s_ref[0] * HALF_WIDTH, HALF_WIDTH), HALF_WIDTH)
-    outs = (x_ref, y_ref)
-    mine = 2 * s_ref[1] + s_ref[2]
+    quarter = 2 * s_ref[1] + s_ref[2]
+    if opposite:
+        quarter = 3 - quarter
     loads, stores = [], []
-    for i, quarter in enumerate((mine, 3 - mine)):
-        start = pl.multiple_of(quarter * PIECE, PIECE)
+    step = PIECE // SLICE_STEPS
+    for n in range(SLICE_STEPS):
+        start = pl.multiple_of(quarter * PIECE + n * step, step)
+        at = pl.ds(n * step, step)
         loads.append(
-            pltpu.make_async_copy(w_ref.at[pl.ds(start, PIECE), columns], buf.at[i], in_sems.at[i])
+            pltpu.make_async_copy(w_ref.at[pl.ds(start, step), columns], buf.at[at], in_sems.at[n])
         )
-        stores.append(pltpu.make_async_copy(buf.at[i], outs[i], out_sems.at[i]))
+        stores.append(pltpu.make_async_copy(buf.at[at], x_ref.at[at], out_sems.at[n]))
     for load in loads:
         load.start()
     for load, store in zip(loads, stores):
@@ -267,21 +324,23 @@
         store.wait()
 
 
-def slices(place, w_out):
-    shape = pltpu.HBM((PIECE, HALF_WIDTH), jnp.bfloat16)
-    return pl.pallas_call(
-        slice_kernel,
+SLICE_STEPS = 4
+
+
+def slice_of(place, w_out, opposite):
+    return pl.pallas_call(
+        functools.partial(slice_kernel, opposite),
         in_specs=[pl.BlockSpec(memory_space=pltpu.SMEM), pl.BlockSpec(memory_space=pl.ANY)],
-        out_specs=[pl.BlockSpec(memory_space=pl.ANY)] * 2,
-        out_shape=[shape, shape],
+        out_specs=pl.BlockSpec(memory_space=pl.ANY),
+        out_shape=pltpu.HBM((PIECE, HALF_WIDTH), jnp.bfloat16),
         scratch_shapes=[
-            pltpu.VMEM((2, PIECE, HALF_WIDTH), jnp.bfloat16),
-            pltpu.SemaphoreType.DMA((2,)),
-            pltpu.SemaphoreType.DMA((2,)),
+            pltpu.VMEM((PIECE, HALF_WIDTH), jnp.bfloat16),
+            pltpu.SemaphoreType.DMA((SLICE_STEPS,)),
+            pltpu.SemaphoreType.DMA((SLICE_STEPS,)),
         ],
         compiler_params=pltpu.CompilerParams(vmem_limit_bytes=SMALL_VMEM),
         cost_estimate=COST,
-        name="slices",
+        name="slice",
     )(place, in_hbm(w_out))
 
 
@@ -335,22 +394,26 @@
 
 def on_device(queries, keys, values, w_out):
     place = jnp.stack([*position(), lax.axis_index("head")])
-    pieces, *col_qkv = lax.optimization_barrier((slices(place, w_out), queries, keys, values))
-    mine = permute(pieces[0], ALONG_X)
+    piece, *col_qkv = lax.optimization_barrier(
+        (slice_of(place, w_out, False), queries, keys, values)
+    )
+    mine = permute(piece, ALONG_X)
     sent = packed(*col_qkv)
     arrived = lax.all_to_all(sent, "ctx", split_axis=0, concat_axis=0, tiled=True)
-    mine, away, *row_qkv = lax.optimization_barrier((mine, pieces[1], queries, keys, values))
+    mine, w_late, *row_qkv = lax.optimization_barrier((mine, w_out, queries, keys, values))
+    away = slice_of(place, w_late, True)
     row_own, row_away = row_attention(*row_qkv)
-    mine, away, row_own, row_away = lax.optimization_barrier((mine, away, row_own, row_away))
-    quarters = [mine, permute(mine, ALONG_Z), permute(mine, ALONG_Y), permute(away, ALONG_N)]
+    acc = project_own_rows(row_own, w_out)
+    mine, away, row_away, acc = lax.optimization_barrier((mine, away, row_away, acc))
+    near = [mine, permute(mine, ALONG_Z), permute(mine, ALONG_Y), permute(away, ALONG_N)]
     row_other = permute(row_away, TO_HEAD)
     col = column_attention(arrived)
-    *quarters, row_other, _ = lax.optimization_barrier((*quarters, row_other, col))
-    quarters += [permute(quarter, TO_CORE) for quarter in quarters]
+    near, row_other, _ = lax.optimization_barrier((near, row_other, col))
+    far = [permute(piece, TO_CORE) for piece in near]
     col = col.reshape(2 * ROWS, 8, LOCAL)
     col = lax.all_to_all(col, ("ctx", "head"), split_axis=0, concat_axis=0, tiled=True)
-    joined = join(place, row_own, row_other, col.reshape(ROWS, 2, 8, LOCAL))
-    return project(place, joined, w_out, quarters)
+    joined = join(place, col.reshape(ROWS, 2, 8, LOCAL))
+    return project(place, row_other, joined, acc, w_out, near + far)
 
 
 def solution(mesh):

time: 113 us -> 108 us (0.956)
  waiting for transfers between devices: 42.6 us -> 35 us
  Pallas kernels: 39.9 us -> 42.8 us
    all_to_all x1, waiting for transfers between devices: 22.3 us -> 13.5 us  [on_device(): lax.all_to_all(sent, 'ctx', split_axis=0, concat_axis=0, tiled=True)]
    pallas_call x4 -> x6, Pallas kernels: 26 us -> 28.9 us  [the longest x1 11.3 us: project(): pl.pallas_call(project_kernel, in_specs=[pl.BlockSpec(memory_space=pltpu....]
    ppermute x9, waiting for transfers between devices: 5.82 us -> 6.96 us  [permute(): return lax.ppermute(x, ('ctx', 'head'), pairs)]
  transfers between devices with their start and end apart: 11 -> 11, of which waited for: 3 -> 3; matrix products, arithmetic and copies ran while one was open for 0% -> 0% of each run, Pallas kernels for 19% -> 27%
where the time goes in v3:
time: 108 us
  Pallas kernels  42.8 us (40%)
  waiting for transfers between devices  35 us (32%)
  starting transfers between devices  29.6 us (27%)
    all_to_all x1, waiting for transfers between devices, on_device(): lax.all_to_all(col, ('ctx', 'head'), split_axis=0, concat_axis=0, tiled=T...  14.5 us
    all_to_all x1, waiting for transfers between devices, on_device(): lax.all_to_all(sent, 'ctx', split_axis=0, concat_axis=0, tiled=True)  13.5 us
    ppermute x9, starting transfers between devices, permute(): return lax.ppermute(x, ('ctx', 'head'), pairs)  13.1 us
    pallas_call x1, Pallas kernels, project(): pl.pallas_call(project_kernel, in_specs=[pl.BlockSpec(memory_space=pltpu....  11.3 us
    pallas_call x1, Pallas kernels, row_attention(): pl.pallas_call(row_kernel, grid=(GROUP,), in_specs=[spec] * 3, out_specs=...  10.7 us
    all_to_all x1, starting transfers between devices, on_device(): lax.all_to_all(sent, 'ctx', split_axis=0, concat_axis=0, tiled=True)  10.5 us
    ppermute x9, waiting for transfers between devices, permute(): return lax.ppermute(x, ('ctx', 'head'), pairs)  6.96 us
    pallas_call x1, Pallas kernels, project_own_rows(): pl.pallas_call(own_rows_kernel, grid=(TILES,), in_specs=[pl.BlockSpec((HA...  6.33 us
  transfers between devices with their start and end apart: 11, of which 3 were waited for; matrix products, arithmetic and copies ran while one was open for 0% of the time, Pallas kernels for 27%

profile of v3, /device:TPU:1, one launch (start us, length us, event | category | flops | bytes accessed | tf_op | source)
XLA Modules:
  0.0 107.7 jit_solution(4760520619165129403)
XLA Ops:
  0.0 0.1 pad_add_fusion.s_ref
  0.1 0.0 copy-start
  0.1 2.5 %slice.2 = bf16[256,2048]{1,0:T(8,128)(2,1)} custom-call(s32[4]{0:T(128)S(1)} %pad_add_fusion.s_ref, bf16[1024,4096]{1,0:T(8,128)(2,1)} %w_ref.6), custom_call_target="tpu_custom_call" | custom-call | flops 1048576 | bytes 1024 | tf_op jit(solution)/shard_map/slice/pallas_call | solution.py:331
  2.6 0.0 copy-done
  2.6 3.4 %collective-permute-start = (bf16[256,2048]{1,0:T(8,128)(2,1)}, bf16[256,2048]{1,0:T(8,128)(2,1)}, u32[]{:S(2)}, u32[]{:S(2)}) collective-permute-start(bf16[256,2048]{1,0:T(8,128)(2,1)} %slice.2), channel_id=1, source_target_pairs={{0,1},{2,19},{32,33},{34,51},{64,65},{66,83},{96,97},{98,115},{4,5... | collective-permute-start | bytes 3145736 | tf_op jit(solution)/shard_map/ppermute | solution.py:57
  6.0 3.1 %pack.1 = bf16[64,6,8,512]{3,2,1,0:T(8,128)(2,1)} custom-call(bf16[1,2,64,8,1024]{4,3,2,1,0:T(8,128)(2,1)} %bitcast.13, bf16[1,2,64,8,1024]{4,3,2,1,0:T(8,128)(2,1)} %bitcast.14, bf16[1,2,64,8,1024]{4,3,2,1,0:T(8,128)(2,1)} %bitcast.15), custom_call_target="tpu_custom_call" | custom-call | flops 1048576 | bytes 1024 | tf_op jit(solution)/shard_map/pack/pallas_call | solution.py:379
  9.1 10.5 %all-to-all-start = ((bf16[64,48,512]{2,1,0:T(8,128)(2,1)}), bf16[64,48,512]{2,1,0:T(8,128)(2,1)}, u32[]{:S(2)}, u32[]{:S(2)}) async-start(bf16[64,48,512]{2,1,0:T(8,128)(2,1)} %bitcast.11), calls=%async_computation | async-start | bytes 6291456 | tf_op jit(solution)/shard_map/all_to_all | solution.py:402
  19.7 0.0 collective-permute-done.refs_0_
  19.7 0.0 copy-start.1
  19.7 10.7 %row_attention.1 = (bf16[512,512]{1,0:T(8,128)(2,1)}, bf16[1024,512]{1,0:T(8,128)(2,1)}) custom-call(bf16[1,1024,1024]{2,1,0:T(8,128)(2,1)} %q_ref, bf16[1,1024,1024]{2,1,0:T(8,128)(2,1)} %k_ref, bf16[1,1024,1024]{2,1,0:T(8,128)(2,1)} %v_ref), custom_call_target="tpu_custom_call" | custom-call | flops 274877906944 | bytes 1048576 | tf_op jit(solution)/shard_map/row_attention/pallas_call | solution.py:109
  30.4 0.0 copy-done.1
  30.4 2.6 %slice.3 = bf16[256,2048]{1,0:T(8,128)(2,1)} custom-call(s32[4]{0:T(128)S(1)} %copy-done.1, bf16[1024,4096]{1,0:T(8,128)(2,1)} %w_ref.6), custom_call_target="tpu_custom_call" | custom-call | flops 1048576 | bytes 1024 | tf_op jit(solution)/shard_map/slice/pallas_call | solution.py:331
  33.0 0.0 copy-start.2
  33.1 6.3 %own_rows.1.acc_ref = bf16[512,4096]{1,0:T(8,128)(2,1)} custom-call(bf16[512,512]{1,0:T(8,128)(2,1)} %get-tuple-element.32.a_ref, bf16[1024,4096]{1,0:T(8,128)(2,1)} %w_ref.6), custom_call_target="tpu_custom_call" | custom-call | flops 1048576 | bytes 1024 | tf_op jit(solution)/shard_map/own_rows/pallas_call | solution.py:191
  39.4 0.0 copy-done.2
  39.4 1.9 %collective-permute-start.3 = (bf16[256,2048]{1,0:T(8,128)(2,1)S(1)}, bf16[256,2048]{1,0:T(8,128)(2,1)}, u32[]{:S(2)}, u32[]{:S(2)}) collective-permute-start(bf16[256,2048]{1,0:T(8,128)(2,1)S(1)} %copy-done.2), channel_id=1, source_target_pairs={{0,17},{2,19},{32,49},{34,51},{64,81},{66,83},{96,113},{98,115},{4... | collective-permute-start | bytes 3145736 | tf_op jit(solution)/shard_map/ppermute | solution.py:57
  41.3 0.7 collective-permute-start.4
  42.0 2.4 %collective-permute-start.2 = (bf16[256,2048]{1,0:T(8,128)(2,1)}, bf16[256,2048]{1,0:T(8,128)(2,1)}, u32[]{:S(2)}, u32[]{:S(2)}) collective-permute-start(bf16[256,2048]{1,0:T(8,128)(2,1)} %collective-permute-done.refs_0_), channel_id=1, source_target_pairs={{0,4},{2,14},{32,36},{34,46},{64,68},{66,78},{96,100},{98,110},{4,... | collective-permute-start | bytes 3145736 | tf_op jit(solution)/shard_map/ppermute | solution.py:57
  44.3 3.3 %collective-permute-start.1 = (bf16[256,2048]{1,0:T(8,128)(2,1)}, bf16[256,2048]{1,0:T(8,128)(2,1)}, u32[]{:S(2)}, u32[]{:S(2)}) collective-permute-start(bf16[256,2048]{1,0:T(8,128)(2,1)} %collective-permute-done.refs_0_), channel_id=1, source_target_pairs={{0,32},{2,98},{32,0},{34,66},{64,96},{66,34},{96,64},{98,2},{4,36}... | collective-permute-start | bytes 3145736 | tf_op jit(solution)/shard_map/ppermute | solution.py:57
  47.7 13.5 %all-to-all-done.x_ref = bf16[64,48,512]{2,1,0:T(8,128)(2,1)} async-done(((bf16[64,48,512]{2,1,0:T(8,128)(2,1)}), bf16[64,48,512]{2,1,0:T(8,128)(2,1)}, u32[]{:S(2)}, u32[]{:S(2)}) %all-to-all-start) | async-done | bytes 3145760 | tf_op jit(solution)/shard_map/all_to_all | solution.py:402
  61.2 5.6 %column_attention.1 = bf16[64,16,512]{2,1,0:T(8,128)(2,1)} custom-call(bf16[64,48,512]{2,1,0:T(8,128)(2,1)} %all-to-all-done.x_ref), custom_call_target="tpu_custom_call" | custom-call | flops 1048576 | bytes 1024 | tf_op jit(solution)/shard_map/column_attention/pallas_call | solution.py:166
  66.8 5.9 %all-to-all-start.1 = ((bf16[128,8,512]{2,1,0:T(8,128)(2,1)}), bf16[128,8,512]{2,1,0:T(8,128)(2,1)S(1)}, u32[]{:S(2)}, u32[]{:S(2)}) async-start(bf16[128,8,512]{2,1,0:T(8,128)(2,1)} %bitcast.12), calls=%async_computation.1 | async-start | bytes 2097152 | tf_op jit(solution)/shard_map/all_to_all | solution.py:414
  72.7 6.9 %collective-permute-done.3.refs_3_ = bf16[256,2048]{1,0:T(8,128)(2,1)} collective-permute-done((bf16[256,2048]{1,0:T(8,128)(2,1)S(1)}, bf16[256,2048]{1,0:T(8,128)(2,1)}, u32[]{:S(2)}, u32[]{:S(2)}) %collective-permute-start.3) | collective-permute-done | bytes 1048608 | tf_op jit(solution)/shard_map/ppermute | solution.py:57
  79.7 0.0 collective-permute-done.4.x_ref
  79.7 0.0 collective-permute-done.2.refs_2_
  79.7 0.0 collective-permute-done.1.refs_1_
  79.7 0.8 collective-permute-start.5
  80.5 0.1 collective-permute-start.6
  80.6 0.4 collective-permute-start.7
  81.0 0.1 collective-permute-start.8
  81.1 14.5 %all-to-all-done.1 = bf16[128,8,512]{2,1,0:T(8,128)(2,1)S(1)} async-done(((bf16[128,8,512]{2,1,0:T(8,128)(2,1)}), bf16[128,8,512]{2,1,0:T(8,128)(2,1)S(1)}, u32[]{:S(2)}, u32[]{:S(2)}) %all-to-all-start.1) | async-done | bytes 1048608 | tf_op jit(solution)/shard_map/all_to_all | solution.py:414
  95.6 0.6 join.1.y_ref
  96.2 0.0 collective-permute-done.5.refs_4_
  96.3 0.0 collective-permute-done.6.refs_5_
  96.3 0.0 collective-permute-done.7.refs_6_
  96.3 0.0 collective-permute-done.8.refs_7_
  96.3 11.3 %project.1 = bf16[1,512,4096]{2,1,0:T(8,128)(2,1)} custom-call(s32[4]{0:T(128)S(1)} %copy-done.1, bf16[1024,512]{1,0:T(8,128)(2,1)S(1)} %collective-permute-done.4.x_ref, bf16[512,1024]{1,0:T(8,128)(2,1)S(1)} %join.1.y_ref, bf16[512,4096]{1,0:T(8,128)(2,1)} %own_rows.1.acc_ref, bf16[1024,4096]{1,0:T(8,128)(2,1)} %w_ref.6, ...), custom_call_target="tpu_custom_call" | custom-call | flops 1048576 | bytes 1024 | tf_op jit(solution)/shard_map/project/pallas_call | solution.py:280
Async XLA Ops:
  0.1 2.6 %copy-start = (s32[4]{0:T(128)}, s32[4]{0:T(128)S(1)}, u32[]{:S(2)}) copy-start(s32[4]{0:T(128)S(1)} %pad_add_fusion.s_ref) | copy-start | bytes 52
  2.6 17.0 %collective-permute-start = (bf16[256,2048]{1,0:T(8,128)(2,1)}, bf16[256,2048]{1,0:T(8,128)(2,1)}, u32[]{:S(2)}, u32[]{:S(2)}) collective-permute-start(bf16[256,2048]{1,0:T(8,128)(2,1)} %slice.2), channel_id=1, source_target_pairs={{0,1},{2,19},{32,33},{34,51},{64,65},{66,83},{96,97},{98,115},{4,5... | collective-permute-start | bytes 3145736 | tf_op jit(solution)/shard_map/ppermute | solution.py:57
  9.1 52.1 %all-to-all-start = ((bf16[64,48,512]{2,1,0:T(8,128)(2,1)}), bf16[64,48,512]{2,1,0:T(8,128)(2,1)}, u32[]{:S(2)}, u32[]{:S(2)}) async-start(bf16[64,48,512]{2,1,0:T(8,128)(2,1)} %bitcast.11), calls=%async_computation | async-start | bytes 6291456 | tf_op jit(solution)/shard_map/all_to_all | solution.py:402
  19.7 10.7 %copy-start.1 = (s32[4]{0:T(128)S(1)}, s32[4]{0:T(128)}, u32[]{:S(2)}) copy-start(s32[4]{0:T(128)} %copy-done) | copy-start | bytes 52
  33.0 6.3 %copy-start.2 = (bf16[256,2048]{1,0:T(8,128)(2,1)S(1)}, bf16[256,2048]{1,0:T(8,128)(2,1)}, u32[]{:S(2)}) copy-start(bf16[256,2048]{1,0:T(8,128)(2,1)} %slice.3) | copy-start | bytes 3145732
  39.4 40.3 %collective-permute-start.3 = (bf16[256,2048]{1,0:T(8,128)(2,1)S(1)}, bf16[256,2048]{1,0:T(8,128)(2,1)}, u32[]{:S(2)}, u32[]{:S(2)}) collective-permute-start(bf16[256,2048]{1,0:T(8,128)(2,1)S(1)} %copy-done.2), channel_id=1, source_target_pairs={{0,17},{2,19},{32,49},{34,51},{64,81},{66,83},{96,113},{98,115},{4... | collective-permute-start | bytes 3145736 | tf_op jit(solution)/shard_map/ppermute | solution.py:57
  41.3 38.4 %collective-permute-start.4 = (bf16[1024,512]{1,0:T(8,128)(2,1)}, bf16[1024,512]{1,0:T(8,128)(2,1)S(1)}, u32[]{:S(2)}, u32[]{:S(2)}) collective-permute-start(bf16[1024,512]{1,0:T(8,128)(2,1)} %get-tuple-element.35), channel_id=1, source_target_pairs={{0,1},{2,3},{32,33},{34,35},{64,65},{66,67},{96,97},{98,99},{4,5},... | collective-permute-start | bytes 3145736 | tf_op jit(solution)/shard_map/ppermute | solution.py:57
  42.0 37.7 %collective-permute-start.2 = (bf16[256,2048]{1,0:T(8,128)(2,1)}, bf16[256,2048]{1,0:T(8,128)(2,1)}, u32[]{:S(2)}, u32[]{:S(2)}) collective-permute-start(bf16[256,2048]{1,0:T(8,128)(2,1)} %collective-permute-done.refs_0_), channel_id=1, source_target_pairs={{0,4},{2,14},{32,36},{34,46},{64,68},{66,78},{96,100},{98,110},{4,... | collective-permute-start | bytes 3145736 | tf_op jit(solution)/shard_map/ppermute | solution.py:57
  44.3 35.3 %collective-permute-start.1 = (bf16[256,2048]{1,0:T(8,128)(2,1)}, bf16[256,2048]{1,0:T(8,128)(2,1)}, u32[]{:S(2)}, u32[]{:S(2)}) collective-permute-start(bf16[256,2048]{1,0:T(8,128)(2,1)} %collective-permute-done.refs_0_), channel_id=1, source_target_pairs={{0,32},{2,98},{32,0},{34,66},{64,96},{66,34},{96,64},{98,2},{4,36}... | collective-permute-start | bytes 3145736 | tf_op jit(solution)/shard_map/ppermute | solution.py:57
  66.8 28.8 %all-to-all-start.1 = ((bf16[128,8,512]{2,1,0:T(8,128)(2,1)}), bf16[128,8,512]{2,1,0:T(8,128)(2,1)S(1)}, u32[]{:S(2)}, u32[]{:S(2)}) async-start(bf16[128,8,512]{2,1,0:T(8,128)(2,1)} %bitcast.12), calls=%async_computation.1 | async-start | bytes 2097152 | tf_op jit(solution)/shard_map/all_to_all | solution.py:414
  79.7 16.6 %collective-permute-start.5 = (bf16[256,2048]{1,0:T(8,128)(2,1)}, bf16[256,2048]{1,0:T(8,128)(2,1)}, u32[]{:S(2)}, u32[]{:S(2)}) collective-permute-start(bf16[256,2048]{1,0:T(8,128)(2,1)} %collective-permute-done.refs_0_), channel_id=1, source_target_pairs={{0,2},{2,0},{32,34},{34,32},{64,66},{66,64},{96,98},{98,96},{4,6},... | collective-permute-start | bytes 3145736 | tf_op jit(solution)/shard_map/ppermute | solution.py:57
  80.5 15.7 %collective-permute-start.6 = (bf16[256,2048]{1,0:T(8,128)(2,1)}, bf16[256,2048]{1,0:T(8,128)(2,1)}, u32[]{:S(2)}, u32[]{:S(2)}) collective-permute-start(bf16[256,2048]{1,0:T(8,128)(2,1)} %collective-permute-done.1.refs_1_), channel_id=1, source_target_pairs={{0,2},{2,0},{32,34},{34,32},{64,66},{66,64},{96,98},{98,96},{4,6},... | collective-permute-start | bytes 3145736 | tf_op jit(solution)/shard_map/ppermute | solution.py:57
  80.6 15.7 %collective-permute-start.7 = (bf16[256,2048]{1,0:T(8,128)(2,1)}, bf16[256,2048]{1,0:T(8,128)(2,1)}, u32[]{:S(2)}, u32[]{:S(2)}) collective-permute-start(bf16[256,2048]{1,0:T(8,128)(2,1)} %collective-permute-done.2.refs_2_), channel_id=1, source_target_pairs={{0,2},{2,0},{32,34},{34,32},{64,66},{66,64},{96,98},{98,96},{4,6},... | collective-permute-start | bytes 3145736 | tf_op jit(solution)/shard_map/ppermute | solution.py:57
  81.0 15.3 %collective-permute-start.8 = (bf16[256,2048]{1,0:T(8,128)(2,1)}, bf16[256,2048]{1,0:T(8,128)(2,1)}, u32[]{:S(2)}, u32[]{:S(2)}) collective-permute-start(bf16[256,2048]{1,0:T(8,128)(2,1)} %collective-permute-done.3.refs_3_), channel_id=1, source_target_pairs={{0,2},{2,0},{32,34},{34,32},{64,66},{66,64},{96,98},{98,96},{4,6},... | collective-permute-start | bytes 3145736 | tf_op jit(solution)/shard_map/ppermute | solution.py:57

commit v4 on v3

--- a/solution.py
+++ b/solution.py
@@ -203,10 +203,52 @@
     )(in_hbm(own), in_hbm(w_own))
 
 
+def head_of(s_ref, i):
+    head = lax.bitwise_xor(2 * s_ref[1] + s_ref[2], i)
+    return pl.ds(pl.multiple_of(head * HD, HD), HD)
+
+
+def other_rows_kernel(s_ref, a_ref, acc_ref, *refs):
+    pieces, o_ref, join_ref = refs[:4], refs[4], refs[5]
+
+    @pl.when(pl.program_id(0) == 0)
+    def _():
+        for i in range(4):
+            join_ref[:, i * HD : (i + 1) * HD] = a_ref[:, head_of(s_ref, i)]
+
+    weights = jnp.concatenate([piece[...] for piece in pieces], axis=0)
+    total = acc_ref[...].astype(jnp.float32) + dot_nn(join_ref[...], weights)
+    o_ref[...] = total.astype(jnp.bfloat16)
+
+
+def project_other_rows(place, other, acc, pieces):
+    half = TILES // 2
+    return pl.pallas_call(
+        other_rows_kernel,
+        grid_spec=pltpu.PrefetchScalarGridSpec(
+            num_scalar_prefetch=1,
+            grid=(half,),
+            in_specs=[
+                pl.BlockSpec((HALF, LOCAL), lambda n, s: (0, 0)),
+                pl.BlockSpec((HALF, TILE), lambda n, s: (0, n + s[0] * half)),
+                *[pl.BlockSpec((HD, TILE), lambda n, s: (0, n))] * 4,
+            ],
+            out_specs=pl.BlockSpec((HALF, TILE), lambda n, s: (0, n)),
+            scratch_shapes=[pltpu.VMEM((HALF, LOCAL), jnp.bfloat16)],
+        ),
+        out_shape=pltpu.HBM((HALF, HALF_WIDTH), jnp.bfloat16),
+        compiler_params=pltpu.CompilerParams(vmem_limit_bytes=SMALL_VMEM),
+        cost_estimate=COST,
+        name="other_rows",
+    )(place, in_hbm(other), in_hbm(acc), *map(in_hbm, pieces))
+
+
 def join_kernel(s_ref, x_ref, a_ref):
     me = s_ref[3]
     a_ref[:, :LOCAL] = x_ref[:, me].reshape(HALF, LOCAL)
-    a_ref[:, LOCAL:] = x_ref[:, 1 - me].reshape(HALF, LOCAL)
+    for i in range(4):
+        other = x_ref[:, 1 - me, :, head_of(s_ref, i)].reshape(HALF, HD)
+        a_ref[:, LOCAL + i * HD : LOCAL + (i + 1) * HD] = other
 
 
 def join(place, attended):
@@ -221,30 +263,32 @@
     )(place, attended)
 
 
-def project_kernel(s_ref, x_ref, y_ref, acc_ref, w_ref, *refs):
+def project_kernel(s_ref, x_ref, y_ref, near_ref, far_ref, w_ref, *refs):
     pieces, o_ref = refs[:8], refs[8]
-    a_buf, w_buf, acc_buf, o_buf, load_sems, store_sems = refs[9:]
-    core, mine = s_ref[0], 2 * s_ref[1] + s_ref[2]
+    a_buf, w_buf, acc_buf, o_buf, load_sems, store_sems, row_sems = refs[9:]
     half = CHUNKS // 2
+    depth = 2 * LOCAL
 
     def columns_of(n):
-        at = lax.rem(n + core * half, CHUNKS)
+        at = lax.rem(n + s_ref[0] * half, CHUNKS)
         return pl.ds(pl.multiple_of(at * CHUNK, CHUNK), CHUNK)
 
     def loads_of(n):
         columns = columns_of(n)
         there = pl.ds(n % half * CHUNK, CHUNK)
-        rows = pl.ds(LOCAL, LOCAL)
-        loads = [
-            pltpu.make_async_copy(acc_ref.at[:, columns], acc_buf.at[n], load_sems.at[n, 0]),
-            pltpu.make_async_copy(
-                w_ref.at[rows, columns], w_buf.at[n, pl.ds(0, LOCAL)], load_sems.at[n, 1]
-            ),
+        sems = load_sems.at[n]
+        acc = near_ref.at[:, there] if n < half else far_ref.at[:, columns]
+        copies = [
+            (acc, acc_buf.at[n]),
+            (w_ref.at[pl.ds(LOCAL, LOCAL), columns], w_buf.at[n, pl.ds(0, LOCAL)]),
         ]
         for i, piece in enumerate(pieces[:4] if n < half else pieces[4:]):
-            to = w_buf.at[n, pl.ds(LOCAL + i * PIECE, PIECE)]
-            loads.append(pltpu.make_async_copy(piece.at[:, there], to, load_sems.at[n, 2 + i]))
-        return loads
+            to = w_buf.at[n, pl.ds(LOCAL + i * HD, HD)]
+            copies.append((piece.at[pl.ds(HD, HD), there], to))
+            if n >= half:
+                to = w_buf.at[n, pl.ds(depth + i * HD, HD)]
+                copies.append((piece.at[pl.ds(0, HD), there], to))
+        return [pltpu.make_async_copy(*copy, sems.at[i]) for i, copy in enumerate(copies)]
 
     def store_of(n):
         return pltpu.make_async_copy(o_buf.at[n], o_ref.at[0, :, columns_of(n)], store_sems.at[n])
@@ -252,64 +296,64 @@
     for n in range(CHUNKS):
         for load in loads_of(n):
             load.start()
-    a_buf[:, :LOCAL] = y_ref[:, :LOCAL]
-    for i in range(4):
-        quarter = lax.bitwise_xor(mine, i)
-        to = slice(LOCAL + i * PIECE, LOCAL + (i + 1) * PIECE)
-
-        @pl.when(quarter < 2)
-        def _():
-            a_buf[:, to] = x_ref[:HALF, pl.ds(pl.multiple_of(quarter * PIECE, PIECE), PIECE)]
-
-        @pl.when(quarter >= 2)
-        def _():
-            a_buf[:, to] = y_ref[:, pl.ds(pl.multiple_of(quarter * PIECE, PIECE), PIECE)]
-
+    rows = [
+        pltpu.make_async_copy(
+            x_ref.at[pl.ds(0, HALF), head_of(s_ref, i)],
+            a_buf.at[:, pl.ds(i * HD, HD)],
+            row_sems.at[i],
+        )
+        for i in range(4)
+    ]
+    for load in rows:
+        load.start()
     for n in range(CHUNKS):
-        for load in loads_of(n):
+        for load in loads_of(n) + (rows if n == half else []):
             load.wait()
-        total = acc_buf[n].astype(jnp.float32) + dot_nn(a_buf[...], w_buf[n])
+        total = acc_buf[n].astype(jnp.float32) + dot_nn(y_ref[...], w_buf[n, :depth])
+        if n >= half:
+            total += dot_nn(a_buf[...], w_buf[n, depth:])
         o_buf[n] = total.astype(jnp.bfloat16)
         store_of(n).start()
     for n in range(CHUNKS):
         store_of(n).wait()
 
 
-def project(place, row_other, joined, acc, w_own, pieces):
-    depth = LOCAL + 4 * PIECE
+def project(place, row_other, joined, acc_near, acc, w_own, pieces):
     return pl.pallas_call(
         project_kernel,
         in_specs=[
             pl.BlockSpec(memory_space=pltpu.SMEM),
+            ANYWHERE,
             WHOLE,
-            WHOLE,
-            *[ANYWHERE] * 10,
+            *[ANYWHERE] * 11,
         ],
         out_specs=ANYWHERE,
         out_shape=pltpu.HBM((1, HALF, WIDTH), jnp.bfloat16),
         scratch_shapes=[
-            pltpu.VMEM((HALF, depth), jnp.bfloat16),
-            pltpu.VMEM((CHUNKS, depth, CHUNK), jnp.bfloat16),
+            pltpu.VMEM((HALF, LOCAL), jnp.bfloat16),
+            pltpu.VMEM((CHUNKS, 3 * LOCAL, CHUNK), jnp.bfloat16),
             pltpu.VMEM((CHUNKS, HALF, CHUNK), jnp.bfloat16),
             pltpu.VMEM((CHUNKS, HALF, CHUNK), jnp.bfloat16),
-            pltpu.SemaphoreType.DMA((CHUNKS, 6)),
+            pltpu.SemaphoreType.DMA((CHUNKS, 10)),
             pltpu.SemaphoreType.DMA((CHUNKS,)),
+            pltpu.SemaphoreType.DMA((4,)),
         ],
         compiler_params=pltpu.CompilerParams(vmem_limit_bytes=40 << 20),
         cost_estimate=COST,
         name="project",
-    )(place, row_other, joined, in_hbm(acc), in_hbm(w_own), *map(in_hbm, pieces))
+    )(place, in_hbm(row_other), joined, *map(in_hbm, (acc_near, acc, w_own, *pieces)))
 
 
 def slice_kernel(opposite, s_ref, w_ref, x_ref, buf, in_sems, out_sems):
     columns = pl.ds(pl.multiple_of(s_ref[0] * HALF_WIDTH, HALF_WIDTH), HALF_WIDTH)
-    quarter = 2 * s_ref[1] + s_ref[2]
+    head = 2 * s_ref[1] + s_ref[2]
     if opposite:
-        quarter = 3 - quarter
+        head = 3 - head
     loads, stores = [], []
     step = PIECE // SLICE_STEPS
+    each = SLICE_STEPS // 2
     for n in range(SLICE_STEPS):
-        start = pl.multiple_of(quarter * PIECE + n * step, step)
+        start = pl.multiple_of(n // each * LOCAL + head * HD + n % each * step, step)
         at = pl.ds(n * step, step)
         loads.append(
             pltpu.make_async_copy(w_ref.at[pl.ds(start, step), columns], buf.at[at], in_sems.at[n])
@@ -412,8 +456,10 @@
     far = [permute(piece, TO_CORE) for piece in near]
     col = col.reshape(2 * ROWS, 8, LOCAL)
     col = lax.all_to_all(col, ("ctx", "head"), split_axis=0, concat_axis=0, tiled=True)
+    acc_near = project_other_rows(place, row_other, acc, near)
+    col, acc_near = lax.optimization_barrier((col, acc_near))
     joined = join(place, col.reshape(ROWS, 2, 8, LOCAL))
-    return project(place, row_other, joined, acc, w_out, near + far)
+    return project(place, row_other, joined, acc_near, acc, w_out, near + far)
 
 
 def solution(mesh):

time: 108 us -> 109 us (level)
  Pallas kernels: 42.8 us -> 48.9 us
  waiting for transfers between devices: 35 us -> 30 us
    all_to_all x1, waiting for transfers between devices: 14.5 us -> 9.52 us  [on_device(): lax.all_to_all(col, ('ctx', 'head'), split_axis=0, concat_axis=0, tiled=T...]
    pallas_call x0 -> x1, Pallas kernels: none -> 4.97 us  [project_other_rows(): pl.pallas_call(other_rows_kernel, grid_spec=pltpu.PrefetchScalarGridSpec(...]
  transfers between devices with their start and end apart: 11 -> 11, of which waited for: 3 -> 3; matrix products, arithmetic and copies ran while one was open for 0% -> 0% of each run, Pallas kernels for 27% -> 31%
where the time goes in v4:
time: 109 us
  Pallas kernels  48.9 us (45%)
  waiting for transfers between devices  30 us (28%)
  starting transfers between devices  29.6 us (27%)
    all_to_all x1, waiting for transfers between devices, on_device(): lax.all_to_all(sent, 'ctx', split_axis=0, concat_axis=0, tiled=True)  13.5 us
    ppermute x9, starting transfers between devices, permute(): return lax.ppermute(x, ('ctx', 'head'), pairs)  13.1 us
    pallas_call x1, Pallas kernels, project(): pl.pallas_call(project_kernel, in_specs=[pl.BlockSpec(memory_space=pltpu....  12.3 us
    pallas_call x1, Pallas kernels, row_attention(): pl.pallas_call(row_kernel, grid=(GROUP,), in_specs=[spec] * 3, out_specs=...  10.7 us
    all_to_all x1, starting transfers between devices, on_device(): lax.all_to_all(sent, 'ctx', split_axis=0, concat_axis=0, tiled=True)  10.5 us
    all_to_all x1, waiting for transfers between devices, on_device(): lax.all_to_all(col, ('ctx', 'head'), split_axis=0, concat_axis=0, tiled=T...  9.52 us
    ppermute x9, waiting for transfers between devices, permute(): return lax.ppermute(x, ('ctx', 'head'), pairs)  6.97 us
    pallas_call x1, Pallas kernels, project_own_rows(): pl.pallas_call(own_rows_kernel, grid=(TILES,), in_specs=[pl.BlockSpec((HA...  6.38 us
  transfers between devices with their start and end apart: 11, of which 3 were waited for; matrix products, arithmetic and copies ran while one was open for 0% of the time, Pallas kernels for 31%

profile of v4, /device:TPU:1, one launch (start us, length us, event | category | flops | bytes accessed | tf_op | source)
XLA Modules:
  0.0 108.9 jit_solution(13530051050994260409)
XLA Ops:
  0.0 0.1 pad_add_fusion.s_ref
  0.1 0.0 copy-start
  0.1 2.6 %slice.2 = bf16[256,2048]{1,0:T(8,128)(2,1)} custom-call(s32[4]{0:T(128)S(1)} %pad_add_fusion.s_ref, bf16[1024,4096]{1,0:T(8,128)(2,1)} %w_ref.6), custom_call_target="tpu_custom_call" | custom-call | flops 1048576 | bytes 1024 | tf_op jit(solution)/shard_map/slice/pallas_call | solution.py:375
  2.6 0.0 copy-done
  2.6 3.4 %collective-permute-start = (bf16[256,2048]{1,0:T(8,128)(2,1)}, bf16[256,2048]{1,0:T(8,128)(2,1)}, u32[]{:S(2)}, u32[]{:S(2)}) collective-permute-start(bf16[256,2048]{1,0:T(8,128)(2,1)} %slice.2), channel_id=1, source_target_pairs={{0,1},{2,19},{32,33},{34,51},{64,65},{66,83},{96,97},{98,115},{4,5... | collective-permute-start | bytes 3145736 | tf_op jit(solution)/shard_map/ppermute | solution.py:57
  6.0 3.1 %pack.1 = bf16[64,6,8,512]{3,2,1,0:T(8,128)(2,1)} custom-call(bf16[1,2,64,8,1024]{4,3,2,1,0:T(8,128)(2,1)} %bitcast.13, bf16[1,2,64,8,1024]{4,3,2,1,0:T(8,128)(2,1)} %bitcast.14, bf16[1,2,64,8,1024]{4,3,2,1,0:T(8,128)(2,1)} %bitcast.15), custom_call_target="tpu_custom_call" | custom-call | flops 1048576 | bytes 1024 | tf_op jit(solution)/shard_map/pack/pallas_call | solution.py:423
  9.1 10.5 %all-to-all-start = ((bf16[64,48,512]{2,1,0:T(8,128)(2,1)}), bf16[64,48,512]{2,1,0:T(8,128)(2,1)}, u32[]{:S(2)}, u32[]{:S(2)}) async-start(bf16[64,48,512]{2,1,0:T(8,128)(2,1)} %bitcast.11), calls=%async_computation | async-start | bytes 6291456 | tf_op jit(solution)/shard_map/all_to_all | solution.py:446
  19.7 0.0 collective-permute-done.refs_0_
  19.7 0.0 copy-start.1
  19.7 10.7 %row_attention.1 = (bf16[512,512]{1,0:T(8,128)(2,1)}, bf16[1024,512]{1,0:T(8,128)(2,1)}) custom-call(bf16[1,1024,1024]{2,1,0:T(8,128)(2,1)} %q_ref, bf16[1,1024,1024]{2,1,0:T(8,128)(2,1)} %k_ref, bf16[1,1024,1024]{2,1,0:T(8,128)(2,1)} %v_ref), custom_call_target="tpu_custom_call" | custom-call | flops 274877906944 | bytes 1048576 | tf_op jit(solution)/shard_map/row_attention/pallas_call | solution.py:109
  30.4 0.0 copy-done.1
  30.4 2.6 %slice.3 = bf16[256,2048]{1,0:T(8,128)(2,1)} custom-call(s32[4]{0:T(128)S(1)} %copy-done.1, bf16[1024,4096]{1,0:T(8,128)(2,1)} %w_ref.6), custom_call_target="tpu_custom_call" | custom-call | flops 1048576 | bytes 1024 | tf_op jit(solution)/shard_map/slice/pallas_call | solution.py:375
  33.0 0.0 copy-start.3
  33.1 6.4 %own_rows.1.acc_ref.far_ref = bf16[512,4096]{1,0:T(8,128)(2,1)} custom-call(bf16[512,512]{1,0:T(8,128)(2,1)} %get-tuple-element.34.a_ref, bf16[1024,4096]{1,0:T(8,128)(2,1)} %w_ref.6), custom_call_target="tpu_custom_call" | custom-call | flops 1048576 | bytes 1024 | tf_op jit(solution)/shard_map/own_rows/pallas_call | solution.py:191
  39.4 0.0 copy-done.3
  39.4 1.9 %collective-permute-start.3 = (bf16[256,2048]{1,0:T(8,128)(2,1)S(1)}, bf16[256,2048]{1,0:T(8,128)(2,1)}, u32[]{:S(2)}, u32[]{:S(2)}) collective-permute-start(bf16[256,2048]{1,0:T(8,128)(2,1)S(1)} %copy-done.3), channel_id=1, source_target_pairs={{0,17},{2,19},{32,49},{34,51},{64,81},{66,83},{96,113},{98,115},{4... | collective-permute-start | bytes 3145736 | tf_op jit(solution)/shard_map/ppermute | solution.py:57
  41.4 0.6 collective-permute-start.4
  42.0 2.4 %collective-permute-start.2 = (bf16[256,2048]{1,0:T(8,128)(2,1)}, bf16[256,2048]{1,0:T(8,128)(2,1)}, u32[]{:S(2)}, u32[]{:S(2)}) collective-permute-start(bf16[256,2048]{1,0:T(8,128)(2,1)} %collective-permute-done.refs_0_), channel_id=1, source_target_pairs={{0,4},{2,14},{32,36},{34,46},{64,68},{66,78},{96,100},{98,110},{4,... | collective-permute-start | bytes 3145736 | tf_op jit(solution)/shard_map/ppermute | solution.py:57
  44.4 3.3 %collective-permute-start.1 = (bf16[256,2048]{1,0:T(8,128)(2,1)}, bf16[256,2048]{1,0:T(8,128)(2,1)}, u32[]{:S(2)}, u32[]{:S(2)}) collective-permute-start(bf16[256,2048]{1,0:T(8,128)(2,1)} %collective-permute-done.refs_0_), channel_id=1, source_target_pairs={{0,32},{2,98},{32,0},{34,66},{64,96},{66,34},{96,64},{98,2},{4,36}... | collective-permute-start | bytes 3145736 | tf_op jit(solution)/shard_map/ppermute | solution.py:57
  47.7 13.5 %all-to-all-done.x_ref = bf16[64,48,512]{2,1,0:T(8,128)(2,1)} async-done(((bf16[64,48,512]{2,1,0:T(8,128)(2,1)}), bf16[64,48,512]{2,1,0:T(8,128)(2,1)}, u32[]{:S(2)}, u32[]{:S(2)}) %all-to-all-start) | async-done | bytes 3145760 | tf_op jit(solution)/shard_map/all_to_all | solution.py:446
  61.2 5.6 %column_attention.1 = bf16[64,16,512]{2,1,0:T(8,128)(2,1)} custom-call(bf16[64,48,512]{2,1,0:T(8,128)(2,1)} %all-to-all-done.x_ref), custom_call_target="tpu_custom_call" | custom-call | flops 1048576 | bytes 1024 | tf_op jit(solution)/shard_map/column_attention/pallas_call | solution.py:166
  66.8 5.9 %all-to-all-start.1 = ((bf16[128,8,512]{2,1,0:T(8,128)(2,1)}), bf16[128,8,512]{2,1,0:T(8,128)(2,1)S(1)}, u32[]{:S(2)}, u32[]{:S(2)}) async-start(bf16[128,8,512]{2,1,0:T(8,128)(2,1)} %bitcast.12), calls=%async_computation.1 | async-start | bytes 2097152 | tf_op jit(solution)/shard_map/all_to_all | solution.py:458
  72.7 6.9 %collective-permute-done.3.refs_3_ = bf16[256,2048]{1,0:T(8,128)(2,1)} collective-permute-done((bf16[256,2048]{1,0:T(8,128)(2,1)S(1)}, bf16[256,2048]{1,0:T(8,128)(2,1)}, u32[]{:S(2)}, u32[]{:S(2)}) %collective-permute-start.3) | collective-permute-done | bytes 1048608 | tf_op jit(solution)/shard_map/ppermute | solution.py:57
  79.7 0.0 collective-permute-done.4.a_ref.x_ref
  79.7 0.0 copy-start.2
  79.7 0.0 collective-permute-done.2.refs_2_
  79.7 0.0 collective-permute-done.1.refs_1_
  79.7 0.8 collective-permute-start.5
  80.5 0.1 collective-permute-start.6
  80.6 0.4 collective-permute-start.7
  81.0 0.1 collective-permute-start.8
  81.1 0.0 copy-done.2
  81.1 5.0 %other_rows.1.near_ref = bf16[512,2048]{1,0:T(8,128)(2,1)} custom-call(s32[4]{0:T(128)S(1)} %copy-done.1, bf16[1024,512]{1,0:T(8,128)(2,1)} %copy-done.2, bf16[512,4096]{1,0:T(8,128)(2,1)} %own_rows.1.acc_ref.far_ref, bf16[256,2048]{1,0:T(8,128)(2,1)} %collective-permute-done.refs_0_, bf16[256,2048]{1,0:T(8,128)(2,1)} %collective-permute-done.1.refs_1_, ...), custom_call_target="tpu_custom_call" | custom-call | flops 1048576 | bytes 1024 | tf_op jit(solution)/shard_map/other_rows/pallas_call | solution.py:226
  86.1 9.5 %all-to-all-done.1 = bf16[128,8,512]{2,1,0:T(8,128)(2,1)S(1)} async-done(((bf16[128,8,512]{2,1,0:T(8,128)(2,1)}), bf16[128,8,512]{2,1,0:T(8,128)(2,1)S(1)}, u32[]{:S(2)}, u32[]{:S(2)}) %all-to-all-start.1) | async-done | bytes 1048608 | tf_op jit(solution)/shard_map/all_to_all | solution.py:458
  95.6 0.7 join.1.y_ref
  96.4 0.0 collective-permute-done.5.refs_4_
  96.4 0.0 collective-permute-done.6.refs_5_
  96.4 0.0 collective-permute-done.7.refs_6_
  96.4 0.0 collective-permute-done.8.refs_7_
  96.4 12.3 %project.1 = bf16[1,512,4096]{2,1,0:T(8,128)(2,1)} custom-call(s32[4]{0:T(128)S(1)} %copy-done.1, bf16[1024,512]{1,0:T(8,128)(2,1)} %copy-done.2, bf16[512,1024]{1,0:T(8,128)(2,1)S(1)} %join.1.y_ref, bf16[512,2048]{1,0:T(8,128)(2,1)} %other_rows.1.near_ref, bf16[512,4096]{1,0:T(8,128)(2,1)} %own_rows.1.acc_ref.far_ref, bf16[1024,4096]{1,0:T(8,128)(2,1)} %w_ref.6, ...), custom_call_target="tpu_custom_call" | custom-call | flops 1048576 | bytes 1024 | tf_op jit(solution)/shard_map/project/pallas_call | solution.py:322
Async XLA Ops:
  0.1 2.6 %copy-start = (s32[4]{0:T(128)}, s32[4]{0:T(128)S(1)}, u32[]{:S(2)}) copy-start(s32[4]{0:T(128)S(1)} %pad_add_fusion.s_ref) | copy-start | bytes 52
  2.6 17.0 %collective-permute-start = (bf16[256,2048]{1,0:T(8,128)(2,1)}, bf16[256,2048]{1,0:T(8,128)(2,1)}, u32[]{:S(2)}, u32[]{:S(2)}) collective-permute-start(bf16[256,2048]{1,0:T(8,128)(2,1)} %slice.2), channel_id=1, source_target_pairs={{0,1},{2,19},{32,33},{34,51},{64,65},{66,83},{96,97},{98,115},{4,5... | collective-permute-start | bytes 3145736 | tf_op jit(solution)/shard_map/ppermute | solution.py:57
  9.1 52.1 %all-to-all-start = ((bf16[64,48,512]{2,1,0:T(8,128)(2,1)}), bf16[64,48,512]{2,1,0:T(8,128)(2,1)}, u32[]{:S(2)}, u32[]{:S(2)}) async-start(bf16[64,48,512]{2,1,0:T(8,128)(2,1)} %bitcast.11), calls=%async_computation | async-start | bytes 6291456 | tf_op jit(solution)/shard_map/all_to_all | solution.py:446
  19.7 10.7 %copy-start.1 = (s32[4]{0:T(128)S(1)}, s32[4]{0:T(128)}, u32[]{:S(2)}) copy-start(s32[4]{0:T(128)} %copy-done) | copy-start | bytes 52
  33.0 6.4 %copy-start.3 = (bf16[256,2048]{1,0:T(8,128)(2,1)S(1)}, bf16[256,2048]{1,0:T(8,128)(2,1)}, u32[]{:S(2)}) copy-start(bf16[256,2048]{1,0:T(8,128)(2,1)} %slice.3) | copy-start | bytes 3145732
  39.4 40.2 %collective-permute-start.3 = (bf16[256,2048]{1,0:T(8,128)(2,1)S(1)}, bf16[256,2048]{1,0:T(8,128)(2,1)}, u32[]{:S(2)}, u32[]{:S(2)}) collective-permute-start(bf16[256,2048]{1,0:T(8,128)(2,1)S(1)} %copy-done.3), channel_id=1, source_target_pairs={{0,17},{2,19},{32,49},{34,51},{64,81},{66,83},{96,113},{98,115},{4... | collective-permute-start | bytes 3145736 | tf_op jit(solution)/shard_map/ppermute | solution.py:57
  41.4 38.3 %collective-permute-start.4 = (bf16[1024,512]{1,0:T(8,128)(2,1)}, bf16[1024,512]{1,0:T(8,128)(2,1)S(1)}, u32[]{:S(2)}, u32[]{:S(2)}) collective-permute-start(bf16[1024,512]{1,0:T(8,128)(2,1)} %get-tuple-element.37), channel_id=1, source_target_pairs={{0,1},{2,3},{32,33},{34,35},{64,65},{66,67},{96,97},{98,99},{4,5},... | collective-permute-start | bytes 3145736 | tf_op jit(solution)/shard_map/ppermute | solution.py:57
  42.0 37.7 %collective-permute-start.2 = (bf16[256,2048]{1,0:T(8,128)(2,1)}, bf16[256,2048]{1,0:T(8,128)(2,1)}, u32[]{:S(2)}, u32[]{:S(2)}) collective-permute-start(bf16[256,2048]{1,0:T(8,128)(2,1)} %collective-permute-done.refs_0_), channel_id=1, source_target_pairs={{0,4},{2,14},{32,36},{34,46},{64,68},{66,78},{96,100},{98,110},{4,... | collective-permute-start | bytes 3145736 | tf_op jit(solution)/shard_map/ppermute | solution.py:57
  44.4 35.3 %collective-permute-start.1 = (bf16[256,2048]{1,0:T(8,128)(2,1)}, bf16[256,2048]{1,0:T(8,128)(2,1)}, u32[]{:S(2)}, u32[]{:S(2)}) collective-permute-start(bf16[256,2048]{1,0:T(8,128)(2,1)} %collective-permute-done.refs_0_), channel_id=1, source_target_pairs={{0,32},{2,98},{32,0},{34,66},{64,96},{66,34},{96,64},{98,2},{4,36}... | collective-permute-start | bytes 3145736 | tf_op jit(solution)/shard_map/ppermute | solution.py:57
  66.8 28.8 %all-to-all-start.1 = ((bf16[128,8,512]{2,1,0:T(8,128)(2,1)}), bf16[128,8,512]{2,1,0:T(8,128)(2,1)S(1)}, u32[]{:S(2)}, u32[]{:S(2)}) async-start(bf16[128,8,512]{2,1,0:T(8,128)(2,1)} %bitcast.12), calls=%async_computation.1 | async-start | bytes 2097152 | tf_op jit(solution)/shard_map/all_to_all | solution.py:458
  79.7 1.5 %copy-start.2 = (bf16[1024,512]{1,0:T(8,128)(2,1)}, bf16[1024,512]{1,0:T(8,128)(2,1)S(1)}, u32[]{:S(2)}) copy-start(bf16[1024,512]{1,0:T(8,128)(2,1)S(1)} %collective-permute-done.4.a_ref.x_ref) | copy-start | bytes 3145732
  79.7 16.7 %collective-permute-start.5 = (bf16[256,2048]{1,0:T(8,128)(2,1)}, bf16[256,2048]{1,0:T(8,128)(2,1)}, u32[]{:S(2)}, u32[]{:S(2)}) collective-permute-start(bf16[256,2048]{1,0:T(8,128)(2,1)} %collective-permute-done.refs_0_), channel_id=1, source_target_pairs={{0,2},{2,0},{32,34},{34,32},{64,66},{66,64},{96,98},{98,96},{4,6},... | collective-permute-start | bytes 3145736 | tf_op jit(solution)/shard_map/ppermute | solution.py:57
  80.5 15.8 %collective-permute-start.6 = (bf16[256,2048]{1,0:T(8,128)(2,1)}, bf16[256,2048]{1,0:T(8,128)(2,1)}, u32[]{:S(2)}, u32[]{:S(2)}) collective-permute-start(bf16[256,2048]{1,0:T(8,128)(2,1)} %collective-permute-done.1.refs_1_), channel_id=1, source_target_pairs={{0,2},{2,0},{32,34},{34,32},{64,66},{66,64},{96,98},{98,96},{4,6},... | collective-permute-start | bytes 3145736 | tf_op jit(solution)/shard_map/ppermute | solution.py:57
  80.6 15.8 %collective-permute-start.7 = (bf16[256,2048]{1,0:T(8,128)(2,1)}, bf16[256,2048]{1,0:T(8,128)(2,1)}, u32[]{:S(2)}, u32[]{:S(2)}) collective-permute-start(bf16[256,2048]{1,0:T(8,128)(2,1)} %collective-permute-done.2.refs_2_), channel_id=1, source_target_pairs={{0,2},{2,0},{32,34},{34,32},{64,66},{66,64},{96,98},{98,96},{4,6},... | collective-permute-start | bytes 3145736 | tf_op jit(solution)/shard_map/ppermute | solution.py:57
  81.0 15.3 %collective-permute-start.8 = (bf16[256,2048]{1,0:T(8,128)(2,1)}, bf16[256,2048]{1,0:T(8,128)(2,1)}, u32[]{:S(2)}, u32[]{:S(2)}) collective-permute-start(bf16[256,2048]{1,0:T(8,128)(2,1)} %collective-permute-done.3.refs_3_), channel_id=1, source_target_pairs={{0,2},{2,0},{32,34},{34,32},{64,66},{66,64},{96,98},{98,96},{4,6},... | collective-permute-start | bytes 3145736 | tf_op jit(solution)/shard_map/ppermute | solution.py:57

commit v5 on v4

--- a/solution.py
+++ b/solution.py
@@ -265,7 +265,7 @@
 
 def project_kernel(s_ref, x_ref, y_ref, near_ref, far_ref, w_ref, *refs):
     pieces, o_ref = refs[:8], refs[8]
-    a_buf, w_buf, acc_buf, o_buf, load_sems, store_sems, row_sems = refs[9:]
+    a_buf, w_buf, acc_buf, o_buf, load_sems, store_sems, x_buf, row_sem = refs[9:]
     half = CHUNKS // 2
     depth = 2 * LOCAL
 
@@ -296,19 +296,15 @@
     for n in range(CHUNKS):
         for load in loads_of(n):
             load.start()
-    rows = [
-        pltpu.make_async_copy(
-            x_ref.at[pl.ds(0, HALF), head_of(s_ref, i)],
-            a_buf.at[:, pl.ds(i * HD, HD)],
-            row_sems.at[i],
-        )
-        for i in range(4)
-    ]
-    for load in rows:
-        load.start()
+    rows = pltpu.make_async_copy(x_ref.at[pl.ds(0, HALF)], x_buf, row_sem)
+    rows.start()
     for n in range(CHUNKS):
-        for load in loads_of(n) + (rows if n == half else []):
+        for load in loads_of(n):
             load.wait()
+        if n == half:
+            rows.wait()
+            for i in range(4):
+                a_buf[:, i * HD : (i + 1) * HD] = x_buf[:, head_of(s_ref, i)]
         total = acc_buf[n].astype(jnp.float32) + dot_nn(y_ref[...], w_buf[n, :depth])
         if n >= half:
             total += dot_nn(a_buf[...], w_buf[n, depth:])
@@ -336,7 +332,8 @@
             pltpu.VMEM((CHUNKS, HALF, CHUNK), jnp.bfloat16),
             pltpu.SemaphoreType.DMA((CHUNKS, 10)),
             pltpu.SemaphoreType.DMA((CHUNKS,)),
-            pltpu.SemaphoreType.DMA((4,)),
+            pltpu.VMEM((HALF, LOCAL), jnp.bfloat16),
+            pltpu.SemaphoreType.DMA(()),
         ],
         compiler_params=pltpu.CompilerParams(vmem_limit_bytes=40 << 20),
         cost_estimate=COST,

time: 109 us -> 109 us (level)
  no operation moved by 1% of the time
where the time goes in v5:
time: 109 us
  Pallas kernels  48.9 us (45%)
  waiting for transfers between devices  30 us (28%)
  starting transfers between devices  29.6 us (27%)
    all_to_all x1, waiting for transfers between devices, on_device(): lax.all_to_all(sent, 'ctx', split_axis=0, concat_axis=0, tiled=True)  13.5 us
    ppermute x9, starting transfers between devices, permute(): return lax.ppermute(x, ('ctx', 'head'), pairs)  13.1 us
    pallas_call x1, Pallas kernels, project(): pl.pallas_call(project_kernel, in_specs=[pl.BlockSpec(memory_space=pltpu....  12.3 us
    pallas_call x1, Pallas kernels, row_attention(): pl.pallas_call(row_kernel, grid=(GROUP,), in_specs=[spec] * 3, out_specs=...  10.7 us
    all_to_all x1, starting transfers between devices, on_device(): lax.all_to_all(sent, 'ctx', split_axis=0, concat_axis=0, tiled=True)  10.5 us
    all_to_all x1, waiting for transfers between devices, on_device(): lax.all_to_all(col, ('ctx', 'head'), split_axis=0, concat_axis=0, tiled=T...  9.52 us
    ppermute x9, waiting for transfers between devices, permute(): return lax.ppermute(x, ('ctx', 'head'), pairs)  6.97 us
    pallas_call x1, Pallas kernels, project_own_rows(): pl.pallas_call(own_rows_kernel, grid=(TILES,), in_specs=[pl.BlockSpec((HA...  6.38 us
  transfers between devices with their start and end apart: 11, of which 3 were waited for; matrix products, arithmetic and copies ran while one was open for 0% of the time, Pallas kernels for 31%

profile of v5, /device:TPU:1, one launch (start us, length us, event | category | flops | bytes accessed | tf_op | source)
XLA Modules:
  0.0 108.9 jit_solution(15334217347269888583)
XLA Ops:
  0.0 0.1 pad_add_fusion.s_ref
  0.1 0.0 copy-start
  0.1 2.6 %slice.2 = bf16[256,2048]{1,0:T(8,128)(2,1)} custom-call(s32[4]{0:T(128)S(1)} %pad_add_fusion.s_ref, bf16[1024,4096]{1,0:T(8,128)(2,1)} %w_ref.6), custom_call_target="tpu_custom_call" | custom-call | flops 1048576 | bytes 1024 | tf_op jit(solution)/shard_map/slice/pallas_call | solution.py:372
  2.6 0.0 copy-done
  2.6 3.4 %collective-permute-start = (bf16[256,2048]{1,0:T(8,128)(2,1)}, bf16[256,2048]{1,0:T(8,128)(2,1)}, u32[]{:S(2)}, u32[]{:S(2)}) collective-permute-start(bf16[256,2048]{1,0:T(8,128)(2,1)} %slice.2), channel_id=1, source_target_pairs={{0,1},{2,19},{32,33},{34,51},{64,65},{66,83},{96,97},{98,115},{4,5... | collective-permute-start | bytes 3145736 | tf_op jit(solution)/shard_map/ppermute | solution.py:57
  6.0 3.1 %pack.1 = bf16[64,6,8,512]{3,2,1,0:T(8,128)(2,1)} custom-call(bf16[1,2,64,8,1024]{4,3,2,1,0:T(8,128)(2,1)} %bitcast.13, bf16[1,2,64,8,1024]{4,3,2,1,0:T(8,128)(2,1)} %bitcast.14, bf16[1,2,64,8,1024]{4,3,2,1,0:T(8,128)(2,1)} %bitcast.15), custom_call_target="tpu_custom_call" | custom-call | flops 1048576 | bytes 1024 | tf_op jit(solution)/shard_map/pack/pallas_call | solution.py:420
  9.1 10.5 %all-to-all-start = ((bf16[64,48,512]{2,1,0:T(8,128)(2,1)}), bf16[64,48,512]{2,1,0:T(8,128)(2,1)}, u32[]{:S(2)}, u32[]{:S(2)}) async-start(bf16[64,48,512]{2,1,0:T(8,128)(2,1)} %bitcast.11), calls=%async_computation | async-start | bytes 6291456 | tf_op jit(solution)/shard_map/all_to_all | solution.py:443
  19.7 0.0 collective-permute-done.refs_0_
  19.7 0.0 copy-start.1
  19.7 10.7 %row_attention.1 = (bf16[512,512]{1,0:T(8,128)(2,1)}, bf16[1024,512]{1,0:T(8,128)(2,1)}) custom-call(bf16[1,1024,1024]{2,1,0:T(8,128)(2,1)} %q_ref, bf16[1,1024,1024]{2,1,0:T(8,128)(2,1)} %k_ref, bf16[1,1024,1024]{2,1,0:T(8,128)(2,1)} %v_ref), custom_call_target="tpu_custom_call" | custom-call | flops 274877906944 | bytes 1048576 | tf_op jit(solution)/shard_map/row_attention/pallas_call | solution.py:109
  30.4 0.0 copy-done.1
  30.4 2.6 %slice.3 = bf16[256,2048]{1,0:T(8,128)(2,1)} custom-call(s32[4]{0:T(128)S(1)} %copy-done.1, bf16[1024,4096]{1,0:T(8,128)(2,1)} %w_ref.6), custom_call_target="tpu_custom_call" | custom-call | flops 1048576 | bytes 1024 | tf_op jit(solution)/shard_map/slice/pallas_call | solution.py:372
  33.0 0.0 copy-start.3
  33.1 6.4 %own_rows.1.acc_ref.far_ref = bf16[512,4096]{1,0:T(8,128)(2,1)} custom-call(bf16[512,512]{1,0:T(8,128)(2,1)} %get-tuple-element.34.a_ref, bf16[1024,4096]{1,0:T(8,128)(2,1)} %w_ref.6), custom_call_target="tpu_custom_call" | custom-call | flops 1048576 | bytes 1024 | tf_op jit(solution)/shard_map/own_rows/pallas_call | solution.py:191
  39.4 0.0 copy-done.3
  39.4 1.9 %collective-permute-start.3 = (bf16[256,2048]{1,0:T(8,128)(2,1)S(1)}, bf16[256,2048]{1,0:T(8,128)(2,1)}, u32[]{:S(2)}, u32[]{:S(2)}) collective-permute-start(bf16[256,2048]{1,0:T(8,128)(2,1)S(1)} %copy-done.3), channel_id=1, source_target_pairs={{0,17},{2,19},{32,49},{34,51},{64,81},{66,83},{96,113},{98,115},{4... | collective-permute-start | bytes 3145736 | tf_op jit(solution)/shard_map/ppermute | solution.py:57
  41.4 0.6 collective-permute-start.4
  42.0 2.4 %collective-permute-start.2 = (bf16[256,2048]{1,0:T(8,128)(2,1)}, bf16[256,2048]{1,0:T(8,128)(2,1)}, u32[]{:S(2)}, u32[]{:S(2)}) collective-permute-start(bf16[256,2048]{1,0:T(8,128)(2,1)} %collective-permute-done.refs_0_), channel_id=1, source_target_pairs={{0,4},{2,14},{32,36},{34,46},{64,68},{66,78},{96,100},{98,110},{4,... | collective-permute-start | bytes 3145736 | tf_op jit(solution)/shard_map/ppermute | solution.py:57
  44.4 3.3 %collective-permute-start.1 = (bf16[256,2048]{1,0:T(8,128)(2,1)}, bf16[256,2048]{1,0:T(8,128)(2,1)}, u32[]{:S(2)}, u32[]{:S(2)}) collective-permute-start(bf16[256,2048]{1,0:T(8,128)(2,1)} %collective-permute-done.refs_0_), channel_id=1, source_target_pairs={{0,32},{2,98},{32,0},{34,66},{64,96},{66,34},{96,64},{98,2},{4,36}... | collective-permute-start | bytes 3145736 | tf_op jit(solution)/shard_map/ppermute | solution.py:57
  47.7 13.5 %all-to-all-done.x_ref = bf16[64,48,512]{2,1,0:T(8,128)(2,1)} async-done(((bf16[64,48,512]{2,1,0:T(8,128)(2,1)}), bf16[64,48,512]{2,1,0:T(8,128)(2,1)}, u32[]{:S(2)}, u32[]{:S(2)}) %all-to-all-start) | async-done | bytes 3145760 | tf_op jit(solution)/shard_map/all_to_all | solution.py:443
  61.2 5.6 %column_attention.1 = bf16[64,16,512]{2,1,0:T(8,128)(2,1)} custom-call(bf16[64,48,512]{2,1,0:T(8,128)(2,1)} %all-to-all-done.x_ref), custom_call_target="tpu_custom_call" | custom-call | flops 1048576 | bytes 1024 | tf_op jit(solution)/shard_map/column_attention/pallas_call | solution.py:166
  66.8 5.9 %all-to-all-start.1 = ((bf16[128,8,512]{2,1,0:T(8,128)(2,1)}), bf16[128,8,512]{2,1,0:T(8,128)(2,1)S(1)}, u32[]{:S(2)}, u32[]{:S(2)}) async-start(bf16[128,8,512]{2,1,0:T(8,128)(2,1)} %bitcast.12), calls=%async_computation.1 | async-start | bytes 2097152 | tf_op jit(solution)/shard_map/all_to_all | solution.py:455
  72.7 6.9 %collective-permute-done.3.refs_3_ = bf16[256,2048]{1,0:T(8,128)(2,1)} collective-permute-done((bf16[256,2048]{1,0:T(8,128)(2,1)S(1)}, bf16[256,2048]{1,0:T(8,128)(2,1)}, u32[]{:S(2)}, u32[]{:S(2)}) %collective-permute-start.3) | collective-permute-done | bytes 1048608 | tf_op jit(solution)/shard_map/ppermute | solution.py:57
  79.7 0.0 collective-permute-done.4.a_ref.x_ref
  79.7 0.0 copy-start.2
  79.7 0.0 collective-permute-done.2.refs_2_
  79.7 0.0 collective-permute-done.1.refs_1_
  79.7 0.8 collective-permute-start.5
  80.5 0.1 collective-permute-start.6
  80.6 0.4 collective-permute-start.7
  81.0 0.1 collective-permute-start.8
  81.1 0.0 copy-done.2
  81.1 5.0 %other_rows.1.near_ref = bf16[512,2048]{1,0:T(8,128)(2,1)} custom-call(s32[4]{0:T(128)S(1)} %copy-done.1, bf16[1024,512]{1,0:T(8,128)(2,1)} %copy-done.2, bf16[512,4096]{1,0:T(8,128)(2,1)} %own_rows.1.acc_ref.far_ref, bf16[256,2048]{1,0:T(8,128)(2,1)} %collective-permute-done.refs_0_, bf16[256,2048]{1,0:T(8,128)(2,1)} %collective-permute-done.1.refs_1_, ...), custom_call_target="tpu_custom_call" | custom-call | flops 1048576 | bytes 1024 | tf_op jit(solution)/shard_map/other_rows/pallas_call | solution.py:226
  86.1 9.5 %all-to-all-done.1 = bf16[128,8,512]{2,1,0:T(8,128)(2,1)S(1)} async-done(((bf16[128,8,512]{2,1,0:T(8,128)(2,1)}), bf16[128,8,512]{2,1,0:T(8,128)(2,1)S(1)}, u32[]{:S(2)}, u32[]{:S(2)}) %all-to-all-start.1) | async-done | bytes 1048608 | tf_op jit(solution)/shard_map/all_to_all | solution.py:455
  95.6 0.7 join.1.y_ref
  96.4 0.0 collective-permute-done.5.refs_4_
  96.4 0.0 collective-permute-done.6.refs_5_
  96.4 0.0 collective-permute-done.7.refs_6_
  96.4 0.0 collective-permute-done.8.refs_7_
  96.4 12.3 %project.1 = bf16[1,512,4096]{2,1,0:T(8,128)(2,1)} custom-call(s32[4]{0:T(128)S(1)} %copy-done.1, bf16[1024,512]{1,0:T(8,128)(2,1)} %copy-done.2, bf16[512,1024]{1,0:T(8,128)(2,1)S(1)} %join.1.y_ref, bf16[512,2048]{1,0:T(8,128)(2,1)} %other_rows.1.near_ref, bf16[512,4096]{1,0:T(8,128)(2,1)} %own_rows.1.acc_ref.far_ref, bf16[1024,4096]{1,0:T(8,128)(2,1)} %w_ref.6, ...), custom_call_target="tpu_custom_call" | custom-call | flops 1048576 | bytes 1024 | tf_op jit(solution)/shard_map/project/pallas_call | solution.py:318
Async XLA Ops:
  0.1 2.6 %copy-start = (s32[4]{0:T(128)}, s32[4]{0:T(128)S(1)}, u32[]{:S(2)}) copy-start(s32[4]{0:T(128)S(1)} %pad_add_fusion.s_ref) | copy-start | bytes 52
  2.6 17.0 %collective-permute-start = (bf16[256,2048]{1,0:T(8,128)(2,1)}, bf16[256,2048]{1,0:T(8,128)(2,1)}, u32[]{:S(2)}, u32[]{:S(2)}) collective-permute-start(bf16[256,2048]{1,0:T(8,128)(2,1)} %slice.2), channel_id=1, source_target_pairs={{0,1},{2,19},{32,33},{34,51},{64,65},{66,83},{96,97},{98,115},{4,5... | collective-permute-start | bytes 3145736 | tf_op jit(solution)/shard_map/ppermute | solution.py:57
  9.1 52.1 %all-to-all-start = ((bf16[64,48,512]{2,1,0:T(8,128)(2,1)}), bf16[64,48,512]{2,1,0:T(8,128)(2,1)}, u32[]{:S(2)}, u32[]{:S(2)}) async-start(bf16[64,48,512]{2,1,0:T(8,128)(2,1)} %bitcast.11), calls=%async_computation | async-start | bytes 6291456 | tf_op jit(solution)/shard_map/all_to_all | solution.py:443
  19.7 10.7 %copy-start.1 = (s32[4]{0:T(128)S(1)}, s32[4]{0:T(128)}, u32[]{:S(2)}) copy-start(s32[4]{0:T(128)} %copy-done) | copy-start | bytes 52
  33.0 6.4 %copy-start.3 = (bf16[256,2048]{1,0:T(8,128)(2,1)S(1)}, bf16[256,2048]{1,0:T(8,128)(2,1)}, u32[]{:S(2)}) copy-start(bf16[256,2048]{1,0:T(8,128)(2,1)} %slice.3) | copy-start | bytes 3145732
  39.4 40.2 %collective-permute-start.3 = (bf16[256,2048]{1,0:T(8,128)(2,1)S(1)}, bf16[256,2048]{1,0:T(8,128)(2,1)}, u32[]{:S(2)}, u32[]{:S(2)}) collective-permute-start(bf16[256,2048]{1,0:T(8,128)(2,1)S(1)} %copy-done.3), channel_id=1, source_target_pairs={{0,17},{2,19},{32,49},{34,51},{64,81},{66,83},{96,113},{98,115},{4... | collective-permute-start | bytes 3145736 | tf_op jit(solution)/shard_map/ppermute | solution.py:57
  41.4 38.3 %collective-permute-start.4 = (bf16[1024,512]{1,0:T(8,128)(2,1)}, bf16[1024,512]{1,0:T(8,128)(2,1)S(1)}, u32[]{:S(2)}, u32[]{:S(2)}) collective-permute-start(bf16[1024,512]{1,0:T(8,128)(2,1)} %get-tuple-element.37), channel_id=1, source_target_pairs={{0,1},{2,3},{32,33},{34,35},{64,65},{66,67},{96,97},{98,99},{4,5},... | collective-permute-start | bytes 3145736 | tf_op jit(solution)/shard_map/ppermute | solution.py:57
  42.0 37.7 %collective-permute-start.2 = (bf16[256,2048]{1,0:T(8,128)(2,1)}, bf16[256,2048]{1,0:T(8,128)(2,1)}, u32[]{:S(2)}, u32[]{:S(2)}) collective-permute-start(bf16[256,2048]{1,0:T(8,128)(2,1)} %collective-permute-done.refs_0_), channel_id=1, source_target_pairs={{0,4},{2,14},{32,36},{34,46},{64,68},{66,78},{96,100},{98,110},{4,... | collective-permute-start | bytes 3145736 | tf_op jit(solution)/shard_map/ppermute | solution.py:57
  44.4 35.3 %collective-permute-start.1 = (bf16[256,2048]{1,0:T(8,128)(2,1)}, bf16[256,2048]{1,0:T(8,128)(2,1)}, u32[]{:S(2)}, u32[]{:S(2)}) collective-permute-start(bf16[256,2048]{1,0:T(8,128)(2,1)} %collective-permute-done.refs_0_), channel_id=1, source_target_pairs={{0,32},{2,98},{32,0},{34,66},{64,96},{66,34},{96,64},{98,2},{4,36}... | collective-permute-start | bytes 3145736 | tf_op jit(solution)/shard_map/ppermute | solution.py:57
  66.8 28.8 %all-to-all-start.1 = ((bf16[128,8,512]{2,1,0:T(8,128)(2,1)}), bf16[128,8,512]{2,1,0:T(8,128)(2,1)S(1)}, u32[]{:S(2)}, u32[]{:S(2)}) async-start(bf16[128,8,512]{2,1,0:T(8,128)(2,1)} %bitcast.12), calls=%async_computation.1 | async-start | bytes 2097152 | tf_op jit(solution)/shard_map/all_to_all | solution.py:455
  79.7 1.5 %copy-start.2 = (bf16[1024,512]{1,0:T(8,128)(2,1)}, bf16[1024,512]{1,0:T(8,128)(2,1)S(1)}, u32[]{:S(2)}) copy-start(bf16[1024,512]{1,0:T(8,128)(2,1)S(1)} %collective-permute-done.4.a_ref.x_ref) | copy-start | bytes 3145732
  79.7 16.7 %collective-permute-start.5 = (bf16[256,2048]{1,0:T(8,128)(2,1)}, bf16[256,2048]{1,0:T(8,128)(2,1)}, u32[]{:S(2)}, u32[]{:S(2)}) collective-permute-start(bf16[256,2048]{1,0:T(8,128)(2,1)} %collective-permute-done.refs_0_), channel_id=1, source_target_pairs={{0,2},{2,0},{32,34},{34,32},{64,66},{66,64},{96,98},{98,96},{4,6},... | collective-permute-start | bytes 3145736 | tf_op jit(solution)/shard_map/ppermute | solution.py:57
  80.5 15.8 %collective-permute-start.6 = (bf16[256,2048]{1,0:T(8,128)(2,1)}, bf16[256,2048]{1,0:T(8,128)(2,1)}, u32[]{:S(2)}, u32[]{:S(2)}) collective-permute-start(bf16[256,2048]{1,0:T(8,128)(2,1)} %collective-permute-done.1.refs_1_), channel_id=1, source_target_pairs={{0,2},{2,0},{32,34},{34,32},{64,66},{66,64},{96,98},{98,96},{4,6},... | collective-permute-start | bytes 3145736 | tf_op jit(solution)/shard_map/ppermute | solution.py:57
  80.6 15.8 %collective-permute-start.7 = (bf16[256,2048]{1,0:T(8,128)(2,1)}, bf16[256,2048]{1,0:T(8,128)(2,1)}, u32[]{:S(2)}, u32[]{:S(2)}) collective-permute-start(bf16[256,2048]{1,0:T(8,128)(2,1)} %collective-permute-done.2.refs_2_), channel_id=1, source_target_pairs={{0,2},{2,0},{32,34},{34,32},{64,66},{66,64},{96,98},{98,96},{4,6},... | collective-permute-start | bytes 3145736 | tf_op jit(solution)/shard_map/ppermute | solution.py:57
  81.0 15.3 %collective-permute-start.8 = (bf16[256,2048]{1,0:T(8,128)(2,1)}, bf16[256,2048]{1,0:T(8,128)(2,1)}, u32[]{:S(2)}, u32[]{:S(2)}) collective-permute-start(bf16[256,2048]{1,0:T(8,128)(2,1)} %collective-permute-done.3.refs_3_), channel_id=1, source_target_pairs={{0,2},{2,0},{32,34},{34,32},{64,66},{66,64},{96,98},{98,96},{4,6},... | collective-permute-start | bytes 3145736 | tf_op jit(solution)/shard_map/ppermute | solution.py:57

commit v6 on v5

--- a/solution.py
+++ b/solution.py
@@ -293,11 +293,11 @@
     def store_of(n):
         return pltpu.make_async_copy(o_buf.at[n], o_ref.at[0, :, columns_of(n)], store_sems.at[n])
 
+    rows = pltpu.make_async_copy(x_ref.at[pl.ds(0, HALF)], x_buf, row_sem)
+    rows.start()
     for n in range(CHUNKS):
         for load in loads_of(n):
             load.start()
-    rows = pltpu.make_async_copy(x_ref.at[pl.ds(0, HALF)], x_buf, row_sem)
-    rows.start()
     for n in range(CHUNKS):
         for load in loads_of(n):
             load.wait()

time: 109 us -> 109 us (level)
  no operation moved by 1% of the time
where the time goes in v6:
time: 109 us
  Pallas kernels  48.9 us (45%)
  waiting for transfers between devices  30 us (28%)
  starting transfers between devices  29.6 us (27%)
    all_to_all x1, waiting for transfers between devices, on_device(): lax.all_to_all(sent, 'ctx', split_axis=0, concat_axis=0, tiled=True)  13.5 us
    ppermute x9, starting transfers between devices, permute(): return lax.ppermute(x, ('ctx', 'head'), pairs)  13.1 us
    pallas_call x1, Pallas kernels, project(): pl.pallas_call(project_kernel, in_specs=[pl.BlockSpec(memory_space=pltpu....  12.3 us
    pallas_call x1, Pallas kernels, row_attention(): pl.pallas_call(row_kernel, grid=(GROUP,), in_specs=[spec] * 3, out_specs=...  10.7 us
    all_to_all x1, starting transfers between devices, on_device(): lax.all_to_all(sent, 'ctx', split_axis=0, concat_axis=0, tiled=True)  10.5 us
    all_to_all x1, waiting for transfers between devices, on_device(): lax.all_to_all(col, ('ctx', 'head'), split_axis=0, concat_axis=0, tiled=T...  9.52 us
    ppermute x9, waiting for transfers between devices, permute(): return lax.ppermute(x, ('ctx', 'head'), pairs)  6.97 us
    pallas_call x1, Pallas kernels, project_own_rows(): pl.pallas_call(own_rows_kernel, grid=(TILES,), in_specs=[pl.BlockSpec((HA...  6.38 us
  transfers between devices with their start and end apart: 11, of which 3 were waited for; matrix products, arithmetic and copies ran while one was open for 0% of the time, Pallas kernels for 31%

profile of v6, /device:TPU:1, one launch (start us, length us, event | category | flops | bytes accessed | tf_op | source)
XLA Modules:
  0.0 108.9 jit_solution(15233795178826292114)
XLA Ops:
  0.0 0.1 pad_add_fusion.s_ref
  0.1 0.0 copy-start
  0.1 2.6 %slice.2 = bf16[256,2048]{1,0:T(8,128)(2,1)} custom-call(s32[4]{0:T(128)S(1)} %pad_add_fusion.s_ref, bf16[1024,4096]{1,0:T(8,128)(2,1)} %w_ref.6), custom_call_target="tpu_custom_call" | custom-call | flops 1048576 | bytes 1024 | tf_op jit(solution)/shard_map/slice/pallas_call | solution.py:372
  2.6 0.0 copy-done
  2.6 3.4 %collective-permute-start = (bf16[256,2048]{1,0:T(8,128)(2,1)}, bf16[256,2048]{1,0:T(8,128)(2,1)}, u32[]{:S(2)}, u32[]{:S(2)}) collective-permute-start(bf16[256,2048]{1,0:T(8,128)(2,1)} %slice.2), channel_id=1, source_target_pairs={{0,1},{2,19},{32,33},{34,51},{64,65},{66,83},{96,97},{98,115},{4,5... | collective-permute-start | bytes 3145736 | tf_op jit(solution)/shard_map/ppermute | solution.py:57
  6.0 3.1 %pack.1 = bf16[64,6,8,512]{3,2,1,0:T(8,128)(2,1)} custom-call(bf16[1,2,64,8,1024]{4,3,2,1,0:T(8,128)(2,1)} %bitcast.13, bf16[1,2,64,8,1024]{4,3,2,1,0:T(8,128)(2,1)} %bitcast.14, bf16[1,2,64,8,1024]{4,3,2,1,0:T(8,128)(2,1)} %bitcast.15), custom_call_target="tpu_custom_call" | custom-call | flops 1048576 | bytes 1024 | tf_op jit(solution)/shard_map/pack/pallas_call | solution.py:420
  9.1 10.5 %all-to-all-start = ((bf16[64,48,512]{2,1,0:T(8,128)(2,1)}), bf16[64,48,512]{2,1,0:T(8,128)(2,1)}, u32[]{:S(2)}, u32[]{:S(2)}) async-start(bf16[64,48,512]{2,1,0:T(8,128)(2,1)} %bitcast.11), calls=%async_computation | async-start | bytes 6291456 | tf_op jit(solution)/shard_map/all_to_all | solution.py:443
  19.7 0.0 collective-permute-done.refs_0_
  19.7 0.0 copy-start.1
  19.7 10.7 %row_attention.1 = (bf16[512,512]{1,0:T(8,128)(2,1)}, bf16[1024,512]{1,0:T(8,128)(2,1)}) custom-call(bf16[1,1024,1024]{2,1,0:T(8,128)(2,1)} %q_ref, bf16[1,1024,1024]{2,1,0:T(8,128)(2,1)} %k_ref, bf16[1,1024,1024]{2,1,0:T(8,128)(2,1)} %v_ref), custom_call_target="tpu_custom_call" | custom-call | flops 274877906944 | bytes 1048576 | tf_op jit(solution)/shard_map/row_attention/pallas_call | solution.py:109
  30.4 0.0 copy-done.1
  30.4 2.6 %slice.3 = bf16[256,2048]{1,0:T(8,128)(2,1)} custom-call(s32[4]{0:T(128)S(1)} %copy-done.1, bf16[1024,4096]{1,0:T(8,128)(2,1)} %w_ref.6), custom_call_target="tpu_custom_call" | custom-call | flops 1048576 | bytes 1024 | tf_op jit(solution)/shard_map/slice/pallas_call | solution.py:372
  33.0 0.0 copy-start.3
  33.1 6.4 %own_rows.1.acc_ref.far_ref = bf16[512,4096]{1,0:T(8,128)(2,1)} custom-call(bf16[512,512]{1,0:T(8,128)(2,1)} %get-tuple-element.34.a_ref, bf16[1024,4096]{1,0:T(8,128)(2,1)} %w_ref.6), custom_call_target="tpu_custom_call" | custom-call | flops 1048576 | bytes 1024 | tf_op jit(solution)/shard_map/own_rows/pallas_call | solution.py:191
  39.4 0.0 copy-done.3
  39.4 1.9 %collective-permute-start.3 = (bf16[256,2048]{1,0:T(8,128)(2,1)S(1)}, bf16[256,2048]{1,0:T(8,128)(2,1)}, u32[]{:S(2)}, u32[]{:S(2)}) collective-permute-start(bf16[256,2048]{1,0:T(8,128)(2,1)S(1)} %copy-done.3), channel_id=1, source_target_pairs={{0,17},{2,19},{32,49},{34,51},{64,81},{66,83},{96,113},{98,115},{4... | collective-permute-start | bytes 3145736 | tf_op jit(solution)/shard_map/ppermute | solution.py:57
  41.4 0.6 collective-permute-start.4
  42.0 2.4 %collective-permute-start.2 = (bf16[256,2048]{1,0:T(8,128)(2,1)}, bf16[256,2048]{1,0:T(8,128)(2,1)}, u32[]{:S(2)}, u32[]{:S(2)}) collective-permute-start(bf16[256,2048]{1,0:T(8,128)(2,1)} %collective-permute-done.refs_0_), channel_id=1, source_target_pairs={{0,4},{2,14},{32,36},{34,46},{64,68},{66,78},{96,100},{98,110},{4,... | collective-permute-start | bytes 3145736 | tf_op jit(solution)/shard_map/ppermute | solution.py:57
  44.4 3.3 %collective-permute-start.1 = (bf16[256,2048]{1,0:T(8,128)(2,1)}, bf16[256,2048]{1,0:T(8,128)(2,1)}, u32[]{:S(2)}, u32[]{:S(2)}) collective-permute-start(bf16[256,2048]{1,0:T(8,128)(2,1)} %collective-permute-done.refs_0_), channel_id=1, source_target_pairs={{0,32},{2,98},{32,0},{34,66},{64,96},{66,34},{96,64},{98,2},{4,36}... | collective-permute-start | bytes 3145736 | tf_op jit(solution)/shard_map/ppermute | solution.py:57
  47.7 13.5 %all-to-all-done.x_ref = bf16[64,48,512]{2,1,0:T(8,128)(2,1)} async-done(((bf16[64,48,512]{2,1,0:T(8,128)(2,1)}), bf16[64,48,512]{2,1,0:T(8,128)(2,1)}, u32[]{:S(2)}, u32[]{:S(2)}) %all-to-all-start) | async-done | bytes 3145760 | tf_op jit(solution)/shard_map/all_to_all | solution.py:443
  61.2 5.6 %column_attention.1 = bf16[64,16,512]{2,1,0:T(8,128)(2,1)} custom-call(bf16[64,48,512]{2,1,0:T(8,128)(2,1)} %all-to-all-done.x_ref), custom_call_target="tpu_custom_call" | custom-call | flops 1048576 | bytes 1024 | tf_op jit(solution)/shard_map/column_attention/pallas_call | solution.py:166
  66.8 5.9 %all-to-all-start.1 = ((bf16[128,8,512]{2,1,0:T(8,128)(2,1)}), bf16[128,8,512]{2,1,0:T(8,128)(2,1)S(1)}, u32[]{:S(2)}, u32[]{:S(2)}) async-start(bf16[128,8,512]{2,1,0:T(8,128)(2,1)} %bitcast.12), calls=%async_computation.1 | async-start | bytes 2097152 | tf_op jit(solution)/shard_map/all_to_all | solution.py:455
  72.7 6.9 %collective-permute-done.3.refs_3_ = bf16[256,2048]{1,0:T(8,128)(2,1)} collective-permute-done((bf16[256,2048]{1,0:T(8,128)(2,1)S(1)}, bf16[256,2048]{1,0:T(8,128)(2,1)}, u32[]{:S(2)}, u32[]{:S(2)}) %collective-permute-start.3) | collective-permute-done | bytes 1048608 | tf_op jit(solution)/shard_map/ppermute | solution.py:57
  79.7 0.0 collective-permute-done.4.a_ref.x_ref
  79.7 0.0 copy-start.2
  79.7 0.0 collective-permute-done.2.refs_2_
  79.7 0.0 collective-permute-done.1.refs_1_
  79.7 0.8 collective-permute-start.5
  80.5 0.1 collective-permute-start.6
  80.6 0.4 collective-permute-start.7
  81.0 0.1 collective-permute-start.8
  81.1 0.0 copy-done.2
  81.1 5.0 %other_rows.1.near_ref = bf16[512,2048]{1,0:T(8,128)(2,1)} custom-call(s32[4]{0:T(128)S(1)} %copy-done.1, bf16[1024,512]{1,0:T(8,128)(2,1)} %copy-done.2, bf16[512,4096]{1,0:T(8,128)(2,1)} %own_rows.1.acc_ref.far_ref, bf16[256,2048]{1,0:T(8,128)(2,1)} %collective-permute-done.refs_0_, bf16[256,2048]{1,0:T(8,128)(2,1)} %collective-permute-done.1.refs_1_, ...), custom_call_target="tpu_custom_call" | custom-call | flops 1048576 | bytes 1024 | tf_op jit(solution)/shard_map/other_rows/pallas_call | solution.py:226
  86.1 9.5 %all-to-all-done.1 = bf16[128,8,512]{2,1,0:T(8,128)(2,1)S(1)} async-done(((bf16[128,8,512]{2,1,0:T(8,128)(2,1)}), bf16[128,8,512]{2,1,0:T(8,128)(2,1)S(1)}, u32[]{:S(2)}, u32[]{:S(2)}) %all-to-all-start.1) | async-done | bytes 1048608 | tf_op jit(solution)/shard_map/all_to_all | solution.py:455
  95.6 0.7 join.1.y_ref
  96.4 0.0 collective-permute-done.5.refs_4_
  96.4 0.0 collective-permute-done.6.refs_5_
  96.4 0.0 collective-permute-done.7.refs_6_
  96.4 0.0 collective-permute-done.8.refs_7_
  96.4 12.3 %project.1 = bf16[1,512,4096]{2,1,0:T(8,128)(2,1)} custom-call(s32[4]{0:T(128)S(1)} %copy-done.1, bf16[1024,512]{1,0:T(8,128)(2,1)} %copy-done.2, bf16[512,1024]{1,0:T(8,128)(2,1)S(1)} %join.1.y_ref, bf16[512,2048]{1,0:T(8,128)(2,1)} %other_rows.1.near_ref, bf16[512,4096]{1,0:T(8,128)(2,1)} %own_rows.1.acc_ref.far_ref, bf16[1024,4096]{1,0:T(8,128)(2,1)} %w_ref.6, ...), custom_call_target="tpu_custom_call" | custom-call | flops 1048576 | bytes 1024 | tf_op jit(solution)/shard_map/project/pallas_call | solution.py:318
Async XLA Ops:
  0.1 2.6 %copy-start = (s32[4]{0:T(128)}, s32[4]{0:T(128)S(1)}, u32[]{:S(2)}) copy-start(s32[4]{0:T(128)S(1)} %pad_add_fusion.s_ref) | copy-start | bytes 52
  2.6 17.0 %collective-permute-start = (bf16[256,2048]{1,0:T(8,128)(2,1)}, bf16[256,2048]{1,0:T(8,128)(2,1)}, u32[]{:S(2)}, u32[]{:S(2)}) collective-permute-start(bf16[256,2048]{1,0:T(8,128)(2,1)} %slice.2), channel_id=1, source_target_pairs={{0,1},{2,19},{32,33},{34,51},{64,65},{66,83},{96,97},{98,115},{4,5... | collective-permute-start | bytes 3145736 | tf_op jit(solution)/shard_map/ppermute | solution.py:57
  9.1 52.1 %all-to-all-start = ((bf16[64,48,512]{2,1,0:T(8,128)(2,1)}), bf16[64,48,512]{2,1,0:T(8,128)(2,1)}, u32[]{:S(2)}, u32[]{:S(2)}) async-start(bf16[64,48,512]{2,1,0:T(8,128)(2,1)} %bitcast.11), calls=%async_computation | async-start | bytes 6291456 | tf_op jit(solution)/shard_map/all_to_all | solution.py:443
  19.7 10.7 %copy-start.1 = (s32[4]{0:T(128)S(1)}, s32[4]{0:T(128)}, u32[]{:S(2)}) copy-start(s32[4]{0:T(128)} %copy-done) | copy-start | bytes 52
  33.0 6.4 %copy-start.3 = (bf16[256,2048]{1,0:T(8,128)(2,1)S(1)}, bf16[256,2048]{1,0:T(8,128)(2,1)}, u32[]{:S(2)}) copy-start(bf16[256,2048]{1,0:T(8,128)(2,1)} %slice.3) | copy-start | bytes 3145732
  39.4 40.2 %collective-permute-start.3 = (bf16[256,2048]{1,0:T(8,128)(2,1)S(1)}, bf16[256,2048]{1,0:T(8,128)(2,1)}, u32[]{:S(2)}, u32[]{:S(2)}) collective-permute-start(bf16[256,2048]{1,0:T(8,128)(2,1)S(1)} %copy-done.3), channel_id=1, source_target_pairs={{0,17},{2,19},{32,49},{34,51},{64,81},{66,83},{96,113},{98,115},{4... | collective-permute-start | bytes 3145736 | tf_op jit(solution)/shard_map/ppermute | solution.py:57
  41.4 38.3 %collective-permute-start.4 = (bf16[1024,512]{1,0:T(8,128)(2,1)}, bf16[1024,512]{1,0:T(8,128)(2,1)S(1)}, u32[]{:S(2)}, u32[]{:S(2)}) collective-permute-start(bf16[1024,512]{1,0:T(8,128)(2,1)} %get-tuple-element.37), channel_id=1, source_target_pairs={{0,1},{2,3},{32,33},{34,35},{64,65},{66,67},{96,97},{98,99},{4,5},... | collective-permute-start | bytes 3145736 | tf_op jit(solution)/shard_map/ppermute | solution.py:57
  42.0 37.7 %collective-permute-start.2 = (bf16[256,2048]{1,0:T(8,128)(2,1)}, bf16[256,2048]{1,0:T(8,128)(2,1)}, u32[]{:S(2)}, u32[]{:S(2)}) collective-permute-start(bf16[256,2048]{1,0:T(8,128)(2,1)} %collective-permute-done.refs_0_), channel_id=1, source_target_pairs={{0,4},{2,14},{32,36},{34,46},{64,68},{66,78},{96,100},{98,110},{4,... | collective-permute-start | bytes 3145736 | tf_op jit(solution)/shard_map/ppermute | solution.py:57
  44.4 35.3 %collective-permute-start.1 = (bf16[256,2048]{1,0:T(8,128)(2,1)}, bf16[256,2048]{1,0:T(8,128)(2,1)}, u32[]{:S(2)}, u32[]{:S(2)}) collective-permute-start(bf16[256,2048]{1,0:T(8,128)(2,1)} %collective-permute-done.refs_0_), channel_id=1, source_target_pairs={{0,32},{2,98},{32,0},{34,66},{64,96},{66,34},{96,64},{98,2},{4,36}... | collective-permute-start | bytes 3145736 | tf_op jit(solution)/shard_map/ppermute | solution.py:57
  66.8 28.8 %all-to-all-start.1 = ((bf16[128,8,512]{2,1,0:T(8,128)(2,1)}), bf16[128,8,512]{2,1,0:T(8,128)(2,1)S(1)}, u32[]{:S(2)}, u32[]{:S(2)}) async-start(bf16[128,8,512]{2,1,0:T(8,128)(2,1)} %bitcast.12), calls=%async_computation.1 | async-start | bytes 2097152 | tf_op jit(solution)/shard_map/all_to_all | solution.py:455
  79.7 1.5 %copy-start.2 = (bf16[1024,512]{1,0:T(8,128)(2,1)}, bf16[1024,512]{1,0:T(8,128)(2,1)S(1)}, u32[]{:S(2)}) copy-start(bf16[1024,512]{1,0:T(8,128)(2,1)S(1)} %collective-permute-done.4.a_ref.x_ref) | copy-start | bytes 3145732
  79.7 16.7 %collective-permute-start.5 = (bf16[256,2048]{1,0:T(8,128)(2,1)}, bf16[256,2048]{1,0:T(8,128)(2,1)}, u32[]{:S(2)}, u32[]{:S(2)}) collective-permute-start(bf16[256,2048]{1,0:T(8,128)(2,1)} %collective-permute-done.refs_0_), channel_id=1, source_target_pairs={{0,2},{2,0},{32,34},{34,32},{64,66},{66,64},{96,98},{98,96},{4,6},... | collective-permute-start | bytes 3145736 | tf_op jit(solution)/shard_map/ppermute | solution.py:57
  80.5 15.8 %collective-permute-start.6 = (bf16[256,2048]{1,0:T(8,128)(2,1)}, bf16[256,2048]{1,0:T(8,128)(2,1)}, u32[]{:S(2)}, u32[]{:S(2)}) collective-permute-start(bf16[256,2048]{1,0:T(8,128)(2,1)} %collective-permute-done.1.refs_1_), channel_id=1, source_target_pairs={{0,2},{2,0},{32,34},{34,32},{64,66},{66,64},{96,98},{98,96},{4,6},... | collective-permute-start | bytes 3145736 | tf_op jit(solution)/shard_map/ppermute | solution.py:57
  80.6 15.8 %collective-permute-start.7 = (bf16[256,2048]{1,0:T(8,128)(2,1)}, bf16[256,2048]{1,0:T(8,128)(2,1)}, u32[]{:S(2)}, u32[]{:S(2)}) collective-permute-start(bf16[256,2048]{1,0:T(8,128)(2,1)} %collective-permute-done.2.refs_2_), channel_id=1, source_target_pairs={{0,2},{2,0},{32,34},{34,32},{64,66},{66,64},{96,98},{98,96},{4,6},... | collective-permute-start | bytes 3145736 | tf_op jit(solution)/shard_map/ppermute | solution.py:57
  81.0 15.3 %collective-permute-start.8 = (bf16[256,2048]{1,0:T(8,128)(2,1)}, bf16[256,2048]{1,0:T(8,128)(2,1)}, u32[]{:S(2)}, u32[]{:S(2)}) collective-permute-start(bf16[256,2048]{1,0:T(8,128)(2,1)} %collective-permute-done.3.refs_3_), channel_id=1, source_target_pairs={{0,2},{2,0},{32,34},{34,32},{64,66},{66,64},{96,98},{98,96},{4,6},... | collective-permute-start | bytes 3145736 | tf_op jit(solution)/shard_map/ppermute | solution.py:57

commit v7 on v6

--- a/solution.py
+++ b/solution.py
@@ -265,7 +265,7 @@
 
 def project_kernel(s_ref, x_ref, y_ref, near_ref, far_ref, w_ref, *refs):
     pieces, o_ref = refs[:8], refs[8]
-    a_buf, w_buf, acc_buf, o_buf, load_sems, store_sems, x_buf, row_sem = refs[9:]
+    a_buf, w_buf, acc_buf, o_buf, load_sems, store_sems = refs[9:]
     half = CHUNKS // 2
     depth = 2 * LOCAL
 
@@ -293,18 +293,14 @@
     def store_of(n):
         return pltpu.make_async_copy(o_buf.at[n], o_ref.at[0, :, columns_of(n)], store_sems.at[n])
 
-    rows = pltpu.make_async_copy(x_ref.at[pl.ds(0, HALF)], x_buf, row_sem)
-    rows.start()
     for n in range(CHUNKS):
         for load in loads_of(n):
             load.start()
+    for i in range(4):
+        a_buf[:, i * HD : (i + 1) * HD] = x_ref[:HALF, head_of(s_ref, i)]
     for n in range(CHUNKS):
         for load in loads_of(n):
             load.wait()
-        if n == half:
-            rows.wait()
-            for i in range(4):
-                a_buf[:, i * HD : (i + 1) * HD] = x_buf[:, head_of(s_ref, i)]
         total = acc_buf[n].astype(jnp.float32) + dot_nn(y_ref[...], w_buf[n, :depth])
         if n >= half:
             total += dot_nn(a_buf[...], w_buf[n, depth:])
@@ -319,7 +315,7 @@
         project_kernel,
         in_specs=[
             pl.BlockSpec(memory_space=pltpu.SMEM),
-            ANYWHERE,
+            WHOLE,
             WHOLE,
             *[ANYWHERE] * 11,
         ],
@@ -332,13 +328,11 @@
             pltpu.VMEM((CHUNKS, HALF, CHUNK), jnp.bfloat16),
             pltpu.SemaphoreType.DMA((CHUNKS, 10)),
             pltpu.SemaphoreType.DMA((CHUNKS,)),
-            pltpu.VMEM((HALF, LOCAL), jnp.bfloat16),
-            pltpu.SemaphoreType.DMA(()),
         ],
         compiler_params=pltpu.CompilerParams(vmem_limit_bytes=40 << 20),
         cost_estimate=COST,
         name="project",
-    )(place, in_hbm(row_other), joined, *map(in_hbm, (acc_near, acc, w_own, *pieces)))
+    )(place, row_other, joined, *map(in_hbm, (acc_near, acc, w_own, *pieces)))
 
 
 def slice_kernel(opposite, s_ref, w_ref, x_ref, buf, in_sems, out_sems):

time: 109 us -> 108 us (level)
  Pallas kernels: 48.9 us -> 47 us
    pallas_call x1, Pallas kernels: 12.3 us -> 10.3 us  [project(): pl.pallas_call(project_kernel, in_specs=[pl.BlockSpec(memory_space=pltpu....]
  transfers between devices with their start and end apart: 11 -> 11, of which waited for: 3 -> 3; matrix products, arithmetic and copies ran while one was open for 0% -> 0% of each run, Pallas kernels for 31% -> 32%
where the time goes in v7:
time: 108 us; the launch traced here: 107 us
  Pallas kernels  47 us (44%)
  waiting for transfers between devices  29.9 us (28%)
  starting transfers between devices  29.6 us (27%)
    all_to_all x1, waiting for transfers between devices, on_device(): lax.all_to_all(sent, 'ctx', split_axis=0, concat_axis=0, tiled=True)  13.6 us
    ppermute x9, starting transfers between devices, permute(): return lax.ppermute(x, ('ctx', 'head'), pairs)  13.1 us
    pallas_call x1, Pallas kernels, row_attention(): pl.pallas_call(row_kernel, grid=(GROUP,), in_specs=[spec] * 3, out_specs=...  10.7 us
    all_to_all x1, starting transfers between devices, on_device(): lax.all_to_all(sent, 'ctx', split_axis=0, concat_axis=0, tiled=True)  10.5 us
    pallas_call x1, Pallas kernels, project(): pl.pallas_call(project_kernel, in_specs=[pl.BlockSpec(memory_space=pltpu....  10.3 us
    all_to_all x1, waiting for transfers between devices, on_device(): lax.all_to_all(col, ('ctx', 'head'), split_axis=0, concat_axis=0, tiled=T...  9.49 us
    ppermute x9, waiting for transfers between devices, permute(): return lax.ppermute(x, ('ctx', 'head'), pairs)  6.85 us
    pallas_call x1, Pallas kernels, project_own_rows(): pl.pallas_call(own_rows_kernel, grid=(TILES,), in_specs=[pl.BlockSpec((HA...  6.3 us
  transfers between devices with their start and end apart: 11, of which 3 were waited for; matrix products, arithmetic and copies ran while one was open for 0% of the time, Pallas kernels for 32%

profile of v7, /device:TPU:1, one launch (start us, length us, event | category | flops | bytes accessed | tf_op | source)
XLA Modules:
  0.0 107.3 jit_solution(8920732455950470846)
XLA Ops:
  0.0 0.1 pad_add_fusion.s_ref
  0.1 0.0 copy-start.2
  0.1 2.5 %slice.2 = bf16[256,2048]{1,0:T(8,128)(2,1)} custom-call(s32[4]{0:T(128)S(1)} %pad_add_fusion.s_ref, bf16[1024,4096]{1,0:T(8,128)(2,1)} %w_ref.6), custom_call_target="tpu_custom_call" | custom-call | flops 1048576 | bytes 1024 | tf_op jit(solution)/shard_map/slice/pallas_call | solution.py:366
  2.6 0.0 copy-done.2
  2.6 3.4 %collective-permute-start = (bf16[256,2048]{1,0:T(8,128)(2,1)}, bf16[256,2048]{1,0:T(8,128)(2,1)}, u32[]{:S(2)}, u32[]{:S(2)}) collective-permute-start(bf16[256,2048]{1,0:T(8,128)(2,1)} %slice.2), channel_id=1, source_target_pairs={{0,1},{2,19},{32,33},{34,51},{64,65},{66,83},{96,97},{98,115},{4,5... | collective-permute-start | bytes 3145736 | tf_op jit(solution)/shard_map/ppermute | solution.py:57
  6.0 3.1 %pack.1 = bf16[64,6,8,512]{3,2,1,0:T(8,128)(2,1)} custom-call(bf16[1,2,64,8,1024]{4,3,2,1,0:T(8,128)(2,1)} %bitcast.13, bf16[1,2,64,8,1024]{4,3,2,1,0:T(8,128)(2,1)} %bitcast.14, bf16[1,2,64,8,1024]{4,3,2,1,0:T(8,128)(2,1)} %bitcast.15), custom_call_target="tpu_custom_call" | custom-call | flops 1048576 | bytes 1024 | tf_op jit(solution)/shard_map/pack/pallas_call | solution.py:414
  9.1 10.5 %all-to-all-start = ((bf16[64,48,512]{2,1,0:T(8,128)(2,1)}), bf16[64,48,512]{2,1,0:T(8,128)(2,1)}, u32[]{:S(2)}, u32[]{:S(2)}) async-start(bf16[64,48,512]{2,1,0:T(8,128)(2,1)} %bitcast.11), calls=%async_computation | async-start | bytes 6291456 | tf_op jit(solution)/shard_map/all_to_all | solution.py:437
  19.7 0.0 collective-permute-done.refs_0_
  19.7 0.0 copy-start.3
  19.7 10.7 %row_attention.1 = (bf16[512,512]{1,0:T(8,128)(2,1)}, bf16[1024,512]{1,0:T(8,128)(2,1)}) custom-call(bf16[1,1024,1024]{2,1,0:T(8,128)(2,1)} %q_ref, bf16[1,1024,1024]{2,1,0:T(8,128)(2,1)} %k_ref, bf16[1,1024,1024]{2,1,0:T(8,128)(2,1)} %v_ref), custom_call_target="tpu_custom_call" | custom-call | flops 274877906944 | bytes 1048576 | tf_op jit(solution)/shard_map/row_attention/pallas_call | solution.py:109
  30.4 0.0 copy-done.3
  30.4 2.6 %slice.3 = bf16[256,2048]{1,0:T(8,128)(2,1)} custom-call(s32[4]{0:T(128)S(1)} %copy-done.3, bf16[1024,4096]{1,0:T(8,128)(2,1)} %w_ref.6), custom_call_target="tpu_custom_call" | custom-call | flops 1048576 | bytes 1024 | tf_op jit(solution)/shard_map/slice/pallas_call | solution.py:366
  33.0 0.0 copy-start.4
  33.0 6.3 %own_rows.1.acc_ref.far_ref = bf16[512,4096]{1,0:T(8,128)(2,1)} custom-call(bf16[512,512]{1,0:T(8,128)(2,1)} %get-tuple-element.34.a_ref, bf16[1024,4096]{1,0:T(8,128)(2,1)} %w_ref.6), custom_call_target="tpu_custom_call" | custom-call | flops 1048576 | bytes 1024 | tf_op jit(solution)/shard_map/own_rows/pallas_call | solution.py:191
  39.3 0.0 copy-done.4
  39.4 1.9 %collective-permute-start.3 = (bf16[256,2048]{1,0:T(8,128)(2,1)S(1)}, bf16[256,2048]{1,0:T(8,128)(2,1)}, u32[]{:S(2)}, u32[]{:S(2)}) collective-permute-start(bf16[256,2048]{1,0:T(8,128)(2,1)S(1)} %copy-done.4), channel_id=1, source_target_pairs={{0,17},{2,19},{32,49},{34,51},{64,81},{66,83},{96,113},{98,115},{4... | collective-permute-start | bytes 3145736 | tf_op jit(solution)/shard_map/ppermute | solution.py:57
  41.3 0.7 collective-permute-start.4
  41.9 2.4 %collective-permute-start.2 = (bf16[256,2048]{1,0:T(8,128)(2,1)}, bf16[256,2048]{1,0:T(8,128)(2,1)}, u32[]{:S(2)}, u32[]{:S(2)}) collective-permute-start(bf16[256,2048]{1,0:T(8,128)(2,1)} %collective-permute-done.refs_0_), channel_id=1, source_target_pairs={{0,4},{2,14},{32,36},{34,46},{64,68},{66,78},{96,100},{98,110},{4,... | collective-permute-start | bytes 3145736 | tf_op jit(solution)/shard_map/ppermute | solution.py:57
  44.3 3.3 %collective-permute-start.1 = (bf16[256,2048]{1,0:T(8,128)(2,1)}, bf16[256,2048]{1,0:T(8,128)(2,1)}, u32[]{:S(2)}, u32[]{:S(2)}) collective-permute-start(bf16[256,2048]{1,0:T(8,128)(2,1)} %collective-permute-done.refs_0_), channel_id=1, source_target_pairs={{0,32},{2,98},{32,0},{34,66},{64,96},{66,34},{96,64},{98,2},{4,36}... | collective-permute-start | bytes 3145736 | tf_op jit(solution)/shard_map/ppermute | solution.py:57
  47.7 13.6 %all-to-all-done.x_ref = bf16[64,48,512]{2,1,0:T(8,128)(2,1)} async-done(((bf16[64,48,512]{2,1,0:T(8,128)(2,1)}), bf16[64,48,512]{2,1,0:T(8,128)(2,1)}, u32[]{:S(2)}, u32[]{:S(2)}) %all-to-all-start) | async-done | bytes 3145760 | tf_op jit(solution)/shard_map/all_to_all | solution.py:437
  61.2 5.7 %column_attention.1 = bf16[64,16,512]{2,1,0:T(8,128)(2,1)} custom-call(bf16[64,48,512]{2,1,0:T(8,128)(2,1)} %all-to-all-done.x_ref), custom_call_target="tpu_custom_call" | custom-call | flops 1048576 | bytes 1024 | tf_op jit(solution)/shard_map/column_attention/pallas_call | solution.py:166
  66.9 5.9 %all-to-all-start.1 = ((bf16[128,8,512]{2,1,0:T(8,128)(2,1)}), bf16[128,8,512]{2,1,0:T(8,128)(2,1)S(1)}, u32[]{:S(2)}, u32[]{:S(2)}) async-start(bf16[128,8,512]{2,1,0:T(8,128)(2,1)} %bitcast.12), calls=%async_computation.1 | async-start | bytes 2097152 | tf_op jit(solution)/shard_map/all_to_all | solution.py:449
  72.8 6.8 %collective-permute-done.3.refs_3_ = bf16[256,2048]{1,0:T(8,128)(2,1)} collective-permute-done((bf16[256,2048]{1,0:T(8,128)(2,1)S(1)}, bf16[256,2048]{1,0:T(8,128)(2,1)}, u32[]{:S(2)}, u32[]{:S(2)}) %collective-permute-start.3) | collective-permute-done | bytes 1048608 | tf_op jit(solution)/shard_map/ppermute | solution.py:57
  79.7 0.0 collective-permute-done.4.a_ref.x_ref
  79.7 0.0 copy-start
  79.7 0.0 collective-permute-done.2.refs_2_
  79.7 0.0 collective-permute-done.1.refs_1_
  79.7 0.8 collective-permute-start.5
  80.5 0.1 collective-permute-start.6
  80.6 0.4 collective-permute-start.7
  81.0 0.1 collective-permute-start.8
  81.1 0.0 copy-done
  81.1 5.0 %other_rows.1.near_ref = bf16[512,2048]{1,0:T(8,128)(2,1)} custom-call(s32[4]{0:T(128)S(1)} %copy-done.3, bf16[1024,512]{1,0:T(8,128)(2,1)} %copy-done, bf16[512,4096]{1,0:T(8,128)(2,1)} %own_rows.1.acc_ref.far_ref, bf16[256,2048]{1,0:T(8,128)(2,1)} %collective-permute-done.refs_0_, bf16[256,2048]{1,0:T(8,128)(2,1)} %collective-permute-done.1.refs_1_, ...), custom_call_target="tpu_custom_call" | custom-call | flops 1048576 | bytes 1024 | tf_op jit(solution)/shard_map/other_rows/pallas_call | solution.py:226
  86.1 9.5 %all-to-all-done.1 = bf16[128,8,512]{2,1,0:T(8,128)(2,1)S(1)} async-done(((bf16[128,8,512]{2,1,0:T(8,128)(2,1)}), bf16[128,8,512]{2,1,0:T(8,128)(2,1)S(1)}, u32[]{:S(2)}, u32[]{:S(2)}) %all-to-all-start.1) | async-done | bytes 1048608 | tf_op jit(solution)/shard_map/all_to_all | solution.py:449
  95.6 0.0 copy-start.1
  95.6 0.7 join.1.y_ref
  96.4 0.0 collective-permute-done.5.refs_4_
  96.4 0.0 collective-permute-done.6.refs_5_
  96.4 0.0 collective-permute-done.7.refs_6_
  96.4 0.0 collective-permute-done.8.refs_7_
  96.4 0.5 copy-done.1
  96.9 10.3 %project.1 = bf16[1,512,4096]{2,1,0:T(8,128)(2,1)} custom-call(s32[4]{0:T(128)S(1)} %copy-done.3, bf16[1024,512]{1,0:T(8,128)(2,1)S(1)} %copy-done.1, bf16[512,1024]{1,0:T(8,128)(2,1)S(1)} %join.1.y_ref, bf16[512,2048]{1,0:T(8,128)(2,1)} %other_rows.1.near_ref, bf16[512,4096]{1,0:T(8,128)(2,1)} %own_rows.1.acc_ref.far_ref, bf16[1024,4096]{1,0:T(8,128)(2,1)} %w_ref.6, ...), custom_call_target="tpu_custom_call" | custom-call | flops 1048576 | bytes 1024 | tf_op jit(solution)/shard_map/project/pallas_call | solution.py:314
Async XLA Ops:
  0.1 2.6 %copy-start.2 = (s32[4]{0:T(128)}, s32[4]{0:T(128)S(1)}, u32[]{:S(2)}) copy-start(s32[4]{0:T(128)S(1)} %pad_add_fusion.s_ref) | copy-start | bytes 52
  2.6 17.0 %collective-permute-start = (bf16[256,2048]{1,0:T(8,128)(2,1)}, bf16[256,2048]{1,0:T(8,128)(2,1)}, u32[]{:S(2)}, u32[]{:S(2)}) collective-permute-start(bf16[256,2048]{1,0:T(8,128)(2,1)} %slice.2), channel_id=1, source_target_pairs={{0,1},{2,19},{32,33},{34,51},{64,65},{66,83},{96,97},{98,115},{4,5... | collective-permute-start | bytes 3145736 | tf_op jit(solution)/shard_map/ppermute | solution.py:57
  9.1 52.1 %all-to-all-start = ((bf16[64,48,512]{2,1,0:T(8,128)(2,1)}), bf16[64,48,512]{2,1,0:T(8,128)(2,1)}, u32[]{:S(2)}, u32[]{:S(2)}) async-start(bf16[64,48,512]{2,1,0:T(8,128)(2,1)} %bitcast.11), calls=%async_computation | async-start | bytes 6291456 | tf_op jit(solution)/shard_map/all_to_all | solution.py:437
  19.7 10.7 %copy-start.3 = (s32[4]{0:T(128)S(1)}, s32[4]{0:T(128)}, u32[]{:S(2)}) copy-start(s32[4]{0:T(128)} %copy-done.2) | copy-start | bytes 52
  33.0 6.3 %copy-start.4 = (bf16[256,2048]{1,0:T(8,128)(2,1)S(1)}, bf16[256,2048]{1,0:T(8,128)(2,1)}, u32[]{:S(2)}) copy-start(bf16[256,2048]{1,0:T(8,128)(2,1)} %slice.3) | copy-start | bytes 3145732
  39.4 40.3 %collective-permute-start.3 = (bf16[256,2048]{1,0:T(8,128)(2,1)S(1)}, bf16[256,2048]{1,0:T(8,128)(2,1)}, u32[]{:S(2)}, u32[]{:S(2)}) collective-permute-start(bf16[256,2048]{1,0:T(8,128)(2,1)S(1)} %copy-done.4), channel_id=1, source_target_pairs={{0,17},{2,19},{32,49},{34,51},{64,81},{66,83},{96,113},{98,115},{4... | collective-permute-start | bytes 3145736 | tf_op jit(solution)/shard_map/ppermute | solution.py:57
  41.3 38.4 %collective-permute-start.4 = (bf16[1024,512]{1,0:T(8,128)(2,1)}, bf16[1024,512]{1,0:T(8,128)(2,1)S(1)}, u32[]{:S(2)}, u32[]{:S(2)}) collective-permute-start(bf16[1024,512]{1,0:T(8,128)(2,1)} %get-tuple-element.37), channel_id=1, source_target_pairs={{0,1},{2,3},{32,33},{34,35},{64,65},{66,67},{96,97},{98,99},{4,5},... | collective-permute-start | bytes 3145736 | tf_op jit(solution)/shard_map/ppermute | solution.py:57
  41.9 37.8 %collective-permute-start.2 = (bf16[256,2048]{1,0:T(8,128)(2,1)}, bf16[256,2048]{1,0:T(8,128)(2,1)}, u32[]{:S(2)}, u32[]{:S(2)}) collective-permute-start(bf16[256,2048]{1,0:T(8,128)(2,1)} %collective-permute-done.refs_0_), channel_id=1, source_target_pairs={{0,4},{2,14},{32,36},{34,46},{64,68},{66,78},{96,100},{98,110},{4,... | collective-permute-start | bytes 3145736 | tf_op jit(solution)/shard_map/ppermute | solution.py:57
  44.3 35.4 %collective-permute-start.1 = (bf16[256,2048]{1,0:T(8,128)(2,1)}, bf16[256,2048]{1,0:T(8,128)(2,1)}, u32[]{:S(2)}, u32[]{:S(2)}) collective-permute-start(bf16[256,2048]{1,0:T(8,128)(2,1)} %collective-permute-done.refs_0_), channel_id=1, source_target_pairs={{0,32},{2,98},{32,0},{34,66},{64,96},{66,34},{96,64},{98,2},{4,36}... | collective-permute-start | bytes 3145736 | tf_op jit(solution)/shard_map/ppermute | solution.py:57
  66.9 28.7 %all-to-all-start.1 = ((bf16[128,8,512]{2,1,0:T(8,128)(2,1)}), bf16[128,8,512]{2,1,0:T(8,128)(2,1)S(1)}, u32[]{:S(2)}, u32[]{:S(2)}) async-start(bf16[128,8,512]{2,1,0:T(8,128)(2,1)} %bitcast.12), calls=%async_computation.1 | async-start | bytes 2097152 | tf_op jit(solution)/shard_map/all_to_all | solution.py:449
  79.7 1.5 %copy-start = (bf16[1024,512]{1,0:T(8,128)(2,1)}, bf16[1024,512]{1,0:T(8,128)(2,1)S(1)}, u32[]{:S(2)}) copy-start(bf16[1024,512]{1,0:T(8,128)(2,1)S(1)} %collective-permute-done.4.a_ref.x_ref) | copy-start | bytes 3145732
  79.7 16.7 %collective-permute-start.5 = (bf16[256,2048]{1,0:T(8,128)(2,1)}, bf16[256,2048]{1,0:T(8,128)(2,1)}, u32[]{:S(2)}, u32[]{:S(2)}) collective-permute-start(bf16[256,2048]{1,0:T(8,128)(2,1)} %collective-permute-done.refs_0_), channel_id=1, source_target_pairs={{0,2},{2,0},{32,34},{34,32},{64,66},{66,64},{96,98},{98,96},{4,6},... | collective-permute-start | bytes 3145736 | tf_op jit(solution)/shard_map/ppermute | solution.py:57
  80.5 15.8 %collective-permute-start.6 = (bf16[256,2048]{1,0:T(8,128)(2,1)}, bf16[256,2048]{1,0:T(8,128)(2,1)}, u32[]{:S(2)}, u32[]{:S(2)}) collective-permute-start(bf16[256,2048]{1,0:T(8,128)(2,1)} %collective-permute-done.1.refs_1_), channel_id=1, source_target_pairs={{0,2},{2,0},{32,34},{34,32},{64,66},{66,64},{96,98},{98,96},{4,6},... | collective-permute-start | bytes 3145736 | tf_op jit(solution)/shard_map/ppermute | solution.py:57
  80.6 15.8 %collective-permute-start.7 = (bf16[256,2048]{1,0:T(8,128)(2,1)}, bf16[256,2048]{1,0:T(8,128)(2,1)}, u32[]{:S(2)}, u32[]{:S(2)}) collective-permute-start(bf16[256,2048]{1,0:T(8,128)(2,1)} %collective-permute-done.2.refs_2_), channel_id=1, source_target_pairs={{0,2},{2,0},{32,34},{34,32},{64,66},{66,64},{96,98},{98,96},{4,6},... | collective-permute-start | bytes 3145736 | tf_op jit(solution)/shard_map/ppermute | solution.py:57
  81.0 15.3 %collective-permute-start.8 = (bf16[256,2048]{1,0:T(8,128)(2,1)}, bf16[256,2048]{1,0:T(8,128)(2,1)}, u32[]{:S(2)}, u32[]{:S(2)}) collective-permute-start(bf16[256,2048]{1,0:T(8,128)(2,1)} %collective-permute-done.3.refs_3_), channel_id=1, source_target_pairs={{0,2},{2,0},{32,34},{34,32},{64,66},{66,64},{96,98},{98,96},{4,6},... | collective-permute-start | bytes 3145736 | tf_op jit(solution)/shard_map/ppermute | solution.py:57
  95.6 1.2 %copy-start.1 = (bf16[1024,512]{1,0:T(8,128)(2,1)S(1)}, bf16[1024,512]{1,0:T(8,128)(2,1)}, u32[]{:S(2)}) copy-start(bf16[1024,512]{1,0:T(8,128)(2,1)} %copy-done) | copy-start | bytes 3145732
